TPU v7x, 32 devices: a whole 2x2x4 slice. The times are simulated.
32 devices in a mesh: dp: 8 (over z, y), tensor: 4 (over x, core).
Axes of the slice: x: 2, y: 2, z: 4, core: 2. Of those that a mesh axis runs over, the one named last changes fastest.
Arguments:
- block_input: bfloat16 [12288, 768], P(('dp', 'tensor')), may hold values from -6 to 6
- passage_lengths: int32 [24, 4], P('dp'), may hold values from 0 to 512, as said below
- qkv_weight: bfloat16 [2, 3, 768, 768], P(None, None, 'dp', 'tensor'), may hold values from -0.21875 to 0.21875
- qv_bias: bfloat16 [2, 2, 768], P(None, None, ('tensor', 'dp')), may hold values from -3 to 3
- out_weight: bfloat16 [2, 768, 768], P(None, 'tensor', 'dp'), may hold values from -1.25 to 1.25
- out_bias: float32 [2, 768], replicated, may hold values from -3 to 3
- first_gain: float32 [2, 768], replicated, may hold values from 0.5 to 1.5
- first_shift: float32 [2, 768], replicated, may hold values from -2 to 2
- up_weight: bfloat16 [2, 768, 3072], P(None, 'dp', 'tensor'), may hold values from -0.21875 to 0.21875
- up_bias: bfloat16 [2, 3072], P(None, ('tensor', 'dp')), may hold values from -3 to 3
- down_weight: bfloat16 [2, 3072, 768], P(None, 'tensor', 'dp'), may hold values from -0.109375 to 0.109375
- down_bias: float32 [2, 768], replicated, may hold values from -3 to 3
- second_gain: float32 [2, 768], replicated, may hold values from 0.5 to 1.5
- second_shift: float32 [2, 768], replicated, may hold values from -2 to 2
- output_grad: float32 [12288, 768], P(('dp', 'tensor')), may hold values from -6 to 6
Outputs:
- block_output: float32 [12288, 768], P(('dp', 'tensor'))
- input_grad: float32 [12288, 768], P(('dp', 'tensor'))
- qkv_weight_grad: float32 [2, 3, 768, 768], P(None, None, 'dp', 'tensor')
- qv_bias_grad: float32 [2, 2, 768], P(None, None, ('tensor', 'dp'))
- out_weight_grad: float32 [2, 768, 768], P(None, 'tensor', 'dp')
- out_bias_grad: float32 [2, 768], replicated
- first_gain_grad: float32 [2, 768], replicated
- first_shift_grad: float32 [2, 768], replicated
- up_weight_grad: float32 [2, 768, 3072], P(None, 'dp', 'tensor')
- up_bias_grad: float32 [2, 3072], P(None, ('tensor', 'dp'))
- down_weight_grad: float32 [2, 3072, 768], P(None, 'tensor', 'dp')
- down_bias_grad: float32 [2, 768], replicated
- second_gain_grad: float32 [2, 768], replicated
- second_shift_grad: float32 [2, 768], replicated
Inputs may be any that keep to these rules, and one draw needn't show every extreme that they name: `passage_lengths`: in every packed row the passage lengths sum to at least 1 and at most 512, the slots after the last passage being padding; some row of every draw holds one passage of exactly 512 slots; passages may be empty.
All inputs are finite; a program needn't handle non-finite values.
Results may differ from a plain program's by a relative error of at most 0.04.
Values may be sent and summed in bfloat16 or wider, within the bound.
A program may use at most 192 MiB of HBM per device.

v0:
```python
from functools import partial

import jax
import jax.numpy as jnp
from jax import lax
from jax.sharding import PartitionSpec as P

HD = 64
PACK = 512


eps = 1e-05


def normalize(value, gain, shift):
    average = jnp.mean(value, axis=-1, keepdims=True)
    centered = value - average
    variance = jnp.mean(centered * centered, axis=-1, keepdims=True)
    scaled = lax.rsqrt(variance + eps)
    normed = centered * scaled
    return (normed * gain + shift, normed, scaled)


def normalize_back(grad, normed, scaled, gain):
    inner = grad * gain
    centered = inner - jnp.mean(inner, axis=-1, keepdims=True)
    result = scaled * (centered - normed * jnp.mean(inner * normed, axis=-1, keepdims=True))
    return (result, jnp.sum(grad * normed, axis=0), jnp.sum(grad, axis=0))


def visible(lengths, width):
    segments = lengths.shape[1]
    ends = jnp.cumsum(lengths, axis=1, dtype=jnp.int32)
    places = jnp.arange(width, dtype=jnp.int32)
    passage = jnp.sum(
        (places[None, :, None] >= ends[:, None, :]).astype(jnp.int32), axis=2, dtype=jnp.int32
    )
    padding = passage == segments
    matching = passage[:, :, None] == passage[:, None, :]
    return jnp.logical_and(
        jnp.logical_not(padding)[:, None, :], jnp.logical_or(matching, padding[:, :, None])
    )


def attend_rows(query, key, value, allowed, factor):

    def one_row(item):
        query_row, key_row, value_row, mask_row = item
        scores = (
            jnp.einsum("qhd,khd->hqk", query_row, key_row, preferred_element_type=jnp.float32)
            * factor
        )
        scores = jnp.where(mask_row[None], scores, -jnp.inf)
        peak = jnp.max(scores, axis=-1, keepdims=True)
        weights = jnp.exp(scores - peak)
        totals = jnp.sum(weights, axis=-1, keepdims=True)
        probs = (weights / totals).astype(jnp.bfloat16)
        context = jnp.einsum("hqk,khd->qhd", probs, value_row, preferred_element_type=jnp.float32)
        return (context.astype(jnp.bfloat16), peak + jnp.log(totals))

    return lax.map(one_row, (query, key, value, allowed))


def attend_back(query, key, value, dcontext, logsum, allowed, factor):

    def one_row(item):
        query_row, key_row, value_row, grad_row, logsum_row, mask_row = item
        scores = (
            jnp.einsum("qhd,khd->hqk", query_row, key_row, preferred_element_type=jnp.float32)
            * factor
        )
        probs = jnp.where(mask_row[None], jnp.exp(scores - logsum_row), 0.0)
        dprobs = jnp.einsum("qhd,khd->hqk", grad_row, value_row, preferred_element_type=jnp.float32)
        dvalue = jnp.einsum(
            "hqk,qhd->khd", probs.astype(jnp.bfloat16), grad_row, preferred_element_type=jnp.float32
        )
        inner = jnp.sum(probs * dprobs, axis=-1, keepdims=True)
        dscores = (factor * probs * (dprobs - inner)).astype(jnp.bfloat16)
        dquery = jnp.einsum("hqk,khd->qhd", dscores, key_row, preferred_element_type=jnp.float32)
        dkey = jnp.einsum("hqk,qhd->khd", dscores, query_row, preferred_element_type=jnp.float32)
        return (dquery, dkey, dvalue)

    return lax.map(one_row, (query, key, value, dcontext, logsum, allowed))


def forward_layer(hidden, weights, vectors, allowed):
    weight_qkv, bias_qv, weight_out, weight_up, bias_up, weight_down = weights
    out_bias, first_gain, first_shift, down_bias, second_gain, second_shift = vectors
    gathered = lax.all_gather(hidden.astype(jnp.bfloat16), "tensor", axis=0, tiled=True)
    raw = jnp.einsum("nd,cde->cne", gathered, weight_qkv, preferred_element_type=jnp.float32)
    query = (raw[0] + bias_qv[0]).astype(jnp.bfloat16)
    key = raw[1].astype(jnp.bfloat16)
    value = (raw[2] + bias_qv[1]).astype(jnp.bfloat16)
    count = gathered.shape[0]
    width = allowed.shape[1]
    shape = (count // width, width, query.shape[1] // HD, HD)
    query, key, value = (query.reshape(shape), key.reshape(shape), value.reshape(shape))
    context, logsum = attend_rows(query, key, value, allowed, HD ** (-0.5))
    context = context.reshape(count, -1)
    first_sum = (
        hidden
        + lax.psum_scatter(
            jnp.dot(context, weight_out, preferred_element_type=jnp.float32).astype(jnp.bfloat16),
            "tensor",
            scatter_dimension=0,
            tiled=True,
        ).astype(jnp.float32)
        + out_bias
    )
    middle, unit_first, scale_first = normalize(first_sum, first_gain, first_shift)
    gathered_mid = lax.all_gather(middle.astype(jnp.bfloat16), "tensor", axis=0, tiled=True)
    upper = jnp.dot(gathered_mid, weight_up, preferred_element_type=jnp.float32) + bias_up
    active = jax.nn.gelu(upper, approximate=False).astype(jnp.bfloat16)
    second_sum = (
        middle
        + lax.psum_scatter(
            jnp.dot(active, weight_down, preferred_element_type=jnp.float32).astype(jnp.bfloat16),
            "tensor",
            scatter_dimension=0,
            tiled=True,
        ).astype(jnp.float32)
        + down_bias
    )
    output, unit_second, scale_second = normalize(second_sum, second_gain, second_shift)
    kept = (
        gathered,
        query,
        key,
        value,
        context,
        logsum,
        unit_first,
        scale_first,
        gathered_mid,
        upper,
        active,
        unit_second,
        scale_second,
    )
    return (output, kept)


def backward_layer(grad, weights, vectors, allowed, kept):
    weight_qkv, bias_qv, weight_out, weight_up, bias_up, weight_down = weights
    out_bias, first_gain, first_shift, down_bias, second_gain, second_shift = vectors
    (
        gathered,
        query,
        key,
        value,
        context,
        logsum,
        unit_first,
        scale_first,
        gathered_mid,
        upper,
        active,
        unit_second,
        scale_second,
    ) = kept
    dsecond, second_gain_grad, second_shift_grad = normalize_back(
        grad, unit_second, scale_second, second_gain
    )
    down_bias_grad = jnp.sum(dsecond, axis=0)
    dsecond_low = lax.all_gather(dsecond.astype(jnp.bfloat16), "tensor", axis=0, tiled=True)
    down_weight_grad = jnp.einsum(
        "nf,nd->fd", active, dsecond_low, preferred_element_type=jnp.float32
    )
    dactive = jnp.einsum("nd,fd->nf", dsecond_low, weight_down, preferred_element_type=jnp.float32)
    ignored, pull = jax.vjp(partial(jax.nn.gelu, approximate=False), upper)
    dupper = pull(dactive)[0]
    up_bias_grad = jnp.sum(dupper, axis=0)
    dupper_low = dupper.astype(jnp.bfloat16)
    up_weight_grad = jnp.einsum(
        "nd,nf->df", gathered_mid, dupper_low, preferred_element_type=jnp.float32
    )
    dmiddle = dsecond + lax.psum_scatter(
        jnp.einsum("nf,df->nd", dupper_low, weight_up, preferred_element_type=jnp.float32).astype(
            jnp.bfloat16
        ),
        "tensor",
        scatter_dimension=0,
        tiled=True,
    ).astype(jnp.float32)
    dfirst, first_gain_grad, first_shift_grad = normalize_back(
        dmiddle, unit_first, scale_first, first_gain
    )
    out_bias_grad = jnp.sum(dfirst, axis=0)
    dfirst_low = lax.all_gather(dfirst.astype(jnp.bfloat16), "tensor", axis=0, tiled=True)
    out_weight_grad = jnp.einsum(
        "nh,nd->hd", context, dfirst_low, preferred_element_type=jnp.float32
    )
    dcontext = jnp.einsum(
        "nd,hd->nh", dfirst_low, weight_out, preferred_element_type=jnp.float32
    ).astype(jnp.bfloat16)
    count = context.shape[0]
    dquery, dkey, dvalue = attend_back(
        query, key, value, dcontext.reshape(query.shape), logsum, allowed, HD ** (-0.5)
    )
    dquery, dkey, dvalue = (
        dquery.reshape(count, -1),
        dkey.reshape(count, -1),
        dvalue.reshape(count, -1),
    )
    bias_qv_grad = jnp.stack([jnp.sum(dquery, axis=0), jnp.sum(dvalue, axis=0)])
    dproj_low = jnp.stack([dquery, dkey, dvalue]).astype(jnp.bfloat16)
    qkv_weight_grad = jnp.einsum(
        "nd,cne->cde", gathered, dproj_low, preferred_element_type=jnp.float32
    )
    dhidden = dfirst + lax.psum_scatter(
        jnp.einsum("cne,cde->nd", dproj_low, weight_qkv, preferred_element_type=jnp.float32).astype(
            jnp.bfloat16
        ),
        "tensor",
        scatter_dimension=0,
        tiled=True,
    ).astype(jnp.float32)
    matrix_grads = (
        qkv_weight_grad,
        bias_qv_grad,
        out_weight_grad,
        up_weight_grad,
        up_bias_grad,
        down_weight_grad,
    )
    vector_grads = jnp.stack(
        [
            out_bias_grad,
            first_gain_grad,
            first_shift_grad,
            down_bias_grad,
            second_gain_grad,
            second_shift_grad,
        ]
    )
    return (dhidden, matrix_grads, vector_grads)


def body(
    block_input,
    passage_lengths,
    qkv_weight,
    qv_bias,
    out_weight,
    out_bias,
    first_gain,
    first_shift,
    up_weight,
    up_bias,
    down_weight,
    down_bias,
    second_gain,
    second_shift,
    output_grad,
):
    allowed = visible(passage_lengths, PACK)
    layers = qkv_weight.shape[0]
    hidden = block_input.astype(jnp.float32)
    kept_weights = []
    kept_all = []
    vector_sets = []
    for layer in range(layers):
        weights = (
            lax.all_gather(qkv_weight[layer], "dp", axis=1, tiled=True),
            lax.all_gather(qv_bias[layer], "dp", axis=1, tiled=True),
            lax.all_gather(out_weight[layer], "dp", axis=1, tiled=True),
            lax.all_gather(up_weight[layer], "dp", axis=0, tiled=True),
            lax.all_gather(up_bias[layer], "dp", axis=0, tiled=True),
            lax.all_gather(down_weight[layer], "dp", axis=1, tiled=True),
        )
        vectors = (
            out_bias[layer],
            first_gain[layer],
            first_shift[layer],
            down_bias[layer],
            second_gain[layer],
            second_shift[layer],
        )
        hidden, kept = forward_layer(hidden, weights, vectors, allowed)
        kept_weights.append(weights)
        kept_all.append(kept)
        vector_sets.append(vectors)
    grad = output_grad
    matrix_list = [None] * layers
    vector_list = [None] * layers
    for layer in reversed(range(layers)):
        weights = kept_weights[layer]
        grad, matrix_grads, vector_grads = backward_layer(
            grad, weights, vector_sets[layer], allowed, kept_all[layer]
        )
        matrix_list[layer] = matrix_grads
        vector_list[layer] = vector_grads
    stacked = [
        jnp.stack([matrix_list[layer][member] for layer in range(layers)]) for member in range(6)
    ]
    summed = (
        lax.psum_scatter(
            stacked[0].astype(jnp.bfloat16), "dp", scatter_dimension=2, tiled=True
        ).astype(jnp.float32),
        lax.psum_scatter(
            stacked[1].astype(jnp.bfloat16), "dp", scatter_dimension=2, tiled=True
        ).astype(jnp.float32),
        lax.psum_scatter(
            stacked[2].astype(jnp.bfloat16), "dp", scatter_dimension=2, tiled=True
        ).astype(jnp.float32),
        lax.psum_scatter(
            stacked[3].astype(jnp.bfloat16), "dp", scatter_dimension=1, tiled=True
        ).astype(jnp.float32),
        lax.psum_scatter(
            stacked[4].astype(jnp.bfloat16), "dp", scatter_dimension=1, tiled=True
        ).astype(jnp.float32),
        lax.psum_scatter(
            stacked[5].astype(jnp.bfloat16), "dp", scatter_dimension=2, tiled=True
        ).astype(jnp.float32),
    )
    totals = lax.psum(jnp.stack(vector_list), ("dp", "tensor"))
    return (
        hidden,
        grad,
        summed[0],
        summed[1],
        summed[2],
        totals[:, 0],
        totals[:, 1],
        totals[:, 2],
        summed[3],
        summed[4],
        summed[5],
        totals[:, 3],
        totals[:, 4],
        totals[:, 5],
    )


def solution(mesh):
    in_specs = (
        P(("dp", "tensor"), None),
        P("dp", None),
        P(None, None, "dp", "tensor"),
        P(None, None, ("tensor", "dp")),
        P(None, "tensor", "dp"),
        P(),
        P(),
        P(),
        P(None, "dp", "tensor"),
        P(None, ("tensor", "dp")),
        P(None, "tensor", "dp"),
        P(),
        P(),
        P(),
        P(("dp", "tensor"), None),
    )
    out_specs = (
        P(("dp", "tensor"), None),
        P(("dp", "tensor"), None),
        P(None, None, "dp", "tensor"),
        P(None, None, ("tensor", "dp")),
        P(None, "tensor", "dp"),
        P(),
        P(),
        P(),
        P(None, "dp", "tensor"),
        P(None, ("tensor", "dp")),
        P(None, "tensor", "dp"),
        P(),
        P(),
        P(),
    )
    return jax.shard_map(body, mesh=mesh, in_specs=in_specs, out_specs=out_specs, check_vma=False)
```

profile of v0, /device:TPU:1, one launch (start us, length us, event | category | flops | bytes accessed | tf_op | source)
XLA Modules:
  0.0 1315.4 jit_solution(6085774259164000375)
XLA Ops:
  11.5 33.5 %all-gather = bf16[1,3,768,192]{3,1,0,2:T(4,128)(2,1)S(1)} all-gather(bf16[1,3,96,192]{3,1,0,2:T(4,128)(2,1)S(1)} %copy.234), channel_id=2, replica_groups=mesh['dp'=8,'tensor'=4] {'dp'}, dimensions={2}, use_global_device_ids=true | all-gather | bytes 995328 | tf_op jit(solution)/shard_map/all_gather | solution.py:264
  46.6 24.3 %all-gather.1 = bf16[1,2,192]{1,0,2:T(2,128)(2,1)S(1)} all-gather(bf16[1,2,24]{1,0,2:T(2,128)(2,1)S(1)} %copy.235), channel_id=3, replica_groups=mesh['dp'=8,'tensor'=4] {'dp'}, dimensions={2}, use_global_device_ids=true | all-gather | bytes 864 | tf_op jit(solution)/shard_map/all_gather | solution.py:265
  74.8 26.6 %all-gather.2 = bf16[1,192,768]{1,0,2:T(2,128)(2,1)S(1)} all-gather(bf16[1,192,96]{1,0,2:T(2,128)(2,1)S(1)} %copy.236), channel_id=4, replica_groups=mesh['dp'=8,'tensor'=4] {'dp'}, dimensions={2}, use_global_device_ids=true | all-gather | bytes 331776 | tf_op jit(solution)/shard_map/all_gather | solution.py:266
  115.0 10.7 while.52
  131.9 46.7 %reduce-scatter.20.cloned.1.call-done = bf16[384,768]{1,0:T(8,128)(2,1)} async-done(((bf16[1536,768]{1,0:T(8,128)(2,1)}), bf16[384,768]{1,0:T(8,128)(2,1)}) %reduce-scatter.20.cloned.1.call-update) | async-done | bytes 589840 | tf_op jit(solution)/shard_map/reduce_scatter | solution.py:102
  185.3 18.2 %all-reduce.4 = (bf16[768]{0:T(1024)(128)(2,1)S(1)}, bf16[768]{0:T(1024)(128)(2,1)}) all-reduce(bf16[768]{0:T(1024)(128)(2,1)S(1)} %dynamic-update-slice, bf16[768]{0:T(1024)(128)(2,1)S(1)} %dynamic-update-slice.1), channel_id=6, replica_groups=mesh['dp'=8,'tensor'=4] {'dp'}, use_global_device_ids=true, to_apply=%add | all-reduce | flops 1536 | bytes 6144
  203.5 11.8 all-gather.27.cloned.1.call-done
  215.3 15.2 %multiply_convert_fusion.3 = (bf16[1536,768]{1,0:T(8,128)(2,1)}, f32[1536,768]{1,0:T(8,128)}, f32[1536,768]{1,0:T(8,128)}) fusion(f32[768]{0:T(1024)S(1)} %convert_element_type.237, bf16[1536,768]{1,0:T(8,128)(2,1)} %all-gather.27.cloned.1.call-done, bf16[1,768,768]{2,1,0:T(8,128)(2,1)} %all-gather.41.cloned.1.call-done), kind=kOutput, calls=%fused_computation.131 | convolution fusion | flops 1889796096 | bytes 15338496 | tf_op jit(solution)/shard_map/dot_general | solution.py:112
  230.5 27.3 %all-gather.43.cloned.1.call-done = bf16[1,768,768]{1,2,0:T(8,128)(2,1)} async-done(((bf16[1,768,96]{1,2,0:T(8,128)(2,1)}), bf16[1,768,768]{1,2,0:T(8,128)(2,1)}) %all-gather.43.cloned.1.call-update) | async-done | bytes 1179664 | tf_op jit(solution)/shard_map/all_gather | solution.py:269
  257.8 5.5 convolution_convert_fusion.4
  265.8 30.5 %reduce-scatter.22.cloned.1.call-done = bf16[384,768]{1,0:T(8,128)(2,1)} async-done(((bf16[1536,768]{1,0:T(8,128)(2,1)}), bf16[384,768]{1,0:T(8,128)(2,1)}) %reduce-scatter.22.cloned.1.call-update) | async-done | bytes 589840 | tf_op jit(solution)/shard_map/reduce_scatter | solution.py:116
  299.6 32.7 %all-gather.6 = bf16[1,3,768,192]{3,1,0,2:T(4,128)(2,1)S(1)} all-gather(bf16[1,3,96,192]{3,1,0,2:T(4,128)(2,1)S(1)} %copy.237), channel_id=8, replica_groups=mesh['dp'=8,'tensor'=4] {'dp'}, dimensions={2}, use_global_device_ids=true | all-gather | bytes 995328 | tf_op jit(solution)/shard_map/all_gather | solution.py:264
  335.1 24.5 %all-gather.7 = bf16[1,2,192]{1,0,2:T(2,128)(2,1)S(1)} all-gather(bf16[1,2,24]{1,0,2:T(2,128)(2,1)S(1)} %copy.238), channel_id=9, replica_groups=mesh['dp'=8,'tensor'=4] {'dp'}, dimensions={2}, use_global_device_ids=true | all-gather | bytes 864 | tf_op jit(solution)/shard_map/all_gather | solution.py:265
  364.8 26.4 %all-gather.8 = bf16[1,192,768]{1,0,2:T(2,128)(2,1)S(1)} all-gather(bf16[1,192,96]{1,0,2:T(2,128)(2,1)S(1)} %copy.239), channel_id=10, replica_groups=mesh['dp'=8,'tensor'=4] {'dp'}, dimensions={2}, use_global_device_ids=true | all-gather | bytes 331776 | tf_op jit(solution)/shard_map/all_gather | solution.py:266
  410.7 12.6 while.53
  429.4 47.9 %reduce-scatter.24.cloned.1.call-done = bf16[384,768]{1,0:T(8,128)(2,1)} async-done(((bf16[1536,768]{1,0:T(8,128)(2,1)}), bf16[384,768]{1,0:T(8,128)(2,1)}) %reduce-scatter.24.cloned.1.call-update) | async-done | bytes 589840 | tf_op jit(solution)/shard_map/reduce_scatter | solution.py:102
  481.3 6.0 all-gather.45.cloned.1.call-done
  487.3 26.6 %all-gather.31.cloned.1.call-done = bf16[1536,768]{1,0:T(8,128)(2,1)} async-done(((bf16[384,768]{1,0:T(8,128)(2,1)}), bf16[1536,768]{1,0:T(8,128)(2,1)}) %all-gather.31.cloned.1.call-update) | async-done | bytes 2359312 | tf_op jit(solution)/shard_map/all_gather | solution.py:111
  513.9 15.1 %multiply_convert_fusion.2 = (bf16[1536,768]{1,0:T(8,128)(2,1)}, f32[1536,768]{1,0:T(8,128)}, f32[1536,768]{1,0:T(8,128)}) fusion(f32[768]{0:T(1024)S(1)} %convert_element_type.238, bf16[1536,768]{1,0:T(8,128)(2,1)} %all-gather.31.cloned.1.call-done, bf16[1,768,768]{2,1,0:T(8,128)(2,1)} %all-gather.45.cloned.1.call-done), kind=kOutput, calls=%fused_computation.118 | convolution fusion | flops 1889796096 | bytes 15338496 | tf_op jit(solution)/shard_map/dot_general | solution.py:112
  529.0 26.9 %all-gather.47.cloned.1.call-done = bf16[1,768,768]{1,2,0:T(8,128)(2,1)} async-done(((bf16[1,768,96]{1,2,0:T(8,128)(2,1)}), bf16[1,768,768]{1,2,0:T(8,128)(2,1)}) %all-gather.47.cloned.1.call-update) | async-done | bytes 1179664 | tf_op jit(solution)/shard_map/all_gather | solution.py:269
  555.8 5.4 convolution_convert_fusion.2
  561.3 33.1 %reduce-scatter.26.cloned.1.call-done = bf16[384,768]{1,0:T(8,128)(2,1)} async-done(((bf16[1536,768]{1,0:T(8,128)(2,1)}), bf16[384,768]{1,0:T(8,128)(2,1)}) %reduce-scatter.26.cloned.1.call-update) | async-done | bytes 589840 | tf_op jit(solution)/shard_map/reduce_scatter | solution.py:116
  599.7 24.4 %all-gather.33.cloned.1.call-done = bf16[1536,768]{1,0:T(8,128)(2,1)} async-done(((bf16[384,768]{1,0:T(8,128)(2,1)}), bf16[1536,768]{1,0:T(8,128)(2,1)}) %all-gather.33.cloned.1.call-update) | async-done | bytes 2359312 | tf_op jit(solution)/shard_map/all_gather | solution.py:165
  624.1 8.2 fusion.190
  637.4 32.7 %reduce-scatter.28.cloned.1.call-done = bf16[384,768]{1,0:T(8,128)(2,1)} async-done(((bf16[1536,768]{1,0:T(8,128)(2,1)}), bf16[384,768]{1,0:T(8,128)(2,1)}) %reduce-scatter.28.cloned.1.call-update) | async-done | bytes 589840 | tf_op jit(solution)/shard_map/reduce_scatter | solution.py:177
  676.0 22.5 %all-gather.35.cloned.1.call-done = bf16[1536,768]{1,0:T(8,128)(2,1)} async-done(((bf16[384,768]{1,0:T(8,128)(2,1)}), bf16[1536,768]{1,0:T(8,128)(2,1)}) %all-gather.35.cloned.1.call-update) | async-done | bytes 2359312 | tf_op jit(solution)/shard_map/all_gather | solution.py:189
  708.5 25.7 %while.54 = (s32[]{:T(128)}, f32[3,512,3,64]{1,3,2,0:T(8,128)}, bf16[3,512,3,64]{1,3,2,0:T(8,128)(2,1)}, f32[3,512,3,64]{1,3,2,0:T(8,128)}, bf16[3,512,3,64]{1,3...) while((s32[]{:T(128)}, f32[3,512,3,64]{1,3,2,0:T(8,128)}, ...), condition=%wide.region_29.30_spmd, body=%wide.region_27.29_spmd.sunk | while | flops 511179264 | bytes 31691948 | solution.py:83
  748.0 5.1 bitcast_convert_fusion.1
  753.2 32.8 %reduce-scatter.30.cloned.1.call-done = bf16[384,768]{1,0:T(8,128)(2,1)} async-done(((bf16[1536,768]{1,0:T(8,128)(2,1)}), bf16[384,768]{1,0:T(8,128)(2,1)}) %reduce-scatter.30.cloned.1.call-update) | async-done | bytes 589840 | tf_op jit(solution)/shard_map/reduce_scatter | solution.py:210
  789.6 24.0 %all-gather.37.cloned.1.call-done = bf16[1536,768]{1,0:T(8,128)(2,1)} async-done(((bf16[384,768]{1,0:T(8,128)(2,1)}), bf16[1536,768]{1,0:T(8,128)(2,1)}) %all-gather.37.cloned.1.call-update) | async-done | bytes 2359312 | tf_op jit(solution)/shard_map/all_gather | solution.py:165
  813.6 8.2 fusion.191
  826.8 32.7 %reduce-scatter.32.cloned.1.call-done = bf16[384,768]{1,0:T(8,128)(2,1)} async-done(((bf16[1536,768]{1,0:T(8,128)(2,1)}), bf16[384,768]{1,0:T(8,128)(2,1)}) %reduce-scatter.32.cloned.1.call-update) | async-done | bytes 589840 | tf_op jit(solution)/shard_map/reduce_scatter | solution.py:177
  864.4 4.8 fusion.120
  870.1 4.8 fusion.119
  875.2 4.6 copy.215
  880.1 4.6 fusion.118
  907.1 22.1 %while.55 = (s32[]{:T(128)}, f32[3,512,3,64]{1,3,2,0:T(8,128)}, bf16[3,512,3,64]{1,3,2,0:T(8,128)(2,1)S(1)}, f32[3,512,3,64]{1,3,2,0:T(8,128)}, bf16[3,512,3,64]...) while((s32[]{:T(128)}, f32[3,512,3,64]{1,3,2,0:T(8,128)}, ...), condition=%wide.region_38.39_spmd, body=%wide.region_36.38_spmd.sunk | while | flops 511179264 | bytes 26973300 | solution.py:83
  938.6 3.8 fusion.124
  943.8 4.7 copy.226
  948.5 3.9 reshape.286
  952.7 5.1 bitcast_convert_fusion
  961.0 102.8 %all-reduce.7.cloned.1.call-done = bf16[2,768,768]{1,0,2:T(2,128)(2,1)} async-done(((bf16[2,768,768]{1,0,2:T(2,128)(2,1)}), bf16[2,768,768]{1,0,2:T(2,128)(2,1)}) %all-reduce.7.cloned.1.call-update) | async-done | bytes 2359312
  1065.9 69.4 %reduce-scatter.36.cloned.1.call-done = bf16[2,96,768]{2,1,0:T(8,128)(2,1)} async-done(((bf16[2,768,768]{2,1,0:T(8,128)(2,1)}), bf16[2,96,768]{2,1,0:T(8,128)(2,1)}) %reduce-scatter.36.cloned.1.call-update) | async-done | bytes 294928 | tf_op jit(solution)/shard_map/reduce_scatter | solution.py:306
  1137.1 40.6 %psum.7 = f32[2,6,768]{2,0,1:T(2,128)S(1)} all-reduce(f32[2,6,768]{2,0,1:T(2,128)S(1)} %pad_maximum_fusion.4), channel_id=1, replica_groups=mesh['dp'=8,'tensor'=4] {'dp','tensor'}, use_global_device_ids=true, to_apply=%region_59.60 | all-reduce | flops 9216 | bytes 73728 | tf_op jit(solution)/shard_map/psum | solution.py:316
  1178.5 16.2 %all-reduce.2 = bf16[2,2,192]{2,1,0:T(2,128)(2,1)S(1)} all-reduce(bf16[2,2,192]{2,1,0:T(2,128)(2,1)S(1)} %pad_maximum_fusion.6), channel_id=23, replica_groups=mesh['dp'=8,'tensor'=4] {'dp'}, use_global_device_ids=true, to_apply=%region_45.46.clone | all-reduce | flops 768 | bytes 3072
  1195.4 4.8 reduce-scatter.40.cloned.1.call-done
  1202.0 67.7 %reduce-scatter.38.cloned.1.call-done = bf16[96,1152]{1,0:T(8,128)(2,1)} async-done(((bf16[768,1152]{1,0:T(8,128)(2,1)}), bf16[96,1152]{1,0:T(8,128)(2,1)}) %reduce-scatter.38.cloned.1.call-update) | async-done | bytes 221200
  1272.3 33.1 %reduce-scatter.34.cloned.1.call-done = bf16[384,768]{1,0:T(8,128)(2,1)} async-done(((bf16[1536,768]{1,0:T(8,128)(2,1)}), bf16[384,768]{1,0:T(8,128)(2,1)}) %reduce-scatter.34.cloned.1.call-update) | async-done | bytes 589840 | tf_op jit(solution)/shard_map/reduce_scatter | solution.py:210
  (501 shorter events, 249.9 us)
Async XLA Ops:
  8.0 95.9 %all-gather.25.cloned.1.call-start = ((), (), s32[]{:S(2)}) async-start(), calls=%async_computation.12 | async-start | bytes 2949120 | tf_op jit(solution)/shard_map/all_gather | solution.py:89
  8.7 169.9 %reduce-scatter.20.cloned.1.call-start = ((), (), s32[]{:S(2)}) async-start(), calls=%async_computation.13 | async-start | bytes 2949120 | tf_op jit(solution)/shard_map/reduce_scatter | solution.py:102
  11.3 34.5 %copy-start.73 = (bf16[2,2,24]{2,1,0:T(2,128)(2,1)S(1)}, bf16[2,2,24]{2,1,0:T(2,128)(2,1)}, u32[]{:S(2)}) copy-start(bf16[2,2,24]{2,1,0:T(2,128)(2,1)} %param.26) | copy-start | bytes 580
  11.4 62.6 %copy-start.47 = (bf16[2,192,96]{2,1,0:T(8,128)(2,1)S(1)}, bf16[2,192,96]{2,1,0:T(8,128)(2,1)}, u32[]{:S(2)}) copy-start(bf16[2,192,96]{2,1,0:T(8,128)(2,1)} %param.27) | copy-start | bytes 221188
  45.9 58.1 %copy-start.37 = (bf16[1,3,768,192]{2,3,1,0:T(8,128)(2,1)}, bf16[1,3,768,192]{2,3,1,0:T(8,128)(2,1)S(1)}, u32[]{:S(2)}) copy-start(bf16[1,3,768,192]{2,3,1,0:T(8,128)(2,1)S(1)} %copy.184) | copy-start | bytes 2654212
  129.6 49.0 %copy-start = (bf16[384,768]{1,0:T(8,128)(2,1)S(1)}, bf16[384,768]{1,0:T(8,128)(2,1)}, u32[]{:S(2)}) copy-start(bf16[384,768]{1,0:T(8,128)(2,1)} %param.23) | copy-start | bytes 1769476
  129.6 73.9 %all-gather.41.cloned.1.call-start = ((), (), s32[]{:S(2)}) async-start(), calls=%async_computation.29 | async-start | bytes 1327104 | tf_op jit(solution)/shard_map/all_gather | solution.py:267
  130.4 84.9 %all-gather.27.cloned.1.call-start = ((), (), s32[]{:S(2)}) async-start(), calls=%async_computation.14 | async-start | bytes 2949120 | tf_op jit(solution)/shard_map/all_gather | solution.py:111
  131.3 165.1 %copy-start.41 = (f32[768]{0:T(1024)}, f32[768]{0:T(1024)S(1)}, u32[]{:S(2)}) copy-start(f32[768]{0:T(1024)S(1)} %get-tuple-element.482) | copy-start | bytes 9220
  131.3 165.0 %copy-start.45 = (f32[768]{0:T(1024)}, f32[768]{0:T(1024)S(1)}, u32[]{:S(2)}) copy-start(f32[768]{0:T(1024)S(1)} %get-tuple-element.478) | copy-start | bytes 9220
  180.1 116.3 %copy-start.48 = (f32[384]{0:T(512)}, f32[384]{0:T(512)S(1)}, u32[]{:S(2)}) copy-start(f32[384]{0:T(512)S(1)} %broadcast_multiply_fusion.11) | copy-start | bytes 4612
  181.5 114.8 %copy-start.50 = (f32[384]{0:T(512)}, f32[384]{0:T(512)S(1)}, u32[]{:S(2)}) copy-start(f32[384]{0:T(512)S(1)} %add_rsqrt_fusion.3) | copy-start | bytes 4612
  182.7 75.1 %all-gather.43.cloned.1.call-start = ((), (), s32[]{:S(2)}) async-start(), calls=%async_computation.30 | async-start | bytes 1327104 | tf_op jit(solution)/shard_map/all_gather | solution.py:269
  183.5 112.8 %reduce-scatter.22.cloned.1.call-start = ((), (), s32[]{:S(2)}) async-start(), calls=%async_computation.15 | async-start | bytes 2949120 | tf_op jit(solution)/shard_map/reduce_scatter | solution.py:116
  203.5 27.0 %copy-start.68 = (f32[768]{0:T(1024)}, f32[768]{0:T(1024)S(1)}, u32[]{:S(2)}) copy-start(f32[768]{0:T(1024)S(1)} %convert_element_type.237) | copy-start | bytes 9220
  263.3 129.5 %all-gather.29.cloned.1.call-start = ((), (), s32[]{:S(2)}) async-start(), calls=%async_computation.16 | async-start | bytes 2949120 | tf_op jit(solution)/shard_map/all_gather | solution.py:89
  265.8 33.5 %copy-start.53 = (f32[768]{0:T(1024)}, f32[768]{0:T(1024)S(1)}, u32[]{:S(2)}) copy-start(f32[768]{0:T(1024)S(1)} %get-tuple-element.474) | copy-start | bytes 9220
  299.4 177.9 %reduce-scatter.24.cloned.1.call-start = ((), (), s32[]{:S(2)}) async-start(), calls=%async_computation.17 | async-start | bytes 2949120 | tf_op jit(solution)/shard_map/reduce_scatter | solution.py:102
  426.4 50.9 %copy-start.54 = (f32[768]{0:T(1024)S(1)}, f32[768]{0:T(1024)}, u32[]{:S(2)}) copy-start(f32[768]{0:T(1024)} %copy-done.53) | copy-start | bytes 9220
  426.4 50.9 %copy-start.56 = (f32[768]{0:T(1024)S(1)}, f32[768]{0:T(1024)}, u32[]{:S(2)}) copy-start(f32[768]{0:T(1024)} %get-tuple-element.481) | copy-start | bytes 9220
  428.6 50.5 %copy-start.52 = (f32[768]{0:T(1024)S(1)}, f32[768]{0:T(1024)}, u32[]{:S(2)}) copy-start(f32[768]{0:T(1024)} %get-tuple-element.479) | copy-start | bytes 9220
  428.6 58.7 %all-gather.45.cloned.1.call-start = ((), (), s32[]{:S(2)}) async-start(), calls=%async_computation.31 | async-start | bytes 1327104 | tf_op jit(solution)/shard_map/all_gather | solution.py:267
  429.4 84.5 %all-gather.31.cloned.1.call-start = ((), (), s32[]{:S(2)}) async-start(), calls=%async_computation.18 | async-start | bytes 2949120 | tf_op jit(solution)/shard_map/all_gather | solution.py:111
  480.2 75.6 %all-gather.47.cloned.1.call-start = ((), (), s32[]{:S(2)}) async-start(), calls=%async_computation.32 | async-start | bytes 1327104 | tf_op jit(solution)/shard_map/all_gather | solution.py:269
  480.8 113.6 %reduce-scatter.26.cloned.1.call-start = ((), (), s32[]{:S(2)}) async-start(), calls=%async_computation.19 | async-start | bytes 2949120 | tf_op jit(solution)/shard_map/reduce_scatter | solution.py:116
  561.2 33.2 %copy-start.57 = (f32[768]{0:T(1024)S(1)}, f32[768]{0:T(1024)}, u32[]{:S(2)}) copy-start(f32[768]{0:T(1024)} %get-tuple-element.475) | copy-start | bytes 9220
  561.3 35.2 %copy-start.55 = (f32[768]{0:T(1024)S(1)}, f32[768]{0:T(1024)}, u32[]{:S(2)}) copy-start(f32[768]{0:T(1024)} %get-tuple-element.471) | copy-start | bytes 9220
  561.3 62.8 %all-gather.33.cloned.1.call-start = ((), (), s32[]{:S(2)}) async-start(), calls=%async_computation.20 | async-start | bytes 2949120 | tf_op jit(solution)/shard_map/all_gather | solution.py:165
  599.7 70.5 %reduce-scatter.28.cloned.1.call-start = ((), (), s32[]{:S(2)}) async-start(), calls=%async_computation.21 | async-start | bytes 2949120 | tf_op jit(solution)/shard_map/reduce_scatter | solution.py:177
  637.3 61.1 %all-gather.35.cloned.1.call-start = ((), (), s32[]{:S(2)}) async-start(), calls=%async_computation.22 | async-start | bytes 2949120 | tf_op jit(solution)/shard_map/all_gather | solution.py:189
  674.0 111.9 %reduce-scatter.30.cloned.1.call-start = ((), (), s32[]{:S(2)}) async-start(), calls=%async_computation.23 | async-start | bytes 2949120 | tf_op jit(solution)/shard_map/reduce_scatter | solution.py:210
  753.1 32.8 %copy-start.14 = (f32[384,768]{1,0:T(8,128)S(1)}, f32[384,768]{1,0:T(8,128)}, u32[]{:S(2)}) copy-start(f32[384,768]{1,0:T(8,128)} %get-tuple-element.558) | copy-start | bytes 3538948
  753.1 60.4 %all-gather.37.cloned.1.call-start = ((), (), s32[]{:S(2)}) async-start(), calls=%async_computation.24 | async-start | bytes 2949120 | tf_op jit(solution)/shard_map/all_gather | solution.py:165
  789.1 70.4 %reduce-scatter.32.cloned.1.call-start = ((), (), s32[]{:S(2)}) async-start(), calls=%async_computation.25 | async-start | bytes 2949120 | tf_op jit(solution)/shard_map/reduce_scatter | solution.py:177
  826.7 32.9 %copy-start.1 = (bf16[384,768]{1,0:T(8,128)(2,1)S(1)}, bf16[384,768]{1,0:T(8,128)(2,1)}, u32[]{:S(2)}) copy-start(bf16[384,768]{1,0:T(8,128)(2,1)} %param.23) | copy-start | bytes 1769476
  826.7 32.9 %copy-start.11 = (bf16[384,768]{1,0:T(8,128)(2,1)S(1)}, bf16[384,768]{1,0:T(8,128)(2,1)}, u32[]{:S(2)}) copy-start(bf16[384,768]{1,0:T(8,128)(2,1)} %reduce-scatter.20.cloned.1.call-done) | copy-start | bytes 1769476
  826.7 32.9 %copy-start.42 = (f32[768]{0:T(1024)S(1)}, f32[768]{0:T(1024)}, u32[]{:S(2)}) copy-start(f32[768]{0:T(1024)} %copy-done.41) | copy-start | bytes 9220
  826.7 32.9 %copy-start.46 = (f32[768]{0:T(1024)S(1)}, f32[768]{0:T(1024)}, u32[]{:S(2)}) copy-start(f32[768]{0:T(1024)} %copy-done.45) | copy-start | bytes 9220
  826.7 32.9 %copy-start.49 = (f32[384]{0:T(512)S(1)}, f32[384]{0:T(512)}, u32[]{:S(2)}) copy-start(f32[384]{0:T(512)} %copy-done.48) | copy-start | bytes 4612
  826.7 32.9 %copy-start.51 = (f32[384]{0:T(512)S(1)}, f32[384]{0:T(512)}, u32[]{:S(2)}) copy-start(f32[384]{0:T(512)} %copy-done.50) | copy-start | bytes 4612
  826.7 65.8 %all-gather.39.cloned.1.call-start = ((), (), s32[]{:S(2)}) async-start(), calls=%async_computation.26 | async-start | bytes 2949120 | tf_op jit(solution)/shard_map/all_gather | solution.py:189
  864.0 95.5 %reduce-scatter.42.cloned.1.call-start = ((), (), s32[]{:S(2)}) async-start(), calls=%async_computation.35 | async-start | bytes 221184
  870.0 193.7 %all-reduce.7.cloned.1.call-start = ((), (), s32[]{:S(2)}) async-start(), calls=%async_computation.36 | async-start | bytes 4718592
  879.8 255.4 %reduce-scatter.36.cloned.1.call-start = ((), (), s32[]{:S(2)}) async-start(), calls=%async_computation.28 | async-start | bytes 2654208 | tf_op jit(solution)/shard_map/reduce_scatter | solution.py:306
  892.5 307.6 %reduce-scatter.40.cloned.1.call-start = ((), (), s32[]{:S(2)}) async-start(), calls=%async_computation.34 | async-start | bytes 663552
  933.3 336.4 %reduce-scatter.38.cloned.1.call-start = ((), (), s32[]{:S(2)}) async-start(), calls=%async_computation.33 | async-start | bytes 1990656
  952.4 352.9 %reduce-scatter.34.cloned.1.call-start = ((), (), s32[]{:S(2)}) async-start(), calls=%async_computation.27 | async-start | bytes 2949120 | tf_op jit(solution)/shard_map/reduce_scatter | solution.py:210
  1064.9 240.5 %copy-start.13 = (f32[384,768]{1,0:T(8,128)S(1)}, f32[384,768]{1,0:T(8,128)}, u32[]{:S(2)}) copy-start(f32[384,768]{1,0:T(8,128)} %copy-done.12) | copy-start | bytes 3538948
  (64 other events, 205.7 us)
Sparse Core Ops, SparseCore 0:
  10.4 26.5 all-gather.24
  129.7 48.8 reduce-scatter.19
  299.5 24.5 all-gather.28
  428.7 48.4 reduce-scatter.23
  561.4 33.0 reduce-scatter.25
  637.5 32.6 reduce-scatter.27
  753.3 32.6 reduce-scatter.29
  826.9 32.6 reduce-scatter.31
Sparse Core Ops, SparseCore 1:
  133.1 55.8 all-gather.40
  191.0 24.3 all-gather.26
  218.2 39.6 all-gather.42
  263.4 32.8 reduce-scatter.21
  431.9 55.4 all-gather.44
  489.6 24.3 all-gather.30
  516.2 39.6 all-gather.46
  599.8 24.3 all-gather.32
  674.1 24.3 all-gather.34
  789.2 24.3 all-gather.36
  864.1 24.3 all-gather.38
  892.7 58.9 reduce-scatter.41
  955.5 108.2 all-reduce.6
  1067.2 67.9 reduce-scatter.35
  1139.1 61.0 reduce-scatter.39
  1204.0 65.6 reduce-scatter.37
  1272.3 33.1 reduce-scatter.33
where the time goes:
time: 1330 us; the launch traced here: 1320 us
  waiting for transfers between devices  706 us (53%)
  blocking collectives  243 us (18%)
  matrix products  175 us (13%)
  local copies, waits for them, and re-layouts  106 us (8%)
  other arithmetic  62.7 us (5%)
  between operations  19.5 us (1%)
    unnamed x29, waiting for transfers between devices  178 us
    reduce_scatter x2, waiting for transfers between devices, forward_layer(): lax.psum_scatter(jnp.dot(context, weight_out, preferred_element_type=jnp....  94.5 us
    reduce_scatter x1, waiting for transfers between devices, body(): lax.psum_scatter(stacked[3].astype(jnp.bfloat16), 'dp', scatter_dimension...  69.4 us
    all_gather x2, blocking collectives, body(): lax.all_gather(qkv_weight[layer], 'dp', axis=1, tiled=True)  66.2 us
    reduce_scatter x2, waiting for transfers between devices, backward_layer(): lax.psum_scatter(jnp.einsum('cne,cde->nd', dproj_low, weight_qkv, preferr...  65.8 us
    reduce_scatter x2, waiting for transfers between devices, backward_layer(): lax.psum_scatter(jnp.einsum('nf,df->nd', dupper_low, weight_up, preferred...  65.5 us
    reduce_scatter x2, waiting for transfers between devices, forward_layer(): lax.psum_scatter(jnp.dot(active, weight_down, preferred_element_type=jnp....  63.6 us
    all_gather x2, waiting for transfers between devices, body(): lax.all_gather(down_weight[layer], 'dp', axis=1, tiled=True)  54.2 us
  transfers between devices with their start and end apart: 25, of which 20 were waited for; matrix products, arithmetic and copies ran while one was open for 13% of the time, Pallas kernels for 0%

commit v1 on v0

v1 whole, which is shorter than its diff:
```python
import functools

import jax
import jax.numpy as jnp
from jax import lax
from jax.experimental import pallas as pl
from jax.experimental.pallas import tpu as pltpu
from jax.sharding import PartitionSpec as P

HD = 64
PACK = 512
BLK = 128
WIN = 2 * PACK
EPS = 1e-05
NEG = -1e30
MESH = pl.DeviceIdType.MESH
BF = jnp.bfloat16
F32 = jnp.float32


def dot(a, b):
    return jnp.dot(a, b, preferred_element_type=F32)


def dot_nt(a, b):
    return lax.dot_general(a, b, (((1,), (1,)), ((), ())), preferred_element_type=F32)


def dot_tn(a, b):
    return lax.dot_general(a, b, (((0,), (0,)), ((), ())), preferred_element_type=F32)


def params(**kw):
    return pltpu.CompilerParams(vmem_limit_bytes=60 * 1024 * 1024, **kw)


def whole(shape):
    return pl.BlockSpec(shape, lambda t: (0,) * len(shape))


def per_t(shape, *rest):
    tail = rest if rest else (0,) * (len(shape) - 1)
    return pl.BlockSpec(shape, lambda t: (t,) + tail)


class Place:
    def __init__(self, n_dp):
        self.nz = n_dp // 2
        dp, tensor = lax.axis_index("dp"), lax.axis_index("tensor")
        self.dp, self.tensor = dp, tensor
        self.z, self.y = dp // 2, dp % 2
        self.x, self.c = tensor // 2, tensor % 2
        self.dp_y = 2 * self.z + 1 - self.y
        self.t_x = 2 * (1 - self.x) + self.c
        self.t_c = 2 * self.x + 1 - self.c
        self.t_xc = 2 * (1 - self.x) + 1 - self.c
        self.to_x = (dp, self.t_x)
        self.to_y = (self.dp_y, tensor)
        self.to_c = (dp, self.t_c)

    def d(self, z, same_y=True):
        return 2 * z + (self.y if same_y else 1 - self.y)


def greet(devices):
    barrier = pltpu.get_barrier_semaphore()
    for device in devices:
        pl.semaphore_signal(barrier, inc=1, device_id=device, device_id_type=MESH)
    pl.semaphore_wait(barrier, len(devices))


def gather_kernel(n_dp, own_ref, out_ref, own_sem, send_sem, recv_sem):
    me = Place(n_dp)
    nz = me.nz
    half = own_ref.shape[1] // 2
    barrier = pltpu.get_barrier_semaphore()
    for device in (me.to_x, me.to_y, me.to_c):
        pl.semaphore_signal(barrier, inc=1, device_id=device, device_id_type=MESH)

    @pl.when(me.z > 0)
    def _():
        pl.semaphore_signal(barrier, inc=1, device_id=(me.dp - 2, me.tensor), device_id_type=MESH)

    @pl.when(me.z < nz - 1)
    def _():
        pl.semaphore_signal(barrier, inc=1, device_id=(me.dp + 2, me.tensor), device_id_type=MESH)

    pl.semaphore_wait(barrier, 3 + (me.z > 0).astype(jnp.int32) + (me.z < nz - 1).astype(jnp.int32))

    def piece(t, d, part):
        if part is None:
            return out_ref.at[t, d]
        return out_ref.at[t, d, :, pl.ds(part * half, half)]

    def copy(source, t, d, part, route, z, device):
        slot = route * nz + z
        return pltpu.make_async_remote_copy(
            src_ref=source if source is not None else piece(t, d, part),
            dst_ref=piece(t, d, part),
            send_sem=send_sem.at[slot],
            recv_sem=recv_sem.at[slot],
            device_id=device,
            device_id_type=MESH,
        )

    mine = pltpu.make_async_copy(own_ref, out_ref.at[me.tensor, me.dp], own_sem)
    mine.start()

    def z_copy(p, up, source=None):
        return copy(source, me.tensor, me.d(p), None, 0, p, (me.dp + 2 if up else me.dp - 2, me.tensor))

    def x_copy(p, source=None):
        return copy(source, me.tensor, me.d(p), None, 1, p, me.to_x)

    def y_copy(p, source=None):
        return copy(source, me.tensor, me.d(p), None, 2, p, me.to_y)

    def first_copy(p):
        return copy(None, me.t_x, me.d(p), 0, 3, p, me.to_y)

    def second_copy(p):
        return copy(None, me.tensor, me.d(p, False), 1, 4, p, me.to_x)

    def core_copy(kind, p, source=None):
        t = me.tensor if kind in (0, 2) else me.t_x
        d = me.d(p, kind in (0, 1))
        part = {3: 0, 4: 1}.get(kind)
        return copy(source, t, d, part, 5 + kind, p, me.to_c)

    def arrived(t, d, part, slot):
        pltpu.make_async_copy(piece(t, d, part), piece(t, d, part), recv_sem.at[slot]).wait()

    def own_round():
        @pl.when(me.z < nz - 1)
        def _():
            z_copy(me.z, True, own_ref).start()

        @pl.when(me.z > 0)
        def _():
            copy(own_ref, me.tensor, me.dp, None, 10, me.z, (me.dp - 2, me.tensor)).start()

        x_copy(me.z, own_ref).start()
        y_copy(me.z, own_ref).start()
        core_copy(0, me.z, own_ref).start()

    def z_round(p, up, valid):
        @pl.when(valid)
        def _():
            arrived(me.tensor, me.d(p), None, (0 if up else 10) * nz + p)

            @pl.when(me.z < nz - 1 if up else me.z > 0)
            def _():
                if up:
                    z_copy(p, True).start()
                else:
                    copy(None, me.tensor, me.d(p), None, 10, p, (me.dp - 2, me.tensor)).start()

            x_copy(p).start()
            y_copy(p).start()
            core_copy(0, p).start()

    def xy_round(p, valid):
        @pl.when(valid)
        def _():
            arrived(me.t_x, me.d(p), None, nz + p)
            first_copy(p).start()
            core_copy(1, p).start()
            arrived(me.tensor, me.d(p, False), None, 2 * nz + p)
            second_copy(p).start()
            core_copy(2, p).start()

    def diagonal_round(p, valid):
        @pl.when(valid)
        def _():
            arrived(me.t_x, me.d(p, False), 0, 3 * nz + p)
            core_copy(3, p).start()
            arrived(me.t_x, me.d(p, False), 1, 4 * nz + p)
            core_copy(4, p).start()

    true = me.z >= 0
    own_round()
    for s in range(1, nz + 2):
        if s < nz:
            z_round(me.z - s, True, me.z - s >= 0)
            z_round(me.z + s, False, me.z + s < nz)
        if s == 1:
            xy_round(me.z, true)
        elif s - 1 < nz:
            xy_round(me.z - s + 1, me.z - s + 1 >= 0)
            xy_round(me.z + s - 1, me.z + s - 1 < nz)
        if s == 2:
            diagonal_round(me.z, true)
        elif 2 < s < nz + 2:
            diagonal_round(me.z - s + 2, me.z - s + 2 >= 0)
            diagonal_round(me.z + s - 2, me.z + s - 2 < nz)

    for p in range(nz):
        for kind in range(5):
            t = me.t_c if kind in (0, 2) else me.t_xc
            part = {3: 0, 4: 1}.get(kind)
            arrived(t, me.d(p, kind in (0, 1)), part, (5 + kind) * nz + p)

    mine.wait()
    for p in range(nz):
        @pl.when(jnp.logical_and(me.z < nz - 1, p <= me.z))
        def _():
            z_copy(p, True).wait_send()

        @pl.when(jnp.logical_and(me.z > 0, p >= me.z))
        def _():
            copy(None, me.tensor, me.d(p), None, 10, p, (me.dp - 2, me.tensor)).wait_send()

        x_copy(p).wait_send()
        y_copy(p).wait_send()
        first_copy(p).wait_send()
        second_copy(p).wait_send()
        for kind in range(5):
            core_copy(kind, p).wait_send()


def gather_weights(own, n_dp, n_tensor, collective_id):
    rows, cols = own.shape
    slots = 11 * (n_dp // 2)
    out = pl.pallas_call(
        functools.partial(gather_kernel, n_dp),
        out_shape=jax.ShapeDtypeStruct((n_tensor, n_dp, rows, cols), own.dtype),
        in_specs=[pl.BlockSpec(memory_space=pltpu.MemorySpace.HBM)],
        out_specs=pl.BlockSpec(memory_space=pltpu.MemorySpace.HBM),
        scratch_shapes=[
            pltpu.SemaphoreType.DMA,
            pltpu.SemaphoreType.DMA((slots,)),
            pltpu.SemaphoreType.DMA((slots,)),
        ],
        compiler_params=pltpu.CompilerParams(collective_id=collective_id, has_side_effects=True),
        name="gather_weights",
    )(own)
    return out.reshape(n_tensor, n_dp * rows, cols)


def scatter_kernel(
    n_dp, g_ref, out_ref, mine, core_in, first_in, second_in, x_in, y_in, z_in, load_sem, send_sem, recv_sem
):
    me = Place(n_dp)
    nz = me.nz
    cols = g_ref.shape[-1]
    half = cols // 2
    zs = [lax.rem(me.z + k, nz) for k in range(1, nz)] + [me.z]
    peers = [me.to_x, me.to_y, me.to_c] + [(me.d(z), me.tensor) for z in zs[:-1]]
    greet(peers)

    def owner(place, k):
        x_other, y_other = place in (0, 1), place in (0, 2)
        return x_other, me.d(zs[k], not y_other)

    def remote(source, target, slot, device):
        return pltpu.make_async_remote_copy(
            src_ref=source, dst_ref=target, send_sem=send_sem.at[slot], recv_sem=recv_sem.at[slot],
            device_id=device, device_id_type=MESH,
        )

    def to_core(place, k):
        x_other, d = owner(place, k)
        return remote(g_ref.at[me.t_xc if x_other else me.t_c, d], core_in.at[place, k], place * nz + k, me.to_c)

    def load(place, k):
        x_other, d = owner(place, k)
        return pltpu.make_async_copy(
            g_ref.at[me.t_x if x_other else me.tensor, d], mine.at[place, k], load_sem.at[place * nz + k]
        )

    for k in range(nz):
        for place in range(4):
            to_core(place, k).start()
            load(place, k).start()

    def first(k):
        return remote(mine.at[0, k, :, pl.ds(0, half)], first_in.at[k], 4 * nz + k, me.to_x)

    def second(k):
        return remote(mine.at[0, k, :, pl.ds(half, half)], second_in.at[k], 5 * nz + k, me.to_y)

    def along_x(k):
        return remote(mine.at[1, k], x_in.at[k], 6 * nz + k, me.to_x)

    def along_y(k):
        return remote(mine.at[2, k], y_in.at[k], 7 * nz + k, me.to_y)

    def along_z(k):
        return remote(mine.at[3, k], z_in.at[k], 8 * nz + k, (me.d(zs[k]), me.tensor))

    def both(place, k):
        load(place, k).wait()
        to_core(place, k).wait_recv()
        return mine[place, k].astype(F32) + core_in[place, k].astype(F32)

    for step in range(nz + 2):
        if step < nz:
            k = step
            mine[0, k] = both(0, k).astype(BF)
            first(k).start()
            second(k).start()
        if 0 <= step - 1 < nz:
            k = step - 1
            total = both(1, k)
            second(k).wait_recv()
            mine[1, k, :, :half] = total[:, :half].astype(BF)
            mine[1, k, :, half:] = (total[:, half:] + second_in[k].astype(F32)).astype(BF)
            along_x(k).start()
            total = both(2, k)
            first(k).wait_recv()
            mine[2, k, :, half:] = total[:, half:].astype(BF)
            mine[2, k, :, :half] = (total[:, :half] + first_in[k].astype(F32)).astype(BF)
            along_y(k).start()
        if 0 <= step - 2 < nz:
            k = step - 2
            total = both(3, k)
            along_x(k).wait_recv()
            total += x_in[k].astype(F32)
            along_y(k).wait_recv()
            total += y_in[k].astype(F32)
            if k < nz - 1:
                mine[3, k] = total.astype(BF)
                along_z(k).start()
            else:
                for j in range(nz - 1):
                    along_z(j).wait_recv()
                    total += z_in[j].astype(F32)
                out_ref[...] = total
    for k in range(nz):
        for place in range(4):
            to_core(place, k).wait_send()
        for made in (first, second, along_x, along_y):
            made(k).wait_send()
        if k < nz - 1:
            along_z(k).wait_send()


def scatter_grads(grads, n_dp, n_tensor, collective_id):
    cols = grads.shape[-1]
    rows = grads.shape[1] // n_dp
    nz = n_dp // 2
    return pl.pallas_call(
        functools.partial(scatter_kernel, n_dp),
        out_shape=jax.ShapeDtypeStruct((rows, cols), F32),
        in_specs=[pl.BlockSpec(memory_space=pltpu.MemorySpace.HBM)],
        out_specs=pl.BlockSpec(memory_space=pltpu.MemorySpace.VMEM),
        scratch_shapes=[
            pltpu.VMEM((4, nz, rows, cols), BF),
            pltpu.VMEM((4, nz, rows, cols), BF),
            pltpu.VMEM((nz, rows, cols // 2), BF),
            pltpu.VMEM((nz, rows, cols // 2), BF),
            pltpu.VMEM((nz, rows, cols), BF),
            pltpu.VMEM((nz, rows, cols), BF),
            pltpu.VMEM((nz - 1, rows, cols), BF),
            pltpu.SemaphoreType.DMA((4 * nz,)),
            pltpu.SemaphoreType.DMA((9 * nz,)),
            pltpu.SemaphoreType.DMA((9 * nz,)),
        ],
        compiler_params=params(collective_id=collective_id, has_side_effects=True),
        name="scatter_grads",
    )(grads.reshape(n_tensor, n_dp, rows, cols))


def window_slots(tokens, rows):
    t = lax.axis_index("tensor")
    count = tokens // BLK
    first = jnp.minimum(t * count * BLK // PACK, rows - 2)
    return [(t * count + j) * BLK // PACK - first for j in range(count)]


def lane_masks(first, count):
    slot = lax.broadcasted_iota(jnp.int32, (1, 256), 1) // HD
    return [(slot == first + i).astype(F32).astype(BF) for i in range(count)]


def stack_heads(block, masks):
    return jnp.concatenate([block * mask for mask in masks], axis=0)


def pick_heads(stacked, masks, size):
    total = None
    for i, mask in enumerate(masks):
        part = stacked[i * size : (i + 1) * size] * mask.astype(F32)
        total = part if total is None else total + part
    return total


def norm_forward(value, gain, shift):
    average = jnp.mean(value, axis=-1, keepdims=True)
    centered = value - average
    variance = jnp.mean(centered * centered, axis=-1, keepdims=True)
    scaled = lax.rsqrt(variance + EPS)
    unit = centered * scaled
    return unit * gain + shift, unit, scaled


def norm_back(grad, unit, scaled, gain):
    inner = grad * gain
    centered = inner - jnp.mean(inner, axis=-1, keepdims=True)
    return scaled * (centered - unit * jnp.mean(inner * unit, axis=-1, keepdims=True))


def attn_fwd_kernel(
    rows, win_ref, own_ref, g_ref, qb_ref, kvb_ref, qseg_ref, kseg_ref, vec_ref,
    q_ref, kv_ref, ctx_ref, mid_ref, unit_ref, rs_ref, acc_ref,
):
    step = pl.program_id(0)
    tokens = own_ref.shape[0]
    heads = 3
    kv_ref[0] = (dot(win_ref[...], g_ref[0, :, 384:768]) + kvb_ref[0]).astype(BF)
    q_ref[0] = (dot(own_ref[...].astype(BF), g_ref[0, :, 0:256]) + qb_ref[0]).astype(BF)
    q_masks, c_masks = lane_masks(0, heads), lane_masks(1, heads)
    for j, slot in enumerate(window_slots(tokens, rows)):
        here = pl.ds(j * BLK, BLK)
        keys = pl.ds(pl.multiple_of(slot * PACK, PACK), PACK)
        stacked = stack_heads(q_ref[0, here, :], q_masks)
        scores = dot_nt(stacked, kv_ref[0, keys, 0:256]) * (HD**-0.5)
        kseg = jnp.where(slot == 0, kseg_ref[0:1], kseg_ref[1:2])
        qseg = qseg_ref[here, :]
        allowed = jnp.logical_and(kseg >= 0, jnp.logical_or(kseg == qseg, qseg < 0))
        allowed = jnp.concatenate([allowed] * heads, axis=0)
        scores = jnp.where(allowed, scores, NEG)
        peak = jnp.max(scores, axis=-1, keepdims=True)
        weights = jnp.exp(scores - peak)
        probs = weights * (1.0 / jnp.sum(weights, axis=-1, keepdims=True))
        out = dot(probs.astype(BF), kv_ref[0, keys, 128:384])
        ctx_ref[0, here, :] = pick_heads(out, c_masks, BLK).astype(BF)
    part = dot_nt(ctx_ref[0], g_ref[0, :, 128:384])

    @pl.when(step == 0)
    def _():
        acc_ref[...] = part

    @pl.when(step > 0)
    def _():
        acc_ref[...] += part

    @pl.when(step == pl.num_programs(0) - 1)
    def _():
        total = own_ref[...].astype(F32) + acc_ref[...] + vec_ref[0:1]
        mid_ref[...], unit_ref[...], rs_ref[...] = norm_forward(total, vec_ref[1:2], vec_ref[2:3])


def attn_fwd(win, own, g, qb, kvb, qseg, kseg, vec, rows):
    n, tokens, dim = g.shape[0], own.shape[0], own.shape[1]
    last = g.shape[2] // dim - 1
    return pl.pallas_call(
        functools.partial(attn_fwd_kernel, rows),
        grid=(n,),
        in_specs=[
            whole(win.shape), whole(own.shape), per_t((1, dim, dim), 0, last),
            per_t((1, 1, 256)), per_t((1, 1, 384)), whole(qseg.shape), whole(kseg.shape), whole(vec.shape),
        ],
        out_specs=[
            per_t((1, tokens, 256)), per_t((1, WIN, 384)), per_t((1, tokens, 256)),
            whole((tokens, dim)), whole((tokens, dim)), whole((tokens, 1)),
        ],
        out_shape=[
            jax.ShapeDtypeStruct((n, tokens, 256), BF), jax.ShapeDtypeStruct((n, WIN, 384), BF),
            jax.ShapeDtypeStruct((n, tokens, 256), BF), jax.ShapeDtypeStruct((tokens, dim), F32),
            jax.ShapeDtypeStruct((tokens, dim), F32), jax.ShapeDtypeStruct((tokens, 1), F32),
        ],
        scratch_shapes=[pltpu.VMEM((tokens, dim), F32)],
        compiler_params=params(),
        name="attn_fwd",
    )(win, own, g, qb, kvb, qseg, kseg, vec)


def ffn_fwd_kernel(
    mid_ref, up_ref, down_ref, ub_ref, vec_ref, act_ref, slope_ref, out_ref, low_ref, unit_ref, rs_ref, acc_ref
):
    step = pl.program_id(0)
    upper = dot(mid_ref[...].astype(BF), up_ref[0]) + ub_ref[0]
    half = 0.5 + 0.5 * lax.erf(upper * (0.5**0.5))
    act_ref[0] = (upper * half).astype(BF)
    slope_ref[0] = (half + upper * (jnp.exp(-0.5 * upper * upper) * 0.3989422804014327)).astype(BF)
    part = dot_nt(act_ref[0], down_ref[0])

    @pl.when(step == 0)
    def _():
        acc_ref[...] = part

    @pl.when(step > 0)
    def _():
        acc_ref[...] += part

    @pl.when(step == pl.num_programs(0) - 1)
    def _():
        total = mid_ref[...] + acc_ref[...] + vec_ref[3:4]
        out, unit_ref[...], rs_ref[...] = norm_forward(total, vec_ref[4:5], vec_ref[5:6])
        out_ref[...] = out
        low_ref[...] = out.astype(BF)


def ffn_fwd(mid, g, ub, vec):
    n, (tokens, dim) = g.shape[0], mid.shape
    return pl.pallas_call(
        ffn_fwd_kernel,
        grid=(n,),
        in_specs=[
            whole(mid.shape), per_t((1, dim, dim), 0, 0), per_t((1, dim, dim), 0, 1), per_t((1, 1, dim)), whole(vec.shape),
        ],
        out_specs=[
            per_t((1, tokens, dim)), per_t((1, tokens, dim)),
            whole((tokens, dim)), whole((tokens, dim)), whole((tokens, dim)), whole((tokens, 1)),
        ],
        out_shape=[
            jax.ShapeDtypeStruct((n, tokens, dim), BF), jax.ShapeDtypeStruct((n, tokens, dim), BF),
            jax.ShapeDtypeStruct((tokens, dim), F32), jax.ShapeDtypeStruct((tokens, dim), BF),
            jax.ShapeDtypeStruct((tokens, dim), F32), jax.ShapeDtypeStruct((tokens, 1), F32),
        ],
        scratch_shapes=[pltpu.VMEM((tokens, dim), F32)],
        compiler_params=params(),
        name="ffn_fwd",
    )(mid, g, g, ub, vec)


def column_sum(value):
    return jnp.sum(value, axis=0, keepdims=True)


def ffn_bwd_kernel(
    grad_ref, mid_ref, unit2_ref, rs2_ref, unit1_ref, rs1_ref, up_ref, down_ref, act_ref, slope_ref, vec_ref,
    dg_ref, ub_ref, dvec_ref, dfirst_ref, acc_ref, low_ref, low_t_ref, mid_t_ref,
):
    step = pl.program_id(0)
    dim = grad_ref.shape[1]

    @pl.when(step == 0)
    def _():
        grad = grad_ref[...]
        dsecond = norm_back(grad, unit2_ref[...], rs2_ref[...], vec_ref[4:5])
        dvec_ref[4:5] = column_sum(grad * unit2_ref[...])
        dvec_ref[5:6] = column_sum(grad)
        dvec_ref[3:4] = column_sum(dsecond)
        dvec_ref[6:8] = jnp.zeros((2, dim), F32)
        acc_ref[...] = dsecond
        low_ref[...] = dsecond.astype(BF)
        low_t_ref[...] = dsecond.T.astype(BF)
        mid_t_ref[...] = mid_ref[...].T.astype(BF)

    dupper = dot(low_ref[...], down_ref[0]) * slope_ref[0].astype(F32)
    ub_ref[0] = column_sum(dupper)
    dupper_low = dupper.astype(BF)
    dg_ref[0, :, 0:dim] = dot(mid_t_ref[...], dupper_low).astype(BF)
    dg_ref[0, :, dim : 2 * dim] = dot(low_t_ref[...], act_ref[0]).astype(BF)
    acc_ref[...] += dot_nt(dupper_low, up_ref[0])

    @pl.when(step == pl.num_programs(0) - 1)
    def _():
        dmid = acc_ref[...]
        dfirst = norm_back(dmid, unit1_ref[...], rs1_ref[...], vec_ref[1:2])
        dvec_ref[1:2] = column_sum(dmid * unit1_ref[...])
        dvec_ref[2:3] = column_sum(dmid)
        dvec_ref[0:1] = column_sum(dfirst)
        dfirst_ref[...] = dfirst


def ffn_bwd(grad, mid, unit2, rs2, unit1, rs1, g, act, slope, vec):
    n, (tokens, dim) = g.shape[0], mid.shape
    full = whole((tokens, dim))
    return pl.pallas_call(
        ffn_bwd_kernel,
        grid=(n,),
        in_specs=[
            full, full, full, whole((tokens, 1)), full, whole((tokens, 1)),
            per_t((1, dim, dim), 0, 0), per_t((1, dim, dim), 0, 1),
            per_t((1, tokens, dim)), per_t((1, tokens, dim)), whole(vec.shape),
        ],
        out_specs=[per_t((1, dim, 2 * dim), 0, 0), per_t((1, 1, dim)), whole((8, dim)), full],
        out_shape=[
            jax.ShapeDtypeStruct(g.shape, BF), jax.ShapeDtypeStruct((n, 1, dim), F32),
            jax.ShapeDtypeStruct((8, dim), F32), jax.ShapeDtypeStruct((tokens, dim), F32),
        ],
        scratch_shapes=[
            pltpu.VMEM((tokens, dim), F32), pltpu.VMEM((tokens, dim), BF),
            pltpu.VMEM((dim, tokens), BF), pltpu.VMEM((dim, tokens), BF),
        ],
        compiler_params=params(),
        name="ffn_bwd",
    )(grad, mid, unit2, rs2, unit1, rs1, g, g, act, slope, vec)


def attn_bwd_kernel(
    rows, dg_in, dfirst_ref, own_ref, win_ref, g_ref, q_ref, kv_ref, ctx_ref, qseg_ref, kseg_ref,
    dg_ref, qb_ref, vb_ref, own_grad_ref, win_grad_ref, low_ref, low_t_ref, own_t_ref, win_t_ref, dctx_ref, dq_ref, dkv_ref,
):
    step = pl.program_id(0)
    tokens = own_ref.shape[0]
    heads = 3

    @pl.when(step == 0)
    def _():
        dfirst = dfirst_ref[...]
        low_ref[...] = dfirst.astype(BF)
        low_t_ref[...] = dfirst.T.astype(BF)
        own_t_ref[...] = own_ref[...].astype(F32).T.astype(BF)
        win_t_ref[...] = win_ref[...].astype(F32).T.astype(BF)
        own_grad_ref[...] = dfirst
        win_grad_ref[...] = jnp.zeros(win_grad_ref.shape, F32)

    dctx_ref[...] = dot(low_ref[...], g_ref[0, :, 128:384]).astype(BF)
    dkv_ref[...] = jnp.zeros(dkv_ref.shape, F32)
    q_masks, c_masks = lane_masks(0, heads), lane_masks(1, heads)
    for j, slot in enumerate(window_slots(tokens, rows)):
        here = pl.ds(j * BLK, BLK)
        keys = pl.ds(pl.multiple_of(slot * PACK, PACK), PACK)
        q_stack = stack_heads(q_ref[0, here, :], q_masks)
        d_stack = stack_heads(dctx_ref[here, :], c_masks)
        scores = dot_nt(kv_ref[0, keys, 0:256], q_stack) * (HD**-0.5)
        kseg = kseg_ref[keys, :]
        qseg = qseg_ref[j : j + 1, :]
        allowed = jnp.logical_and(kseg >= 0, jnp.logical_or(kseg == qseg, qseg < 0))
        allowed = jnp.concatenate([allowed] * heads, axis=1)
        scores = jnp.where(allowed, scores, NEG)
        peak = jnp.max(scores, axis=0, keepdims=True)
        weights = jnp.exp(scores - peak)
        probs = weights * (1.0 / jnp.sum(weights, axis=0, keepdims=True))
        dprobs = dot_nt(kv_ref[0, keys, 128:384], d_stack)
        weighted = probs * dprobs
        inner = jnp.sum(weighted, axis=0, keepdims=True)
        dscores = ((weighted - probs * inner) * (HD**-0.5)).astype(BF)
        dkv_ref[keys, 128:384] += dot(probs.astype(BF), d_stack)
        dkv_ref[keys, 0:256] += dot(dscores, q_stack)
        dq_ref[here, :] = pick_heads(dot_tn(dscores, kv_ref[0, keys, 0:256]), q_masks, BLK)
    dq, dkv = dq_ref[...], dkv_ref[...]
    qb_ref[0] = column_sum(dq)
    vb_ref[0] = column_sum(dkv)
    dq_low, dkv_low = dq.astype(BF), dkv.astype(BF)
    grad_q = dot(own_t_ref[...], dq_low)
    grad_o = dot(low_t_ref[...], ctx_ref[0])
    dg_ref[0, :, 0:128] = grad_q[:, 0:128].astype(BF)
    dg_ref[0, :, 128:256] = (grad_q[:, 128:256] + grad_o[:, 0:128]).astype(BF)
    dg_ref[0, :, 256:384] = grad_o[:, 128:256].astype(BF)
    dg_ref[0, :, 384:768] = dot(win_t_ref[...], dkv_low).astype(BF)
    own_grad_ref[...] += dot_nt(dq_low, g_ref[0, :, 0:256])
    win_grad_ref[...] += dot_nt(dkv_low, g_ref[0, :, 384:768])


def attn_bwd(dg, dfirst, own, win, g, q, kv, ctx, qseg, kseg, rows):
    n, (tokens, dim) = g.shape[0], own.shape
    last = g.shape[2] // dim - 1
    return pl.pallas_call(
        functools.partial(attn_bwd_kernel, rows),
        grid=(n,),
        in_specs=[
            pl.BlockSpec(memory_space=pl.ANY), whole((tokens, dim)), whole((tokens, dim)), whole(win.shape),
            per_t((1, dim, dim), 0, last), per_t((1, tokens, 256)), per_t((1, WIN, 384)), per_t((1, tokens, 256)),
            whole(qseg.shape), whole(kseg.shape),
        ],
        out_specs=[
            per_t((1, dim, dim), 0, last), per_t((1, 1, 256)), per_t((1, 1, 384)),
            whole((tokens, dim)), whole((WIN, dim)),
        ],
        out_shape=[
            jax.ShapeDtypeStruct(dg.shape, BF), jax.ShapeDtypeStruct((n, 1, 256), F32),
            jax.ShapeDtypeStruct((n, 1, 384), F32), jax.ShapeDtypeStruct((tokens, dim), F32),
            jax.ShapeDtypeStruct((WIN, dim), F32),
        ],
        scratch_shapes=[
            pltpu.VMEM((tokens, dim), BF), pltpu.VMEM((dim, tokens), BF), pltpu.VMEM((dim, tokens), BF),
            pltpu.VMEM((dim, WIN), BF), pltpu.VMEM((tokens, 256), BF), pltpu.VMEM((tokens, 256), F32),
            pltpu.VMEM((WIN, 384), F32),
        ],
        input_output_aliases={0: 0},
        compiler_params=params(),
        name="attn_bwd",
    )(dg, dfirst, own, win, g, q, kv, ctx, qseg, kseg)


def body(n_dp, n_tensor, block_input, passage_lengths, qkv_weight, qv_bias, out_weight, out_bias, first_gain,
         first_shift, up_weight, up_bias, down_weight, down_bias, second_gain, second_shift, output_grad):
    layers = qkv_weight.shape[0]
    tokens, dim = block_input.shape
    rows, segments = passage_lengths.shape
    t = lax.axis_index("tensor")
    dp = lax.axis_index("dp")
    shard, units = qkv_weight.shape[2], qkv_weight.shape[3]
    hidden_units = up_weight.shape[2]

    packs = [
        jnp.concatenate(
            [up_weight[l], down_weight[l].T, qkv_weight[l, 0], out_weight[l].T, qkv_weight[l, 1], qkv_weight[l, 2]], axis=1
        )
        for l in range(layers)
    ]
    small = jnp.concatenate([qv_bias.reshape(layers, -1), up_bias], axis=1)
    small = lax.all_gather(small, ("tensor", "dp"), axis=0).astype(F32)
    small = small.reshape(n_tensor, n_dp, layers, -1)
    piece = qv_bias.shape[2]
    qv = small[..., : 2 * piece].reshape(n_tensor, n_dp, layers, 2, piece).transpose(2, 3, 0, 1, 4)
    qv = qv.reshape(layers, 2, n_tensor, 1, units)
    q_bias = jnp.pad(qv[:, 0], ((0, 0), (0, 0), (0, 0), (0, 256 - units)))
    kv_bias = jnp.pad(qv[:, 1], ((0, 0), (0, 0), (0, 0), (units, 0)))
    u_bias = small[..., 2 * piece :].transpose(2, 0, 1, 3).reshape(layers, n_tensor, 1, hidden_units)

    zero = jnp.zeros((1, dim), F32)
    vecs = [
        jnp.concatenate(
            [v[l : l + 1] for v in (out_bias, first_gain, first_shift, down_bias, second_gain, second_shift)] + [zero, zero],
            axis=0,
        )
        for l in range(layers)
    ]

    ends = jnp.cumsum(passage_lengths, axis=1, dtype=jnp.int32)
    places = jnp.arange(PACK, dtype=jnp.int32)
    seg = jnp.sum((places[None, :, None] >= ends[:, None, :]).astype(jnp.int32), axis=2, dtype=jnp.int32)
    seg = jnp.where(seg == segments, -1, seg)
    first_row = jnp.minimum(t * tokens // PACK, rows - 2)
    kseg = lax.dynamic_slice(seg, (first_row, 0), (2, PACK))
    kcol = kseg.reshape(WIN, 1)
    qseg = lax.dynamic_slice(seg.reshape(-1), (t * tokens,), (tokens,))
    qcol = qseg.reshape(tokens, 1)
    qrow = qseg.reshape(tokens // BLK, BLK)

    pad = PACK // 2
    start = pad + first_row * PACK - (t - 1) * tokens
    up = [(i, i + 1) for i in range(n_tensor - 1)]
    down = [(i + 1, i) for i in range(n_tensor - 1)]
    edge = jnp.zeros((pad, dim), BF)

    def window(low):
        before = lax.ppermute(low, "tensor", up)
        after = lax.ppermute(low, "tensor", down)
        line = jnp.concatenate([edge, before, low, after, edge], axis=0)
        return lax.dynamic_slice(line, (start, 0), (WIN, dim))

    def window_back(own_grad, win_grad):
        line = lax.dynamic_update_slice(jnp.zeros((2 * pad + 3 * tokens, dim), F32), win_grad, (start, 0))
        before = lax.ppermute(line[pad : pad + tokens].astype(BF), "tensor", down)
        after = lax.ppermute(line[pad + 2 * tokens : pad + 3 * tokens].astype(BF), "tensor", up)
        return own_grad + line[pad + tokens : pad + 2 * tokens] + before.astype(F32) + after.astype(F32)

    own, win = block_input, window(block_input)
    kept = []
    for l in range(layers):
        g = gather_weights(packs[l], n_dp, n_tensor, 0)
        q, kv, ctx, mid, unit1, rs1 = attn_fwd(win, own, g, q_bias[l], kv_bias[l], qcol, kseg, vecs[l], rows)
        act, slope, out, low, unit2, rs2 = ffn_fwd(mid, g, u_bias[l], vecs[l])
        kept.append((own, win, g, q, kv, ctx, mid, unit1, rs1, act, slope, unit2, rs2))
        own = out
        if l < layers - 1:
            win = window(low)
    block_output = own

    grad = output_grad
    pieces, smalls = [None] * layers, [None] * layers
    for l in reversed(range(layers)):
        own, win, g, q, kv, ctx, mid, unit1, rs1, act, slope, unit2, rs2 = kept[l]
        dg, ub, dvec, dfirst = ffn_bwd(grad, mid, unit2, rs2, unit1, rs1, g, act, slope, vecs[l])
        dg, qb, vb, own_grad, win_grad = attn_bwd(dg, dfirst, own, win, g, q, kv, ctx, qrow, kcol, rows)
        grad = window_back(own_grad, win_grad)
        pieces[l] = scatter_grads(dg, n_dp, n_tensor, 1)
        smalls[l] = jnp.concatenate(
            [dvec[:6].reshape(-1), qb[:, 0, :units].reshape(-1), vb[:, 0, units:].reshape(-1), ub.reshape(-1)]
        )
    totals = lax.psum(jnp.stack(smalls), ("dp", "tensor"))
    vec_totals = totals[:, : 6 * dim].reshape(layers, 6, dim)
    qv_totals = totals[:, 6 * dim : 6 * dim + 2 * n_tensor * units].reshape(layers, 2, n_tensor * units)
    u_totals = totals[:, 6 * dim + 2 * n_tensor * units :]
    qv_grad = lax.dynamic_slice(qv_totals, (0, 0, (t * n_dp + dp) * piece), (layers, 2, piece))
    wide = up_bias.shape[1]
    u_grad = lax.dynamic_slice(u_totals, (0, (t * n_dp + dp) * wide), (layers, wide))

    both = jnp.stack(pieces)
    base = 2 * hidden_units
    cols = [both[:, :, base + i * units : base + (i + 1) * units] for i in range(4)]
    return (
        block_output,
        grad,
        jnp.stack([cols[0], cols[2], cols[3]], axis=1),
        qv_grad,
        cols[1].transpose(0, 2, 1),
        vec_totals[:, 0],
        vec_totals[:, 1],
        vec_totals[:, 2],
        both[:, :, :hidden_units],
        u_grad,
        both[:, :, hidden_units:base].transpose(0, 2, 1),
        vec_totals[:, 3],
        vec_totals[:, 4],
        vec_totals[:, 5],
    )


def solution(mesh):
    n_dp, n_tensor = mesh.shape["dp"], mesh.shape["tensor"]
    tokens = P(("dp", "tensor"), None)
    in_specs = (
        tokens, P("dp", None), P(None, None, "dp", "tensor"), P(None, None, ("tensor", "dp")), P(None, "tensor", "dp"),
        P(), P(), P(), P(None, "dp", "tensor"), P(None, ("tensor", "dp")), P(None, "tensor", "dp"), P(), P(), P(), tokens,
    )
    out_specs = (
        tokens, tokens, P(None, None, "dp", "tensor"), P(None, None, ("tensor", "dp")), P(None, "tensor", "dp"),
        P(), P(), P(), P(None, "dp", "tensor"), P(None, ("tensor", "dp")), P(None, "tensor", "dp"), P(), P(), P(),
    )
    return jax.shard_map(
        functools.partial(body, n_dp, n_tensor), mesh=mesh, in_specs=in_specs, out_specs=out_specs, check_vma=False
    )
```

time: 1330 us -> 701 us (0.53)
  waiting for transfers between devices: 706 us -> 124 us
  Pallas kernels: 0 us -> 426 us
  blocking collectives: 243 us -> 59.3 us
  matrix products: 175 us -> 0 us
  local copies, waits for them, and re-layouts: 106 us -> 33 us
  other arithmetic: 62.7 us -> 13.3 us
  starting transfers between devices: 2.61 us -> 22.7 us
    pallas_call x0 -> x12, Pallas kernels: none -> 426 us  [the longest x2 142 us: scatter_grads(): pl.pallas_call(functools.partial(scatter_kernel, n_dp), out_shape=jax.Sha...]
    reduce_scatter x9 -> x0, waiting for transfers between devices: 359 us -> none  [the longest x2 94.5 us: forward_layer(): lax.psum_scatter(jnp.dot(context, weight_out, preferred_element_type=jnp....]
    unnamed x29 -> x1, waiting for transfers between devices: 178 us -> 0.02 us
    dot_general x65 -> x0, matrix products: 171 us -> none  [the longest x2 30.3 us: forward_layer(): jnp.dot(gathered_mid, weight_up, preferred_element_type=jnp.float32)]
    all_gather x12 -> x0, waiting for transfers between devices: 169 us -> none  [the longest x2 54.2 us: body(): lax.all_gather(down_weight[layer], 'dp', axis=1, tiled=True)]
    psum x0 -> x1, waiting for transfers between devices: none -> 117 us  [body(): totals = lax.psum(jnp.stack(smalls), ('dp', 'tensor'))]
    all_gather x6 -> x1, blocking collectives: 168 us -> 59.3 us  [body(): small = lax.all_gather(small, ('tensor', 'dp'), axis=0).astype(F32)]
    psum x1 -> x0, blocking collectives: 40.6 us -> none  [body(): totals = lax.psum(jnp.stack(vector_list), ('dp', 'tensor'))]
  transfers between devices with their start and end apart: 25 -> 9, of which waited for: 20 -> 2; matrix products, arithmetic and copies ran while one was open for 13% -> 4% of each run, Pallas kernels for 0% -> 40%
where the time goes in v1:
time: 701 us; the launch traced here: 693 us
  Pallas kernels  426 us (61%)
  waiting for transfers between devices  124 us (18%)
  blocking collectives  59.3 us (8%)
  local copies, waits for them, and re-layouts  33 us (5%)
  starting transfers between devices  22.7 us (3%)
  between operations  15 us (2%)
  other arithmetic  13.3 us (2%)
    pallas_call x2, Pallas kernels, scatter_grads(): pl.pallas_call(functools.partial(scatter_kernel, n_dp), out_shape=jax.Sha...  142 us
    pallas_call x2, Pallas kernels, gather_weights(): pl.pallas_call(functools.partial(gather_kernel, n_dp), out_shape=jax.Shap...  137 us
    psum x1, waiting for transfers between devices, body(): totals = lax.psum(jnp.stack(smalls), ('dp', 'tensor'))  117 us
    all_gather x1, blocking collectives, body(): small = lax.all_gather(small, ('tensor', 'dp'), axis=0).astype(F32)  59.3 us
    pallas_call x2, Pallas kernels, attn_bwd(): pl.pallas_call(functools.partial(attn_bwd_kernel, rows), grid=(n,), in_sp...  54 us
    pallas_call x2, Pallas kernels, ffn_bwd(): pl.pallas_call(ffn_bwd_kernel, grid=(n,), in_specs=[full, full, full, who...  35.1 us
    pallas_call x2, Pallas kernels, attn_fwd(): pl.pallas_call(functools.partial(attn_fwd_kernel, rows), grid=(n,), in_sp...  34.4 us
    pallas_call x2, Pallas kernels, ffn_fwd(): pl.pallas_call(ffn_fwd_kernel, grid=(n,), in_specs=[whole(mid.shape), per...  24 us
  transfers between devices with their start and end apart: 9, of which 2 were waited for; matrix products, arithmetic and copies ran while one was open for 4% of the time, Pallas kernels for 40%

profile of v1, /device:TPU:1, one launch (start us, length us, event | category | flops | bytes accessed | tf_op | source)
XLA Modules:
  0.0 693.4 jit_solution(15016868778879568842)
XLA Ops:
  7.2 4.5 collective-permute-start
  11.7 1.9 collective-permute-start.1
  13.7 0.8 reshape.93
  15.2 59.3 %all-gather.1 = bf16[32,2,144]{2,1,0:T(2,128)(2,1)S(1)} all-gather(bf16[1,2,144]{2,1,0:T(2,128)(2,1)S(1)} %maximum_bitcast_fusion.4), channel_id=2, replica_groups=mesh['dp'=8,'tensor'=4] {'tensor','dp'}, dimensions={0}, use_global_device_ids=true | all-gather | bytes 19008 | tf_op jit(solution)/shard_map/all_gather | solution.py:688
  74.6 1.0 slice_bitcast_fusion.1
  75.6 1.0 slice_bitcast_fusion
  76.6 0.9 slice_bitcast_fusion.4
  77.6 0.8 fusion.11
  78.5 0.9 concatenate.28.own_ref
  79.4 71.0 %gather_weights.2 = bf16[4,8,96,2304]{3,2,1,0:T(8,128)(2,1)} custom-call(bf16[96,2304]{1,0:T(8,128)(2,1)} %concatenate.28.own_ref), custom_call_target="tpu_custom_call" | custom-call | tf_op jit(solution)/shard_map/gather_weights/pallas_call | solution.py:224
  151.1 0.8 reshape.121.qseg_ref
  155.4 1.3 constant_dynamic-slice_fusion.3.win_ref
  156.7 17.1 %attn_fwd.2 = (bf16[4,384,256]{2,1,0:T(8,128)(2,1)}, bf16[4,1024,384]{2,1,0:T(8,128)(2,1)}, bf16[4,384,256]{2,1,0:T(8,128)(2,1)}, f32[384,768]{1,0:T(8,128)}, f32[384,768]{1,0:T(8,128)}, /*index=5*/f32[384,1]{1,0:T(8,128)}) custom-call(bf16[1024,768]{1,0:T(8,128)(2,1)} %constant_dynamic-slice_fusion.3.win_ref, bf16[384,768]{1,0:T(8,128)(2,1)} %own_ref.3, ...), custom_call_target="tpu_custom_call" | custom-call | tf_op jit(solution)/shard_map/attn_fwd/pallas_call | solution.py:447
  173.8 12.0 %ffn_fwd.2 = (bf16[4,384,768]{2,1,0:T(8,128)(2,1)}, bf16[4,384,768]{2,1,0:T(8,128)(2,1)}, f32[384,768]{1,0:T(8,128)}, bf16[384,768]{1,0:T(8,128)(2,1)}, f32[384,768]{1,0:T(8,128)}, /*index=5*/f32[384,1]{1,0:T(8,128)}) custom-call(f32[384,768]{1,0:T(8,128)} %get-tuple-element.55.mid_ref, bf16[4,768,2304]{2,1,0:T(8,128)(2,1)} %bitcast.103, ...), custom_call_target="tpu_custom_call" | custom-call | tf_op jit(solution)/shard_map/ffn_fwd/pallas_call | solution.py:497
  185.8 2.0 collective-permute-start.2
  187.9 0.9 concatenate.32.own_ref
  188.8 66.1 %gather_weights.3 = bf16[4,8,96,2304]{3,2,1,0:T(8,128)(2,1)} custom-call(bf16[96,2304]{1,0:T(8,128)(2,1)} %concatenate.32.own_ref), custom_call_target="tpu_custom_call" | custom-call | tf_op jit(solution)/shard_map/gather_weights/pallas_call | solution.py:224
  255.7 2.2 collective-permute-start.3
  257.9 1.0 copy.74
  260.3 6.5 collective-permute-done.3
  266.9 1.2 constant_dynamic-slice_fusion.2.win_ref
  268.2 17.2 %attn_fwd.3 = (bf16[4,384,256]{2,1,0:T(8,128)(2,1)}, bf16[4,1024,384]{2,1,0:T(8,128)(2,1)}, bf16[4,384,256]{2,1,0:T(8,128)(2,1)}, f32[384,768]{1,0:T(8,128)}, f32[384,768]{1,0:T(8,128)}, /*index=5*/f32[384,1]{1,0:T(8,128)}) custom-call(bf16[1024,768]{1,0:T(8,128)(2,1)} %constant_dynamic-slice_fusion.2.win_ref, f32[384,768]{1,0:T(8,128)} %get-tuple-element.57.own_ref, ...), custom_call_target="tpu_custom_call" | custom-call | tf_op jit(solution)/shard_map/attn_fwd/pallas_call | solution.py:447
  285.4 12.0 %ffn_fwd.3 = (bf16[4,384,768]{2,1,0:T(8,128)(2,1)}, bf16[4,384,768]{2,1,0:T(8,128)(2,1)}, f32[384,768]{1,0:T(8,128)}, bf16[384,768]{1,0:T(8,128)(2,1)}, f32[384,768]{1,0:T(8,128)}, /*index=5*/f32[384,1]{1,0:T(8,128)}) custom-call(f32[384,768]{1,0:T(8,128)} %get-tuple-element.58.mid_ref, bf16[4,768,2304]{2,1,0:T(8,128)(2,1)} %bitcast.109, ...), custom_call_target="tpu_custom_call" | custom-call | tf_op jit(solution)/shard_map/ffn_fwd/pallas_call | solution.py:497
  297.4 17.5 %ffn_bwd.2 = (bf16[4,768,2304]{2,1,0:T(8,128)(2,1)}, f32[4,1,768]{2,1,0:T(1,128)}, f32[8,768]{1,0:T(8,128)}, f32[384,768]{1,0:T(8,128)}) custom-call(f32[384,768]{1,0:T(8,128)} %grad_ref.1, f32[384,768]{1,0:T(8,128)} %get-tuple-element.58.mid_ref, f32[384,768]{1,0:T(8,128)} %get-tuple-element.60.unit2_ref, f32[384,1]{1,0:T(8,128)} %get-tuple-element.61.rs2_ref, ...), custom_call_target="tpu_custom_call" | custom-call | tf_op jit(solution)/shard_map/ffn_bwd/pallas_call | solution.py:562
  314.9 27.3 %attn_bwd.2 = (bf16[4,768,2304]{2,1,0:T(8,128)(2,1)}, f32[4,1,256]{2,1,0:T(1,128)}, f32[4,1,384]{2,1,0:T(1,128)}, f32[384,768]{1,0:T(8,128)}, f32[1024,768]{1,0:T(8,128)}) custom-call(bf16[4,768,2304]{2,1,0:T(8,128)(2,1)} %get-tuple-element.66.dg_in, f32[384,768]{1,0:T(8,128)} %get-tuple-element.67.dfirst_ref, ...), custom_call_target="tpu_custom_call", output_to_operand_aliasing={{0}: (0, {})} | custom-call | tf_op jit(solution)/shard_map/attn_bwd/pallas_call | solution.py:643
  342.5 1.5 copy-done.6
  344.6 2.1 copy-done.1
  346.8 1.9 collective-permute-start.5
  348.7 2.4 collective-permute-start.4
  351.2 70.8 %scatter_grads.3 = f32[96,2304]{1,0:T(8,128)} custom-call(bf16[4,8,96,2304]{3,2,1,0:T(8,128)(2,1)} %bitcast.115), custom_call_target="tpu_custom_call" | custom-call | tf_op jit(solution)/shard_map/scatter_grads/pallas_call | solution.py:342
  422.3 1.3 reshape.106
  423.7 1.4 pad_maximum_fusion.5
  425.1 2.5 fusion.3.grad_ref
  427.5 17.6 %ffn_bwd.3 = (bf16[4,768,2304]{2,1,0:T(8,128)(2,1)}, f32[4,1,768]{2,1,0:T(1,128)}, f32[8,768]{1,0:T(8,128)}, f32[384,768]{1,0:T(8,128)}) custom-call(f32[384,768]{1,0:T(8,128)} %fusion.3.grad_ref, f32[384,768]{1,0:T(8,128)} %get-tuple-element.55.mid_ref, f32[384,768]{1,0:T(8,128)} %get-tuple-element.73.unit2_ref, f32[384,1]{1,0:T(8,128)} %get-tuple-element.74.rs2_ref, ...), custom_call_target="tpu_custom_call" | custom-call | tf_op jit(solution)/shard_map/ffn_bwd/pallas_call | solution.py:562
  445.2 26.7 %attn_bwd.3 = (bf16[4,768,2304]{2,1,0:T(8,128)(2,1)}, f32[4,1,256]{2,1,0:T(1,128)}, f32[4,1,384]{2,1,0:T(1,128)}, f32[384,768]{1,0:T(8,128)}, f32[1024,768]{1,0:T(8,128)}) custom-call(bf16[4,768,2304]{2,1,0:T(8,128)(2,1)} %get-tuple-element.79.dg_in, f32[384,768]{1,0:T(8,128)} %get-tuple-element.80.dfirst_ref, ...), custom_call_target="tpu_custom_call", output_to_operand_aliasing={{0}: (0, {})} | custom-call | tf_op jit(solution)/shard_map/attn_bwd/pallas_call | solution.py:643
  472.2 1.5 copy-done.5
  474.3 2.0 copy-done
  476.4 1.1 fusion.9
  477.5 5.6 collective-permute-start.7
  483.0 2.1 collective-permute-start.6
  485.3 70.9 %scatter_grads.2 = f32[96,2304]{1,0:T(8,128)} custom-call(bf16[4,8,96,2304]{3,2,1,0:T(8,128)(2,1)} %bitcast.114), custom_call_target="tpu_custom_call" | custom-call | tf_op jit(solution)/shard_map/scatter_grads/pallas_call | solution.py:342
  557.2 2.2 fusion.4
  559.4 0.8 maximum_bitcast_fusion
  560.3 0.9 copy.67
  561.2 0.8 copy.68
  562.0 117.4 %all-reduce.4.cloned.1.call-done = f32[2,9216]{1,0:T(2,128)} async-done(((f32[2,9216]{1,0:T(2,128)}), f32[2,9216]{1,0:T(2,128)}) %all-reduce.4.cloned.1.call-update) | async-done | bytes 73744 | tf_op jit(solution)/shard_map/psum | solution.py:758
  680.1 0.8 slice.263
  683.5 2.8 fusion.1
  (120 shorter events, 13.9 us)
Async XLA Ops:
  7.2 672.2 %all-reduce.4.cloned.1.call-start = ((), (), s32[]{:S(2)}) async-start(), calls=%async_computation | async-start | bytes 147456 | tf_op jit(solution)/shard_map/psum | solution.py:758
  7.2 148.0 %collective-permute-start = (bf16[384,768]{1,0:T(8,128)(2,1)}, bf16[384,768]{1,0:T(8,128)(2,1)S(1)}, u32[]{:S(2)}, u32[]{:S(2)}) collective-permute-start(bf16[384,768]{1,0:T(8,128)(2,1)} %own_ref.3), channel_id=1, source_target_pairs={{0,1},{1,2},{2,3},{4,5},{5,6},{6,7},{8,9},{9,10},{10,11},{12,13},{... | collective-permute-start | bytes 1769480 | tf_op jit(solution)/shard_map/ppermute | solution.py:724
  11.7 143.6 %collective-permute-start.1 = (bf16[384,768]{1,0:T(8,128)(2,1)}, bf16[384,768]{1,0:T(8,128)(2,1)S(1)}, u32[]{:S(2)}, u32[]{:S(2)}) collective-permute-start(bf16[384,768]{1,0:T(8,128)(2,1)} %own_ref.3), channel_id=1, source_target_pairs={{1,0},{2,1},{3,2},{5,4},{6,5},{7,6},{9,8},{10,9},{11,10},{13,12},{... | collective-permute-start | bytes 1769480 | tf_op jit(solution)/shard_map/ppermute | solution.py:725
  79.4 71.3 %copy-start.24 = (s32[3,4]{1,0:T(4,128)S(1)}, s32[3,4]{1,0:T(4,128)}, u32[]{:S(2)}) copy-start(s32[3,4]{1,0:T(4,128)} %param.16) | copy-start | bytes 148
  79.4 73.2 %copy-start.14 = (f32[2,768]{1,0:T(2,128)S(1)}, f32[2,768]{1,0:T(2,128)}, u32[]{:S(2)}) copy-start(f32[2,768]{1,0:T(2,128)} %param.21) | copy-start | bytes 18436
  79.4 73.2 %copy-start.15 = (f32[2,768]{1,0:T(2,128)S(1)}, f32[2,768]{1,0:T(2,128)}, u32[]{:S(2)}) copy-start(f32[2,768]{1,0:T(2,128)} %param.20) | copy-start | bytes 18436
  79.4 73.2 %copy-start.16 = (f32[2,768]{1,0:T(2,128)S(1)}, f32[2,768]{1,0:T(2,128)}, u32[]{:S(2)}) copy-start(f32[2,768]{1,0:T(2,128)} %param.26) | copy-start | bytes 18436
  79.4 73.2 %copy-start.17 = (f32[2,768]{1,0:T(2,128)S(1)}, f32[2,768]{1,0:T(2,128)}, u32[]{:S(2)}) copy-start(f32[2,768]{1,0:T(2,128)} %param.22) | copy-start | bytes 18436
  79.4 73.2 %copy-start.18 = (f32[2,768]{1,0:T(2,128)S(1)}, f32[2,768]{1,0:T(2,128)}, u32[]{:S(2)}) copy-start(f32[2,768]{1,0:T(2,128)} %param.28) | copy-start | bytes 18436
  79.4 73.2 %copy-start.19 = (f32[2,768]{1,0:T(2,128)S(1)}, f32[2,768]{1,0:T(2,128)}, u32[]{:S(2)}) copy-start(f32[2,768]{1,0:T(2,128)} %param.27) | copy-start | bytes 18436
  150.4 4.9 copy-start.4
  185.8 74.4 %collective-permute-start.2 = (bf16[384,768]{1,0:T(8,128)(2,1)}, bf16[384,768]{1,0:T(8,128)(2,1)S(1)}, u32[]{:S(2)}, u32[]{:S(2)}) collective-permute-start(bf16[384,768]{1,0:T(8,128)(2,1)} %get-tuple-element.56), channel_id=1, source_target_pairs={{0,1},{1,2},{2,3},{4,5},{5,6},{6,7},{8,9},{9,10},{10,11},{12,13},{... | collective-permute-start | bytes 1769480 | tf_op jit(solution)/shard_map/ppermute | solution.py:724
  188.8 66.8 %copy-start.10 = (bf16[384,768]{1,0:T(8,128)(2,1)S(1)}, bf16[384,768]{1,0:T(8,128)(2,1)}, u32[]{:S(2)}) copy-start(bf16[384,768]{1,0:T(8,128)(2,1)} %get-tuple-element.56) | copy-start | bytes 1769476
  255.7 11.2 %collective-permute-start.3 = (bf16[384,768]{1,0:T(8,128)(2,1)S(1)}, bf16[384,768]{1,0:T(8,128)(2,1)S(1)}, u32[]{:S(2)}, u32[]{:S(2)}) collective-permute-start(bf16[384,768]{1,0:T(8,128)(2,1)S(1)} %copy-done.10), channel_id=1, source_target_pairs={{1,0},{2,1},{3,2},{5,4},{6,5},{7,6},{9,8},{10,9},{11,10},{13,12},{... | collective-permute-start | bytes 1769480 | tf_op jit(solution)/shard_map/ppermute | solution.py:725
  342.2 1.9 copy-start.6
  344.4 2.3 copy-start.1
  346.8 78.2 %collective-permute-start.5 = (bf16[384,768]{1,0:T(8,128)(2,1)S(1)}, bf16[384,768]{1,0:T(8,128)(2,1)S(1)}, u32[]{:S(2)}, u32[]{:S(2)}) collective-permute-start(bf16[384,768]{1,0:T(8,128)(2,1)S(1)} %get-tuple-element.155), channel_id=1, source_target_pairs={{0,1},{1,2},{2,3},{4,5},{5,6},{6,7},{8,9},{9,10},{10,11},{12,13},{... | collective-permute-start | bytes 1769480 | tf_op jit(solution)/shard_map/ppermute | solution.py:732
  348.7 76.3 %collective-permute-start.4 = (bf16[384,768]{1,0:T(8,128)(2,1)S(1)}, bf16[384,768]{1,0:T(8,128)(2,1)S(1)}, u32[]{:S(2)}, u32[]{:S(2)}) collective-permute-start(bf16[384,768]{1,0:T(8,128)(2,1)S(1)} %get-tuple-element.154), channel_id=1, source_target_pairs={{1,0},{2,1},{3,2},{5,4},{6,5},{7,6},{9,8},{10,9},{11,10},{13,12},{... | collective-permute-start | bytes 1769480 | tf_op jit(solution)/shard_map/ppermute | solution.py:731
  351.2 70.9 %copy-start.22 = (f32[4,1,384]{2,1,0:T(1,128)S(1)}, f32[4,1,384]{2,1,0:T(1,128)}, u32[]{:S(2)}) copy-start(f32[4,1,384]{2,1,0:T(1,128)} %get-tuple-element.94) | copy-start | bytes 18436
  351.2 71.0 %copy-start.20 = (f32[4,1,256]{2,1,0:T(1,128)S(1)}, f32[4,1,256]{2,1,0:T(1,128)}, u32[]{:S(2)}) copy-start(f32[4,1,256]{2,1,0:T(1,128)} %get-tuple-element.93) | copy-start | bytes 12292
  351.2 73.8 %copy-start.8 = (f32[384,768]{1,0:T(8,128)S(1)}, f32[384,768]{1,0:T(8,128)}, u32[]{:S(2)}) copy-start(f32[384,768]{1,0:T(8,128)} %get-tuple-element.71) | copy-start | bytes 3538948
  471.9 1.9 copy-start.5
  474.1 2.3 copy-start
  477.5 206.1 %collective-permute-start.7 = (bf16[384,768]{1,0:T(8,128)(2,1)}, bf16[384,768]{1,0:T(8,128)(2,1)}, u32[]{:S(2)}, u32[]{:S(2)}) collective-permute-start(bf16[384,768]{1,0:T(8,128)(2,1)} %get-tuple-element.153), channel_id=1, source_target_pairs={{0,1},{1,2},{2,3},{4,5},{5,6},{6,7},{8,9},{9,10},{10,11},{12,13},{... | collective-permute-start | bytes 1769480 | tf_op jit(solution)/shard_map/ppermute | solution.py:732
  483.0 200.5 %collective-permute-start.6 = (bf16[384,768]{1,0:T(8,128)(2,1)}, bf16[384,768]{1,0:T(8,128)(2,1)}, u32[]{:S(2)}, u32[]{:S(2)}) collective-permute-start(bf16[384,768]{1,0:T(8,128)(2,1)} %get-tuple-element.152), channel_id=1, source_target_pairs={{1,0},{2,1},{3,2},{5,4},{6,5},{7,6},{9,8},{10,9},{11,10},{13,12},{... | collective-permute-start | bytes 1769480 | tf_op jit(solution)/shard_map/ppermute | solution.py:731
  485.2 71.0 %copy-start.23 = (f32[4,1,384]{2,1,0:T(1,128)S(1)}, f32[4,1,384]{2,1,0:T(1,128)}, u32[]{:S(2)}) copy-start(f32[4,1,384]{2,1,0:T(1,128)} %get-tuple-element.90) | copy-start | bytes 18436
  485.2 71.2 %copy-start.21 = (f32[4,1,256]{2,1,0:T(1,128)S(1)}, f32[4,1,256]{2,1,0:T(1,128)}, u32[]{:S(2)}) copy-start(f32[4,1,256]{2,1,0:T(1,128)} %get-tuple-element.89) | copy-start | bytes 12292
  485.2 71.3 %copy-start.12 = (f32[8,768]{1,0:T(8,128)S(1)}, f32[8,768]{1,0:T(8,128)}, u32[]{:S(2)}) copy-start(f32[8,768]{1,0:T(8,128)} %get-tuple-element.88) | copy-start | bytes 73732
  485.2 71.3 %copy-start.13 = (f32[4,1,768]{2,1,0:T(1,128)S(1)}, f32[4,1,768]{2,1,0:T(1,128)}, u32[]{:S(2)}) copy-start(f32[4,1,768]{2,1,0:T(1,128)} %get-tuple-element.91) | copy-start | bytes 36868
  485.2 71.3 %copy-start.11 = (f32[9216]{0:T(1024)S(1)}, f32[9216]{0:T(1024)}, u32[]{:S(2)}) copy-start(f32[9216]{0:T(1024)} %pad_maximum_fusion.5) | copy-start | bytes 110596
  485.2 72.0 %copy-start.2 = (f32[96,2304]{1,0:T(8,128)S(1)}, f32[96,2304]{1,0:T(8,128)}, u32[]{:S(2)}) copy-start(f32[96,2304]{1,0:T(8,128)} %scatter_grads.3) | copy-start | bytes 2654212
  556.2 3.2 copy-start.3
  559.4 124.1 %copy-start.7 = (f32[384,768]{1,0:T(8,128)S(1)}, f32[384,768]{1,0:T(8,128)}, u32[]{:S(2)}) copy-start(f32[384,768]{1,0:T(8,128)} %get-tuple-element.84) | copy-start | bytes 3538948
  560.2 0.9 copy-start.9
Sparse Core Ops, SparseCore 0:
  560.4 118.9 all-reduce.3

commit v2 on v1

--- a/solution.py
+++ b/solution.py
@@ -69,11 +69,91 @@
     pl.semaphore_wait(barrier, len(devices))
 
 
-def gather_kernel(n_dp, own_ref, out_ref, own_sem, send_sem, recv_sem):
+def bits(n):
+    return n.bit_length() - 1
+
+
+def pairs(me, n_dp, n_tensor):
+    found = [(me.dp, me.tensor ^ (1 << b)) for b in range(bits(n_tensor))]
+    return found + [(me.dp ^ (1 << b), me.tensor) for b in range(bits(n_dp))]
+
+
+def doubling_gather(me, n_dp, n_tensor, own_ref, all_ref, own_sem, send_sem, recv_sem):
+    held = []
+    for b in range(bits(n_tensor)):
+        size = 1 << b
+        held.append(all_ref.at[pl.ds(me.tensor // size * size, size), me.dp])
+    for b in range(bits(n_dp)):
+        size = 1 << b
+        held.append(all_ref.at[:, pl.ds(me.dp // size * size, size)])
+    copies = [
+        pltpu.make_async_remote_copy(
+            src_ref=block, dst_ref=block, send_sem=send_sem.at[i], recv_sem=recv_sem.at[i],
+            device_id=device, device_id_type=MESH,
+        )
+        for i, (block, device) in enumerate(zip(held, pairs(me, n_dp, n_tensor)))
+    ]
+    mine = pltpu.make_async_copy(own_ref, all_ref.at[me.tensor, me.dp], own_sem)
+
+    def begin():
+        mine.start()
+        mine.wait()
+        copies[0].start()
+
+    def middle(i):
+        copies[i].wait_recv()
+        if i + 1 < len(copies):
+            copies[i + 1].start()
+
+    def end():
+        for copy in copies:
+            copy.wait_send()
+
+    return [begin] + [functools.partial(middle, i) for i in range(len(copies))] + [end]
+
+
+def doubling_sum(me, n_dp, n_tensor, own_ref, total_ref, part_ref, come_ref, send_sem, recv_sem):
+    devices = pairs(me, n_dp, n_tensor)
+    copies = [
+        pltpu.make_async_remote_copy(
+            src_ref=part_ref.at[i], dst_ref=come_ref.at[i], send_sem=send_sem.at[i], recv_sem=recv_sem.at[i],
+            device_id=device, device_id_type=MESH,
+        )
+        for i, device in enumerate(devices)
+    ]
+
+    def begin():
+        part_ref[0] = own_ref[...]
+        copies[0].start()
+
+    def middle(i):
+        copies[i].wait_recv()
+        total = part_ref[i] + come_ref[i]
+        if i + 1 < len(copies):
+            part_ref[i + 1] = total
+            copies[i + 1].start()
+        else:
+            total_ref[...] = total
+
+    def end():
+        for copy in copies:
+            copy.wait_send()
+
+    return [begin] + [functools.partial(middle, i) for i in range(len(copies))] + [end]
+
+
+def gather_kernel(n_dp, n_tensor, small, *refs):
+    if small:
+        own_ref, few_ref, out_ref, few_out_ref, own_sem, send_sem, recv_sem, few_sem, few_send, few_recv = refs
+    else:
+        own_ref, out_ref, own_sem, send_sem, recv_sem = refs
     me = Place(n_dp)
     nz = me.nz
     half = own_ref.shape[1] // 2
     barrier = pltpu.get_barrier_semaphore()
+    far = [(me.dp ^ (2 << b), me.tensor) for b in range(1, bits(nz))] if small else []
+    for device in far:
+        pl.semaphore_signal(barrier, inc=1, device_id=device, device_id_type=MESH)
     for device in (me.to_x, me.to_y, me.to_c):
         pl.semaphore_signal(barrier, inc=1, device_id=device, device_id_type=MESH)
 
@@ -85,7 +165,8 @@
     def _():
         pl.semaphore_signal(barrier, inc=1, device_id=(me.dp + 2, me.tensor), device_id_type=MESH)
 
-    pl.semaphore_wait(barrier, 3 + (me.z > 0).astype(jnp.int32) + (me.z < nz - 1).astype(jnp.int32))
+    pl.semaphore_wait(barrier, 3 + len(far) + (me.z > 0).astype(jnp.int32) + (me.z < nz - 1).astype(jnp.int32))
+    rounds = doubling_gather(me, n_dp, n_tensor, few_ref, few_out_ref, few_sem, few_send, few_recv) if small else []
 
     def piece(t, d, part):
         if part is None:
@@ -180,6 +261,8 @@
     true = me.z >= 0
     own_round()
     for s in range(1, nz + 2):
+        if rounds:
+            rounds.pop(0)()
         if s < nz:
             z_round(me.z - s, True, me.z - s >= 0)
             z_round(me.z + s, False, me.z + s < nz)
@@ -194,6 +277,9 @@
             diagonal_round(me.z - s + 2, me.z - s + 2 >= 0)
             diagonal_round(me.z + s - 2, me.z + s - 2 < nz)
 
+    for turn in rounds:
+        turn()
+
     for p in range(nz):
         for kind in range(5):
             t = me.t_c if kind in (0, 2) else me.t_xc
@@ -218,28 +304,36 @@
             core_copy(kind, p).wait_send()
 
 
-def gather_weights(own, n_dp, n_tensor, collective_id):
+def gather_weights(own, few, n_dp, n_tensor, collective_id):
     rows, cols = own.shape
     slots = 11 * (n_dp // 2)
+    small = few is not None
+    rounds = bits(n_dp) + bits(n_tensor)
+    hbm = pl.BlockSpec(memory_space=pltpu.MemorySpace.HBM)
+    vmem = pl.BlockSpec(memory_space=pltpu.MemorySpace.VMEM)
+    out_shape = [jax.ShapeDtypeStruct((n_tensor, n_dp, rows, cols), own.dtype)]
+    scratch = [pltpu.SemaphoreType.DMA, pltpu.SemaphoreType.DMA((slots,)), pltpu.SemaphoreType.DMA((slots,))]
+    if small:
+        out_shape.append(jax.ShapeDtypeStruct((n_tensor, n_dp) + few.shape, few.dtype))
+        scratch += [pltpu.SemaphoreType.DMA, pltpu.SemaphoreType.DMA((rounds,)), pltpu.SemaphoreType.DMA((rounds,))]
     out = pl.pallas_call(
-        functools.partial(gather_kernel, n_dp),
-        out_shape=jax.ShapeDtypeStruct((n_tensor, n_dp, rows, cols), own.dtype),
-        in_specs=[pl.BlockSpec(memory_space=pltpu.MemorySpace.HBM)],
-        out_specs=pl.BlockSpec(memory_space=pltpu.MemorySpace.HBM),
-        scratch_shapes=[
-            pltpu.SemaphoreType.DMA,
-            pltpu.SemaphoreType.DMA((slots,)),
-            pltpu.SemaphoreType.DMA((slots,)),
-        ],
+        functools.partial(gather_kernel, n_dp, n_tensor, small),
+        out_shape=out_shape,
+        in_specs=[hbm, vmem] if small else [hbm],
+        out_specs=[hbm, vmem] if small else [hbm],
+        scratch_shapes=scratch,
         compiler_params=pltpu.CompilerParams(collective_id=collective_id, has_side_effects=True),
         name="gather_weights",
-    )(own)
-    return out.reshape(n_tensor, n_dp * rows, cols)
-
-
-def scatter_kernel(
-    n_dp, g_ref, out_ref, mine, core_in, first_in, second_in, x_in, y_in, z_in, load_sem, send_sem, recv_sem
-):
+    )(*([own, few] if small else [own]))
+    return (out[0].reshape(n_tensor, n_dp * rows, cols),) + tuple(out[1:])
+
+
+def scatter_kernel(n_dp, n_tensor, small, *refs):
+    if small:
+        g_ref, few_ref, out_ref, few_out_ref, *refs, few_part, few_come, few_send, few_recv = refs
+    else:
+        g_ref, out_ref, *refs = refs
+    mine, core_in, first_in, second_in, x_in, y_in, z_in, load_sem, send_sem, recv_sem = refs
     me = Place(n_dp)
     nz = me.nz
     cols = g_ref.shape[-1]
@@ -272,6 +366,9 @@
         for place in range(4):
             to_core(place, k).start()
             load(place, k).start()
+    rounds = []
+    if small:
+        rounds = doubling_sum(me, n_dp, n_tensor, few_ref, few_out_ref, few_part, few_come, few_send, few_recv)
 
     def first(k):
         return remote(mine.at[0, k, :, pl.ds(0, half)], first_in.at[k], 4 * nz + k, me.to_x)
@@ -294,6 +391,8 @@
         return mine[place, k].astype(F32) + core_in[place, k].astype(F32)
 
     for step in range(nz + 2):
+        if rounds:
+            rounds.pop(0)()
         if step < nz:
             k = step
             mine[0, k] = both(0, k).astype(BF)
@@ -326,6 +425,8 @@
                     along_z(j).wait_recv()
                     total += z_in[j].astype(F32)
                 out_ref[...] = total
+    for turn in rounds:
+        turn()
     for k in range(nz):
         for place in range(4):
             to_core(place, k).wait_send()
@@ -335,30 +436,44 @@
             along_z(k).wait_send()
 
 
-def scatter_grads(grads, n_dp, n_tensor, collective_id):
+def scatter_grads(grads, few, n_dp, n_tensor, collective_id):
     cols = grads.shape[-1]
     rows = grads.shape[1] // n_dp
     nz = n_dp // 2
+    small = few is not None
+    rounds = bits(n_dp) + bits(n_tensor)
+    hbm = pl.BlockSpec(memory_space=pltpu.MemorySpace.HBM)
+    vmem = pl.BlockSpec(memory_space=pltpu.MemorySpace.VMEM)
+    out_shape = [jax.ShapeDtypeStruct((rows, cols), F32)]
+    scratch = [
+        pltpu.VMEM((4, nz, rows, cols), BF),
+        pltpu.VMEM((4, nz, rows, cols), BF),
+        pltpu.VMEM((nz, rows, cols // 2), BF),
+        pltpu.VMEM((nz, rows, cols // 2), BF),
+        pltpu.VMEM((nz, rows, cols), BF),
+        pltpu.VMEM((nz, rows, cols), BF),
+        pltpu.VMEM((nz - 1, rows, cols), BF),
+        pltpu.SemaphoreType.DMA((4 * nz,)),
+        pltpu.SemaphoreType.DMA((9 * nz,)),
+        pltpu.SemaphoreType.DMA((9 * nz,)),
+    ]
+    operands = [grads.reshape(n_tensor, n_dp, rows, cols)]
+    if small:
+        out_shape.append(jax.ShapeDtypeStruct(few.shape, F32))
+        operands.append(few)
+        scratch += [
+            pltpu.VMEM((rounds,) + few.shape, F32), pltpu.VMEM((rounds,) + few.shape, F32),
+            pltpu.SemaphoreType.DMA((rounds,)), pltpu.SemaphoreType.DMA((rounds,)),
+        ]
     return pl.pallas_call(
-        functools.partial(scatter_kernel, n_dp),
-        out_shape=jax.ShapeDtypeStruct((rows, cols), F32),
-        in_specs=[pl.BlockSpec(memory_space=pltpu.MemorySpace.HBM)],
-        out_specs=pl.BlockSpec(memory_space=pltpu.MemorySpace.VMEM),
-        scratch_shapes=[
-            pltpu.VMEM((4, nz, rows, cols), BF),
-            pltpu.VMEM((4, nz, rows, cols), BF),
-            pltpu.VMEM((nz, rows, cols // 2), BF),
-            pltpu.VMEM((nz, rows, cols // 2), BF),
-            pltpu.VMEM((nz, rows, cols), BF),
-            pltpu.VMEM((nz, rows, cols), BF),
-            pltpu.VMEM((nz - 1, rows, cols), BF),
-            pltpu.SemaphoreType.DMA((4 * nz,)),
-            pltpu.SemaphoreType.DMA((9 * nz,)),
-            pltpu.SemaphoreType.DMA((9 * nz,)),
-        ],
+        functools.partial(scatter_kernel, n_dp, n_tensor, small),
+        out_shape=out_shape,
+        in_specs=[hbm, vmem] if small else [hbm],
+        out_specs=[vmem, vmem] if small else [vmem],
+        scratch_shapes=scratch,
         compiler_params=params(collective_id=collective_id, has_side_effects=True),
         name="scatter_grads",
-    )(grads.reshape(n_tensor, n_dp, rows, cols))
+    )(*operands)
 
 
 def window_slots(tokens, rows):
@@ -684,15 +799,18 @@
         )
         for l in range(layers)
     ]
-    small = jnp.concatenate([qv_bias.reshape(layers, -1), up_bias], axis=1)
-    small = lax.all_gather(small, ("tensor", "dp"), axis=0).astype(F32)
-    small = small.reshape(n_tensor, n_dp, layers, -1)
-    piece = qv_bias.shape[2]
-    qv = small[..., : 2 * piece].reshape(n_tensor, n_dp, layers, 2, piece).transpose(2, 3, 0, 1, 4)
-    qv = qv.reshape(layers, 2, n_tensor, 1, units)
-    q_bias = jnp.pad(qv[:, 0], ((0, 0), (0, 0), (0, 0), (0, 256 - units)))
-    kv_bias = jnp.pad(qv[:, 1], ((0, 0), (0, 0), (0, 0), (units, 0)))
-    u_bias = small[..., 2 * piece :].transpose(2, 0, 1, 3).reshape(layers, n_tensor, 1, hidden_units)
+    def biases(small):
+        small = small.reshape(n_tensor, n_dp, -1)[..., : layers * each].reshape(n_tensor, n_dp, layers, each)
+        qv = small[..., : 2 * piece].reshape(n_tensor, n_dp, layers, 2, piece).transpose(2, 3, 0, 1, 4)
+        qv = qv.reshape(layers, 2, n_tensor, 1, units)
+        q_bias = jnp.pad(qv[:, 0], ((0, 0), (0, 0), (0, 0), (0, 256 - units)))
+        kv_bias = jnp.pad(qv[:, 1], ((0, 0), (0, 0), (0, 0), (units, 0)))
+        return q_bias, kv_bias, small[..., 2 * piece :].transpose(2, 0, 1, 3).reshape(layers, n_tensor, 1, hidden_units)
+
+    piece, wide = qv_bias.shape[2], up_bias.shape[1]
+    each = 2 * piece + wide
+    few = jnp.concatenate([qv_bias.reshape(layers, -1), up_bias], axis=1).astype(F32).reshape(-1)
+    few = jnp.pad(few, (0, -few.shape[0] % 1024)).reshape(-1, 128)
 
     zero = jnp.zeros((1, dim), F32)
     vecs = [
@@ -735,7 +853,11 @@
     own, win = block_input, window(block_input)
     kept = []
     for l in range(layers):
-        g = gather_weights(packs[l], n_dp, n_tensor, 0)
+        if l == 0:
+            g, small = gather_weights(packs[l], few, n_dp, n_tensor, 0)
+            q_bias, kv_bias, u_bias = biases(small)
+        else:
+            (g,) = gather_weights(packs[l], None, n_dp, n_tensor, 2)
         q, kv, ctx, mid, unit1, rs1 = attn_fwd(win, own, g, q_bias[l], kv_bias[l], qcol, kseg, vecs[l], rows)
         act, slope, out, low, unit2, rs2 = ffn_fwd(mid, g, u_bias[l], vecs[l])
         kept.append((own, win, g, q, kv, ctx, mid, unit1, rs1, act, slope, unit2, rs2))
@@ -751,16 +873,20 @@
         dg, ub, dvec, dfirst = ffn_bwd(grad, mid, unit2, rs2, unit1, rs1, g, act, slope, vecs[l])
         dg, qb, vb, own_grad, win_grad = attn_bwd(dg, dfirst, own, win, g, q, kv, ctx, qrow, kcol, rows)
         grad = window_back(own_grad, win_grad)
-        pieces[l] = scatter_grads(dg, n_dp, n_tensor, 1)
         smalls[l] = jnp.concatenate(
             [dvec[:6].reshape(-1), qb[:, 0, :units].reshape(-1), vb[:, 0, units:].reshape(-1), ub.reshape(-1)]
         )
-    totals = lax.psum(jnp.stack(smalls), ("dp", "tensor"))
+        if l == 0:
+            few = jnp.stack(smalls)
+            size = few.shape
+            pieces[l], totals = scatter_grads(dg, few.reshape(-1, 128), n_dp, n_tensor, 1)
+            totals = totals.reshape(size)
+        else:
+            (pieces[l],) = scatter_grads(dg, None, n_dp, n_tensor, 3)
     vec_totals = totals[:, : 6 * dim].reshape(layers, 6, dim)
     qv_totals = totals[:, 6 * dim : 6 * dim + 2 * n_tensor * units].reshape(layers, 2, n_tensor * units)
     u_totals = totals[:, 6 * dim + 2 * n_tensor * units :]
     qv_grad = lax.dynamic_slice(qv_totals, (0, 0, (t * n_dp + dp) * piece), (layers, 2, piece))
-    wide = up_bias.shape[1]
     u_grad = lax.dynamic_slice(u_totals, (0, (t * n_dp + dp) * wide), (layers, wide))
 
     both = jnp.stack(pieces)

time: 701 us -> 521 us (0.74)
  waiting for transfers between devices: 124 us -> 11.4 us
  blocking collectives: 59.3 us -> 0 us
  between operations: 15 us -> 1.64 us
    psum x1 -> x0, waiting for transfers between devices: 117 us -> none  [body(): totals = lax.psum(jnp.stack(smalls), ('dp', 'tensor'))]
    all_gather x1 -> x0, blocking collectives: 59.3 us -> none  [body(): small = lax.all_gather(small, ('tensor', 'dp'), axis=0).astype(F32)]
  transfers between devices with their start and end apart: 9 -> 8, of which waited for: 2 -> 2; matrix products, arithmetic and copies ran while one was open for 4% -> 5% of each run, Pallas kernels for 40% -> 40%
where the time goes in v2:
time: 521 us; the launch traced here: 514 us
  Pallas kernels  433 us (83%)
  local copies, waits for them, and re-layouts  35 us (7%)
  starting transfers between devices  21 us (4%)
  other arithmetic  11.5 us (2%)
  waiting for transfers between devices  11.4 us (2%)
    pallas_call x2, Pallas kernels, scatter_grads(): pl.pallas_call(functools.partial(scatter_kernel, n_dp, n_tensor, small),...  150 us
    pallas_call x2, Pallas kernels, gather_weights(): pl.pallas_call(functools.partial(gather_kernel, n_dp, n_tensor, small), o...  136 us
    pallas_call x2, Pallas kernels, attn_bwd(): pl.pallas_call(functools.partial(attn_bwd_kernel, rows), grid=(n,), in_sp...  54.2 us
    pallas_call x2, Pallas kernels, ffn_bwd(): pl.pallas_call(ffn_bwd_kernel, grid=(n,), in_specs=[full, full, full, who...  35.1 us
    pallas_call x2, Pallas kernels, attn_fwd(): pl.pallas_call(functools.partial(attn_fwd_kernel, rows), grid=(n,), in_sp...  34.4 us
    pallas_call x2, Pallas kernels, ffn_fwd(): pl.pallas_call(ffn_fwd_kernel, grid=(n,), in_specs=[whole(mid.shape), per...  24 us
    unnamed x60, local copies, waits for them, and re-layouts  10.5 us
  transfers between devices with their start and end apart: 8, of which 2 were waited for; matrix products, arithmetic and copies ran while one was open for 5% of the time, Pallas kernels for 40%

profile of v2, /device:TPU:1, one launch (start us, length us, event | category | flops | bytes accessed | tf_op | source)
XLA Modules:
  0.0 513.7 jit_solution(11709350529419292838)
XLA Ops:
  0.7 4.6 collective-permute-start
  5.4 1.9 collective-permute-start.1
  7.3 1.0 slice_bitcast_fusion.1
  8.3 1.0 slice_bitcast_fusion
  9.3 1.0 slice_bitcast_fusion.4
  10.3 0.8 fusion.11
  11.3 0.8 reshape.107
  13.5 0.9 concatenate.28.refs_0_
  14.3 71.2 %gather_weights.2 = (bf16[4,8,96,2304]{3,2,1,0:T(8,128)(2,1)}, f32[4,8,8,128]{3,2,1,0:T(8,128)}) custom-call(bf16[96,2304]{1,0:T(8,128)(2,1)} %concatenate.28.refs_0_, f32[8,128]{1,0:T(8,128)} %bitcast_convert_fusion.refs_1_), custom_call_target="tpu_custom_call" | custom-call | tf_op jit(solution)/shard_map/gather_weights/pallas_call | solution.py:319
  85.6 0.9 reshape.111
  87.4 0.8 reshape.131.qseg_ref
  91.8 1.3 constant_dynamic-slice_fusion.3.win_ref
  93.1 17.1 %attn_fwd.2 = (bf16[4,384,256]{2,1,0:T(8,128)(2,1)}, bf16[4,1024,384]{2,1,0:T(8,128)(2,1)}, bf16[4,384,256]{2,1,0:T(8,128)(2,1)}, f32[384,768]{1,0:T(8,128)}, f32[384,768]{1,0:T(8,128)}, /*index=5*/f32[384,1]{1,0:T(8,128)}) custom-call(bf16[1024,768]{1,0:T(8,128)(2,1)} %constant_dynamic-slice_fusion.3.win_ref, bf16[384,768]{1,0:T(8,128)(2,1)} %own_ref.3, ...), custom_call_target="tpu_custom_call" | custom-call | tf_op jit(solution)/shard_map/attn_fwd/pallas_call | solution.py:562
  110.2 12.0 %ffn_fwd.2 = (bf16[4,384,768]{2,1,0:T(8,128)(2,1)}, bf16[4,384,768]{2,1,0:T(8,128)(2,1)}, f32[384,768]{1,0:T(8,128)}, bf16[384,768]{1,0:T(8,128)(2,1)}, f32[384,768]{1,0:T(8,128)}, /*index=5*/f32[384,1]{1,0:T(8,128)}) custom-call(f32[384,768]{1,0:T(8,128)} %get-tuple-element.61.mid_ref, bf16[4,768,2304]{2,1,0:T(8,128)(2,1)} %bitcast.103, ...), custom_call_target="tpu_custom_call" | custom-call | tf_op jit(solution)/shard_map/ffn_fwd/pallas_call | solution.py:612
  122.2 2.6 collective-permute-start.2
  125.0 0.9 concatenate.32.refs_0_
  125.8 64.7 %gather_weights.3 = bf16[4,8,96,2304]{3,2,1,0:T(8,128)(2,1)} custom-call(bf16[96,2304]{1,0:T(8,128)(2,1)} %concatenate.32.refs_0_), custom_call_target="tpu_custom_call" | custom-call | tf_op jit(solution)/shard_map/gather_weights/pallas_call | solution.py:319
  191.2 2.2 collective-permute-start.3
  193.4 1.0 copy.57
  195.9 7.6 %collective-permute-done.3 = bf16[384,768]{1,0:T(8,128)(2,1)S(1)} collective-permute-done((bf16[384,768]{1,0:T(8,128)(2,1)S(1)}, bf16[384,768]{1,0:T(8,128)(2,1)S(1)}, u32[]{:S(2)}, u32[]{:S(2)}) %collective-permute-start.3) | collective-permute-done | bytes 589856 | tf_op jit(solution)/shard_map/ppermute | solution.py:843
  203.5 1.2 constant_dynamic-slice_fusion.2.win_ref
  204.8 17.2 %attn_fwd.3 = (bf16[4,384,256]{2,1,0:T(8,128)(2,1)}, bf16[4,1024,384]{2,1,0:T(8,128)(2,1)}, bf16[4,384,256]{2,1,0:T(8,128)(2,1)}, f32[384,768]{1,0:T(8,128)}, f32[384,768]{1,0:T(8,128)}, /*index=5*/f32[384,1]{1,0:T(8,128)}) custom-call(bf16[1024,768]{1,0:T(8,128)(2,1)} %constant_dynamic-slice_fusion.2.win_ref, f32[384,768]{1,0:T(8,128)} %get-tuple-element.63.own_ref, ...), custom_call_target="tpu_custom_call" | custom-call | tf_op jit(solution)/shard_map/attn_fwd/pallas_call | solution.py:562
  222.0 12.0 %ffn_fwd.3 = (bf16[4,384,768]{2,1,0:T(8,128)(2,1)}, bf16[4,384,768]{2,1,0:T(8,128)(2,1)}, f32[384,768]{1,0:T(8,128)}, bf16[384,768]{1,0:T(8,128)(2,1)}, f32[384,768]{1,0:T(8,128)}, /*index=5*/f32[384,1]{1,0:T(8,128)}) custom-call(f32[384,768]{1,0:T(8,128)} %get-tuple-element.64.mid_ref, bf16[4,768,2304]{2,1,0:T(8,128)(2,1)} %bitcast.97, ...), custom_call_target="tpu_custom_call" | custom-call | tf_op jit(solution)/shard_map/ffn_fwd/pallas_call | solution.py:612
  234.0 17.5 %ffn_bwd.2 = (bf16[4,768,2304]{2,1,0:T(8,128)(2,1)}, f32[4,1,768]{2,1,0:T(1,128)}, f32[8,768]{1,0:T(8,128)}, f32[384,768]{1,0:T(8,128)}) custom-call(f32[384,768]{1,0:T(8,128)} %grad_ref.1, f32[384,768]{1,0:T(8,128)} %get-tuple-element.64.mid_ref, f32[384,768]{1,0:T(8,128)} %get-tuple-element.66.unit2_ref, f32[384,1]{1,0:T(8,128)} %get-tuple-element.67.rs2_ref, ...), custom_call_target="tpu_custom_call" | custom-call | tf_op jit(solution)/shard_map/ffn_bwd/pallas_call | solution.py:677
  251.5 27.3 %attn_bwd.2 = (bf16[4,768,2304]{2,1,0:T(8,128)(2,1)}, f32[4,1,256]{2,1,0:T(1,128)}, f32[4,1,384]{2,1,0:T(1,128)}, f32[384,768]{1,0:T(8,128)}, f32[1024,768]{1,0:T(8,128)}) custom-call(bf16[4,768,2304]{2,1,0:T(8,128)(2,1)} %get-tuple-element.72.dg_in, f32[384,768]{1,0:T(8,128)} %get-tuple-element.73.dfirst_ref, ...), custom_call_target="tpu_custom_call", output_to_operand_aliasing={{0}: (0, {})} | custom-call | tf_op jit(solution)/shard_map/attn_bwd/pallas_call | solution.py:758
  279.1 1.5 copy-done.6
  281.3 2.1 copy-done.1
  283.4 1.9 collective-permute-start.5
  285.4 2.4 collective-permute-start.4
  287.8 71.0 %scatter_grads.3 = f32[96,2304]{1,0:T(8,128)} custom-call(bf16[4,8,96,2304]{3,2,1,0:T(8,128)(2,1)} %bitcast.109), custom_call_target="tpu_custom_call" | custom-call | tf_op jit(solution)/shard_map/scatter_grads/pallas_call | solution.py:468
  359.1 1.3 reshape.122
  360.5 1.4 pad_maximum_fusion.5
  361.9 2.5 fusion.3.grad_ref
  364.4 17.6 %ffn_bwd.3 = (bf16[4,768,2304]{2,1,0:T(8,128)(2,1)}, f32[4,1,768]{2,1,0:T(1,128)}, f32[8,768]{1,0:T(8,128)}, f32[384,768]{1,0:T(8,128)}) custom-call(f32[384,768]{1,0:T(8,128)} %fusion.3.grad_ref, f32[384,768]{1,0:T(8,128)} %get-tuple-element.61.mid_ref, f32[384,768]{1,0:T(8,128)} %get-tuple-element.79.unit2_ref, f32[384,1]{1,0:T(8,128)} %get-tuple-element.80.rs2_ref, ...), custom_call_target="tpu_custom_call" | custom-call | tf_op jit(solution)/shard_map/ffn_bwd/pallas_call | solution.py:677
  382.0 26.9 %attn_bwd.3 = (bf16[4,768,2304]{2,1,0:T(8,128)(2,1)}, f32[4,1,256]{2,1,0:T(1,128)}, f32[4,1,384]{2,1,0:T(1,128)}, f32[384,768]{1,0:T(8,128)}, f32[1024,768]{1,0:T(8,128)}) custom-call(bf16[4,768,2304]{2,1,0:T(8,128)(2,1)} %get-tuple-element.85.dg_in, f32[384,768]{1,0:T(8,128)} %get-tuple-element.86.dfirst_ref, ...), custom_call_target="tpu_custom_call", output_to_operand_aliasing={{0}: (0, {})} | custom-call | tf_op jit(solution)/shard_map/attn_bwd/pallas_call | solution.py:758
  408.9 0.8 slice_reduce_fusion.4
  411.4 78.5 %scatter_grads.2 = (f32[96,2304]{1,0:T(8,128)}, f32[144,128]{1,0:T(8,128)}) custom-call(bf16[4,8,96,2304]{3,2,1,0:T(8,128)(2,1)} %bitcast.108, f32[144,128]{1,0:T(8,128)} %reshape.124.refs_1_), custom_call_target="tpu_custom_call" | custom-call | tf_op jit(solution)/shard_map/scatter_grads/pallas_call | solution.py:468
  489.9 0.9 reshape.126
  491.5 1.3 copy-done.5
  493.4 2.0 copy-done
  495.4 1.1 fusion.9
  496.5 2.6 collective-permute-start.7
  499.1 2.7 collective-permute-start.6
  502.1 0.9 copy.52
  503.0 0.8 copy.53
  505.1 1.1 fusion.4
  506.8 3.8 collective-permute-done.6
  510.6 2.8 fusion.1
  (120 shorter events, 14.4 us)
Async XLA Ops:
  0.6 86.4 %copy-start.22 = (s32[3,4]{1,0:T(4,128)S(1)}, s32[3,4]{1,0:T(4,128)}, u32[]{:S(2)}) copy-start(s32[3,4]{1,0:T(4,128)} %param.16) | copy-start | bytes 148
  0.7 88.3 %copy-start.14 = (f32[2,768]{1,0:T(2,128)S(1)}, f32[2,768]{1,0:T(2,128)}, u32[]{:S(2)}) copy-start(f32[2,768]{1,0:T(2,128)} %param.21) | copy-start | bytes 18436
  0.7 88.3 %copy-start.15 = (f32[2,768]{1,0:T(2,128)S(1)}, f32[2,768]{1,0:T(2,128)}, u32[]{:S(2)}) copy-start(f32[2,768]{1,0:T(2,128)} %param.20) | copy-start | bytes 18436
  0.7 88.3 %copy-start.16 = (f32[2,768]{1,0:T(2,128)S(1)}, f32[2,768]{1,0:T(2,128)}, u32[]{:S(2)}) copy-start(f32[2,768]{1,0:T(2,128)} %param.26) | copy-start | bytes 18436
  0.7 88.3 %copy-start.17 = (f32[2,768]{1,0:T(2,128)S(1)}, f32[2,768]{1,0:T(2,128)}, u32[]{:S(2)}) copy-start(f32[2,768]{1,0:T(2,128)} %param.22) | copy-start | bytes 18436
  0.7 88.3 %copy-start.18 = (f32[2,768]{1,0:T(2,128)S(1)}, f32[2,768]{1,0:T(2,128)}, u32[]{:S(2)}) copy-start(f32[2,768]{1,0:T(2,128)} %param.28) | copy-start | bytes 18436
  0.7 88.3 %copy-start.19 = (f32[2,768]{1,0:T(2,128)S(1)}, f32[2,768]{1,0:T(2,128)}, u32[]{:S(2)}) copy-start(f32[2,768]{1,0:T(2,128)} %param.27) | copy-start | bytes 18436
  0.7 90.9 %collective-permute-start = (bf16[384,768]{1,0:T(8,128)(2,1)}, bf16[384,768]{1,0:T(8,128)(2,1)S(1)}, u32[]{:S(2)}, u32[]{:S(2)}) collective-permute-start(bf16[384,768]{1,0:T(8,128)(2,1)} %own_ref.3), channel_id=1, source_target_pairs={{0,1},{1,2},{2,3},{4,5},{5,6},{6,7},{8,9},{9,10},{10,11},{12,13},{... | collective-permute-start | bytes 1769480 | tf_op jit(solution)/shard_map/ppermute | solution.py:842
  5.4 86.4 %collective-permute-start.1 = (bf16[384,768]{1,0:T(8,128)(2,1)}, bf16[384,768]{1,0:T(8,128)(2,1)S(1)}, u32[]{:S(2)}, u32[]{:S(2)}) collective-permute-start(bf16[384,768]{1,0:T(8,128)(2,1)} %own_ref.3), channel_id=1, source_target_pairs={{1,0},{2,1},{3,2},{5,4},{6,5},{7,6},{9,8},{10,9},{11,10},{13,12},{... | collective-permute-start | bytes 1769480 | tf_op jit(solution)/shard_map/ppermute | solution.py:843
  9.3 82.4 %copy-start.3 = (bf16[384,768]{1,0:T(8,128)(2,1)S(1)}, bf16[384,768]{1,0:T(8,128)(2,1)}, u32[]{:S(2)}) copy-start(bf16[384,768]{1,0:T(8,128)(2,1)} %own_ref.3) | copy-start | bytes 1769476
  122.2 73.5 %collective-permute-start.2 = (bf16[384,768]{1,0:T(8,128)(2,1)}, bf16[384,768]{1,0:T(8,128)(2,1)S(1)}, u32[]{:S(2)}, u32[]{:S(2)}) collective-permute-start(bf16[384,768]{1,0:T(8,128)(2,1)} %get-tuple-element.62), channel_id=1, source_target_pairs={{0,1},{1,2},{2,3},{4,5},{5,6},{6,7},{8,9},{9,10},{10,11},{12,13},{... | collective-permute-start | bytes 1769480 | tf_op jit(solution)/shard_map/ppermute | solution.py:842
  125.8 65.3 %copy-start.9 = (bf16[384,768]{1,0:T(8,128)(2,1)S(1)}, bf16[384,768]{1,0:T(8,128)(2,1)}, u32[]{:S(2)}) copy-start(bf16[384,768]{1,0:T(8,128)(2,1)} %get-tuple-element.62) | copy-start | bytes 1769476
  191.2 12.3 %collective-permute-start.3 = (bf16[384,768]{1,0:T(8,128)(2,1)S(1)}, bf16[384,768]{1,0:T(8,128)(2,1)S(1)}, u32[]{:S(2)}, u32[]{:S(2)}) collective-permute-start(bf16[384,768]{1,0:T(8,128)(2,1)S(1)} %copy-done.9), channel_id=1, source_target_pairs={{1,0},{2,1},{3,2},{5,4},{6,5},{7,6},{9,8},{10,9},{11,10},{13,12},{... | collective-permute-start | bytes 1769480 | tf_op jit(solution)/shard_map/ppermute | solution.py:843
  278.8 1.9 copy-start.6
  281.0 2.3 copy-start.1
  283.4 78.4 %collective-permute-start.5 = (bf16[384,768]{1,0:T(8,128)(2,1)S(1)}, bf16[384,768]{1,0:T(8,128)(2,1)S(1)}, u32[]{:S(2)}, u32[]{:S(2)}) collective-permute-start(bf16[384,768]{1,0:T(8,128)(2,1)S(1)} %get-tuple-element.151), channel_id=1, source_target_pairs={{0,1},{1,2},{2,3},{4,5},{5,6},{6,7},{8,9},{9,10},{10,11},{12,13},{... | collective-permute-start | bytes 1769480 | tf_op jit(solution)/shard_map/ppermute | solution.py:850
  285.4 76.5 %collective-permute-start.4 = (bf16[384,768]{1,0:T(8,128)(2,1)S(1)}, bf16[384,768]{1,0:T(8,128)(2,1)S(1)}, u32[]{:S(2)}, u32[]{:S(2)}) collective-permute-start(bf16[384,768]{1,0:T(8,128)(2,1)S(1)} %get-tuple-element.150), channel_id=1, source_target_pairs={{1,0},{2,1},{3,2},{5,4},{6,5},{7,6},{9,8},{10,9},{11,10},{13,12},{... | collective-permute-start | bytes 1769480 | tf_op jit(solution)/shard_map/ppermute | solution.py:849
  287.8 71.0 %copy-start.21 = (f32[4,1,384]{2,1,0:T(1,128)S(1)}, f32[4,1,384]{2,1,0:T(1,128)}, u32[]{:S(2)}) copy-start(f32[4,1,384]{2,1,0:T(1,128)} %get-tuple-element.99) | copy-start | bytes 18436
  287.8 71.2 %copy-start.20 = (f32[4,1,256]{2,1,0:T(1,128)S(1)}, f32[4,1,256]{2,1,0:T(1,128)}, u32[]{:S(2)}) copy-start(f32[4,1,256]{2,1,0:T(1,128)} %get-tuple-element.98) | copy-start | bytes 12292
  287.8 74.0 %copy-start.8 = (f32[384,768]{1,0:T(8,128)S(1)}, f32[384,768]{1,0:T(8,128)}, u32[]{:S(2)}) copy-start(f32[384,768]{1,0:T(8,128)} %get-tuple-element.77) | copy-start | bytes 3538948
  382.0 28.6 %copy-start.12 = (f32[8,768]{1,0:T(8,128)S(1)}, f32[8,768]{1,0:T(8,128)}, u32[]{:S(2)}) copy-start(f32[8,768]{1,0:T(8,128)} %get-tuple-element.93) | copy-start | bytes 73732
  382.0 28.6 %copy-start.13 = (f32[4,1,768]{2,1,0:T(1,128)S(1)}, f32[4,1,768]{2,1,0:T(1,128)}, u32[]{:S(2)}) copy-start(f32[4,1,768]{2,1,0:T(1,128)} %get-tuple-element.96) | copy-start | bytes 36868
  382.0 28.6 %copy-start.11 = (f32[9216]{0:T(1024)S(1)}, f32[9216]{0:T(1024)}, u32[]{:S(2)}) copy-start(f32[9216]{0:T(1024)} %pad_maximum_fusion.5) | copy-start | bytes 110596
  490.8 0.6 copy-start.10
  490.9 1.9 copy-start.5
  493.1 2.3 copy-start
  495.4 6.4 %copy-start.2 = (f32[96,2304]{1,0:T(8,128)S(1)}, f32[96,2304]{1,0:T(8,128)}, u32[]{:S(2)}) copy-start(f32[96,2304]{1,0:T(8,128)} %scatter_grads.3) | copy-start | bytes 2654212
  495.4 6.4 %copy-start.4 = (f32[96,2304]{1,0:T(8,128)S(1)}, f32[96,2304]{1,0:T(8,128)}, u32[]{:S(2)}) copy-start(f32[96,2304]{1,0:T(8,128)} %get-tuple-element.101) | copy-start | bytes 2654212
  496.5 6.5 %slice-start = ((f32[2,9216]{1,0:T(2,128)}), f32[2,1536]{1,0:T(2,128)S(1)}, s32[]{:S(2)}) async-start(f32[2,9216]{1,0:T(2,128)} %copy-done.10), calls=%async_computation | async-start | bytes 24576 | tf_op jit(solution)/shard_map/slice | solution.py:887
  496.5 10.3 %collective-permute-start.7 = (bf16[384,768]{1,0:T(8,128)(2,1)}, bf16[384,768]{1,0:T(8,128)(2,1)}, u32[]{:S(2)}, u32[]{:S(2)}) collective-permute-start(bf16[384,768]{1,0:T(8,128)(2,1)} %get-tuple-element.149), channel_id=1, source_target_pairs={{0,1},{1,2},{2,3},{4,5},{5,6},{6,7},{8,9},{9,10},{10,11},{12,13},{... | collective-permute-start | bytes 1769480 | tf_op jit(solution)/shard_map/ppermute | solution.py:850
  499.1 11.5 %collective-permute-start.6 = (bf16[384,768]{1,0:T(8,128)(2,1)}, bf16[384,768]{1,0:T(8,128)(2,1)}, u32[]{:S(2)}, u32[]{:S(2)}) collective-permute-start(bf16[384,768]{1,0:T(8,128)(2,1)} %get-tuple-element.148), channel_id=1, source_target_pairs={{1,0},{2,1},{3,2},{5,4},{6,5},{7,6},{9,8},{10,9},{11,10},{13,12},{... | collective-permute-start | bytes 1769480 | tf_op jit(solution)/shard_map/ppermute | solution.py:849
  501.8 2.0 slice-start.2
  502.1 4.1 slice-start.1
  502.1 8.6 %copy-start.7 = (f32[384,768]{1,0:T(8,128)S(1)}, f32[384,768]{1,0:T(8,128)}, u32[]{:S(2)}) copy-start(f32[384,768]{1,0:T(8,128)} %get-tuple-element.90) | copy-start | bytes 3538948

commit v3 on v1

v3 whole, which is shorter than its diff:
```python
import functools

import jax
import jax.numpy as jnp
from jax import lax
from jax.experimental import pallas as pl
from jax.experimental.pallas import tpu as pltpu
from jax.sharding import PartitionSpec as P

HD = 64
PACK = 512
BLK = 128
PER = PACK // BLK
WIN = 2 * PACK
EPS = 1e-05
NEG = -1e30
MESH = pl.DeviceIdType.MESH
BF = jnp.bfloat16
F32 = jnp.float32
I32 = jnp.int32
HBM = pl.BlockSpec(memory_space=pltpu.MemorySpace.HBM)
VMEM = pl.BlockSpec(memory_space=pltpu.MemorySpace.VMEM)
SMEM = pl.BlockSpec(memory_space=pltpu.MemorySpace.SMEM)
Q_AT, KV_AT, U_AT = 0, 256, 640


def dot(a, b):
    return jnp.dot(a, b, preferred_element_type=F32)


def dot_nt(a, b):
    return lax.dot_general(a, b, (((1,), (1,)), ((), ())), preferred_element_type=F32)


def dot_tn(a, b):
    return lax.dot_general(a, b, (((0,), (0,)), ((), ())), preferred_element_type=F32)


def whole(shape):
    return pl.BlockSpec(shape, lambda t: (0,) * len(shape))


def per_t(shape, *rest):
    tail = rest if rest else (0,) * (len(shape) - 1)
    return pl.BlockSpec(shape, lambda t: (t,) + tail)


def sds(shape, dtype=F32):
    return jax.ShapeDtypeStruct(shape, dtype)


def column_sum(value):
    return jnp.sum(value, axis=0, keepdims=True)


def flip(value):
    return value.astype(F32).T.astype(BF)


class Place:
    def __init__(self, n_dp, n_tensor):
        self.n_dp, self.n_tensor = n_dp, n_tensor
        self.nz = n_dp // 2
        dp, tensor = lax.axis_index("dp"), lax.axis_index("tensor")
        self.dp, self.tensor = dp, tensor
        self.z, self.y = dp // 2, dp % 2
        self.x, self.c = tensor // 2, tensor % 2
        self.dp_y = 2 * self.z + 1 - self.y
        self.t_x = 2 * (1 - self.x) + self.c
        self.t_c = 2 * self.x + 1 - self.c
        self.t_xc = 2 * (1 - self.x) + 1 - self.c
        self.to_x = (dp, self.t_x)
        self.to_y = (self.dp_y, tensor)
        self.to_c = (dp, self.t_c)

    def d(self, z, same_y=True):
        return 2 * z + (self.y if same_y else 1 - self.y)

    def near(self):
        return [(self.to_x, None), (self.to_y, None), (self.to_c, None)]

    def along_z(self):
        return [((self.dp - 2, self.tensor), self.z > 0), ((self.dp + 2, self.tensor), self.z < self.nz - 1)]

    def far_z(self):
        return [((self.dp ^ (2 << b), self.tensor), None) for b in range(1, bits(self.nz))]

    def beside(self):
        other = self.tensor - 1 + 2 * self.c
        return [((self.dp, other), jnp.logical_and(other >= 0, other < self.n_tensor))]


def meet(peers):
    barrier = pltpu.get_barrier_semaphore()
    count = 0
    for device, valid in peers:
        def signal(device=device):
            pl.semaphore_signal(barrier, inc=1, device_id=device, device_id_type=MESH)
        if valid is None:
            signal()
            count = count + 1
        else:
            pl.when(valid)(signal)
            count = count + valid.astype(I32)
    pl.semaphore_wait(barrier, count)


def bits(n):
    return n.bit_length() - 1


def pairs(me):
    found = [(me.dp, me.tensor ^ (1 << b)) for b in range(bits(me.n_tensor))]
    return found + [(me.dp ^ (1 << b), me.tensor) for b in range(bits(me.n_dp))]


def rounds_of(n_dp, n_tensor):
    return bits(n_dp) + bits(n_tensor)


def doubling_sum(me, first, total_ref, part_ref, come_ref, send_sem, recv_sem):
    copies = [
        pltpu.make_async_remote_copy(
            src_ref=part_ref.at[i], dst_ref=come_ref.at[i], send_sem=send_sem.at[i], recv_sem=recv_sem.at[i],
            device_id=device, device_id_type=MESH,
        )
        for i, device in enumerate(pairs(me))
    ]

    def begin():
        first()
        copies[0].start()

    def middle(i):
        copies[i].wait_recv()
        total = part_ref[i] + come_ref[i]
        if i + 1 < len(copies):
            part_ref[i + 1] = total
            copies[i + 1].start()
        else:
            total_ref[...] = total

    def end():
        for copy in copies:
            copy.wait_send()

    return [begin] + [functools.partial(middle, i) for i in range(len(copies))] + [end]


def doubling_scratch(shape, n_dp, n_tensor):
    n = rounds_of(n_dp, n_tensor)
    return [
        pltpu.VMEM((n,) + shape, F32), pltpu.VMEM((n,) + shape, F32),
        pltpu.SemaphoreType.DMA((n,)), pltpu.SemaphoreType.DMA((n,)),
    ]


class Window:
    def __init__(self, me, tokens, rows):
        self.me, self.count, self.rows = me, tokens // BLK, rows

    def first(self, t):
        return jnp.minimum(t * self.count // PER, self.rows - 2)

    def blocks(self):
        t = self.me.tensor
        found = []
        for j in range(self.count):
            g = t * self.count + j
            found.append((g // PER, g // PER - self.first(t), g % PER))
        return found

    def needed(self, source, j, target):
        g = source * self.count + j
        row = g // PER
        inside = jnp.logical_and(row >= target * self.count // PER, row <= (target * self.count + self.count - 1) // PER)
        exists = jnp.logical_and(jnp.logical_and(source >= 0, source < self.me.n_tensor),
                                 jnp.logical_and(target >= 0, target < self.me.n_tensor))
        return jnp.logical_and(inside, exists), g - self.first(target) * PER

    def own_places(self):
        t = self.me.tensor
        return [t * self.count + j - self.first(t) * PER for j in range(self.count)]

    def _each(self, outgoing):
        t = self.me.tensor
        for i, step in enumerate((1, -1)):
            for j in range(self.count):
                source, target = (t, t + step) if outgoing else (t - step, t)
                valid, place = self.needed(source, j, target)
                yield i * self.count + j, j, source, target, valid, pl.multiple_of(place * BLK, BLK)

    def _copy(self, source, target, slot, device, sems):
        return pltpu.make_async_remote_copy(
            src_ref=source, dst_ref=target, send_sem=sems[0].at[slot], recv_sem=sems[1].at[slot],
            device_id=(self.me.dp, device), device_id_type=MESH,
        )

    def send(self, low_ref, win_ref, sems, what="start"):
        for slot, j, source, target, valid, place in self._each(True):
            copy = self._copy(low_ref.at[pl.ds(j * BLK, BLK)], win_ref.at[pl.ds(place, BLK)], slot, target, sems)
            pl.when(valid)(getattr(copy, what))

    def receive(self, win_ref, sems):
        for slot, j, source, target, valid, place in self._each(False):
            here = win_ref.at[pl.ds(place, BLK)]
            pl.when(valid)(pltpu.make_async_copy(here, here, sems[1].at[slot]).wait)

    def send_back(self, grad_ref, back_ref, sems, what="start"):
        for slot, j, source, target, valid, place in self._each(False):
            copy = self._copy(grad_ref.at[pl.ds(place, BLK)], back_ref.at[slot], slot, source, sems)
            pl.when(valid)(getattr(copy, what))

    def receive_back(self, back_ref, sems, add):
        for slot, j, source, target, valid, place in self._each(True):
            def take(slot=slot, j=j):
                pltpu.make_async_copy(back_ref.at[slot], back_ref.at[slot], sems[1].at[slot]).wait()
                add(j, back_ref[slot])
            pl.when(valid)(take)

    def sems(tokens):
        n = 2 * (tokens // BLK)
        return [pltpu.SemaphoreType.DMA((n,)), pltpu.SemaphoreType.DMA((n,))]


class Gather:
    def __init__(self, own, n_dp, n_tensor):
        rows, cols = own.shape
        slots = 12 * (n_dp // 2)
        self.operands, self.in_specs = [own], [HBM]
        self.out_shape, self.out_specs = [sds((n_tensor, n_dp, rows, cols), own.dtype)], [HBM]
        self.scratch = [pltpu.SemaphoreType.DMA, pltpu.SemaphoreType.DMA((slots,)), pltpu.SemaphoreType.DMA((slots,))]

    def peers(self, me):
        return me.near() + me.along_z()

    def rounds(self, me, own_ref, out_ref, own_sem, send_sem, recv_sem):
        nz, cols = me.nz, own_ref.shape[-1]
        sixth = cols // 6 // 128 * 128
        cuts = {None: (0, cols), 0: (0, cols // 2), 1: (cols // 2, cols), 2: (0, sixth), 3: (sixth, 2 * sixth), 4: (2 * sixth, cols)}

        def piece(t, d, part):
            lo, hi = cuts[part]
            return out_ref.at[t, d] if part is None else out_ref.at[t, d, :, pl.ds(lo, hi - lo)]

        def copy(source, t, d, part, route, p, device):
            slot = route * nz + p
            return pltpu.make_async_remote_copy(
                src_ref=source if source is not None else piece(t, d, part), dst_ref=piece(t, d, part),
                send_sem=send_sem.at[slot], recv_sem=recv_sem.at[slot], device_id=device, device_id_type=MESH,
            )

        def arrived(t, d, part, route, p):
            pltpu.make_async_copy(piece(t, d, part), piece(t, d, part), recv_sem.at[route * nz + p]).wait()

        mine = pltpu.make_async_copy(own_ref, out_ref.at[me.tensor, me.dp], own_sem)
        up, down = (me.dp + 2, me.tensor), (me.dp - 2, me.tensor)
        can_up, can_down = me.z < nz - 1, me.z > 0

        def z_copy(p, upward, source=None):
            return copy(source, me.tensor, me.d(p), None, 0 if upward else 1, p, up if upward else down)

        def x_copy(p, source=None):
            return copy(source, me.tensor, me.d(p), None, 2, p, me.to_x)

        def y_copy(p, source=None):
            return copy(source, me.tensor, me.d(p), None, 3, p, me.to_y)

        def first_copy(p, here):
            return copy(None, me.t_x, me.d(p), 0 if here else 2, 4, p, me.to_y)

        def second_copy(p, here):
            return copy(None, me.tensor, me.d(p, False), 1 if here else 3, 5, p, me.to_x)

        def diagonal_z(p, upward):
            return copy(None, me.t_x, me.d(p, False), 4, 6 if upward else 7, p, up if upward else down)

        def core_copy(kind, p, source=None):
            return copy(source, me.tensor if kind in (0, 2) else me.t_x, me.d(p, kind in (0, 1)), None, 8 + kind, p, me.to_c)

        def own_round():
            mine.start()
            pl.when(can_up)(z_copy(me.z, True, own_ref).start)
            pl.when(can_down)(z_copy(me.z, False, own_ref).start)
            x_copy(me.z, own_ref).start()
            y_copy(me.z, own_ref).start()
            core_copy(0, me.z, own_ref).start()

        def z_round(p, upward, valid):
            @pl.when(valid)
            def _():
                arrived(me.tensor, me.d(p), None, 0 if upward else 1, p)
                pl.when(can_up if upward else can_down)(z_copy(p, upward).start)
                x_copy(p).start()
                y_copy(p).start()
                core_copy(0, p).start()

        def xy_round(p, here, valid=None):
            def go():
                arrived(me.t_x, me.d(p), None, 2, p)
                first_copy(p, here).start()
                core_copy(1, p).start()
                arrived(me.tensor, me.d(p, False), None, 3, p)
                second_copy(p, here).start()
                core_copy(2, p).start()
            go() if valid is None else pl.when(valid)(go)

        def diagonal_here():
            arrived(me.t_x, me.d(me.z, False), 0, 4, me.z)
            arrived(me.t_x, me.d(me.z, False), 1, 5, me.z)
            pl.when(can_up)(diagonal_z(me.z, True).start)
            pl.when(can_down)(diagonal_z(me.z, False).start)
            core_copy(3, me.z).start()

        def diagonal_round(p, upward, valid):
            @pl.when(valid)
            def _():
                arrived(me.t_x, me.d(p, False), 4, 6 if upward else 7, p)
                pl.when(can_up if upward else can_down)(diagonal_z(p, upward).start)
                arrived(me.t_x, me.d(p, False), 2, 4, p)
                arrived(me.t_x, me.d(p, False), 3, 5, p)
                core_copy(3, p).start()

        def middle(s):
            low, high = me.z - s, me.z + s
            if s < nz:
                z_round(low, True, low >= 0)
                z_round(high, False, high < nz)
            if s == 1:
                xy_round(me.z, True)
            elif s - 1 < nz:
                xy_round(low + 1, False, low + 1 >= 0)
                xy_round(high - 1, False, high - 1 < nz)
            if s == 2:
                diagonal_here()
            elif 2 < s < nz + 2:
                diagonal_round(low + 2, True, low + 2 >= 0)
                diagonal_round(high - 2, False, high - 2 < nz)

        def end():
            for p in range(nz):
                for kind in range(4):
                    arrived(me.t_c if kind in (0, 2) else me.t_xc, me.d(p, kind in (0, 1)), None, 8 + kind, p)
            mine.wait()
            for p in range(nz):
                here = me.z == p
                pl.when(jnp.logical_and(can_up, p <= me.z))(z_copy(p, True).wait_send)
                pl.when(jnp.logical_and(can_down, p >= me.z))(z_copy(p, False).wait_send)
                x_copy(p).wait_send()
                y_copy(p).wait_send()
                for made in (first_copy, second_copy):
                    pl.when(here)(made(p, True).wait_send)
                    pl.when(jnp.logical_not(here))(made(p, False).wait_send)
                pl.when(jnp.logical_and(can_up, p <= me.z))(diagonal_z(p, True).wait_send)
                pl.when(jnp.logical_and(can_down, p >= me.z))(diagonal_z(p, False).wait_send)
                for kind in range(4):
                    core_copy(kind, p).wait_send()

        return [own_round] + [functools.partial(middle, s) for s in range(1, nz + 2)] + [end]


class Scatter:
    def __init__(self, grads, n_dp, n_tensor):
        rows, cols = grads.shape[1] // n_dp, grads.shape[2]
        nz = n_dp // 2
        self.operands, self.in_specs = [grads.reshape(n_tensor, n_dp, rows, cols)], [HBM]
        self.out_shape, self.out_specs = [sds((rows, cols))], [pl.BlockSpec((rows, cols), lambda *_: (0, 0))]
        self.scratch = [
            pltpu.VMEM((4, nz, rows, cols), BF),
            pltpu.VMEM((4, nz, rows, cols), BF),
            pltpu.VMEM((nz, rows, cols // 2), BF),
            pltpu.VMEM((nz, rows, cols // 2), BF),
            pltpu.VMEM((nz, rows, cols), BF),
            pltpu.VMEM((nz, rows, cols), BF),
            pltpu.VMEM((nz - 1, rows, cols), BF),
            pltpu.SemaphoreType.DMA((4 * nz,)),
            pltpu.SemaphoreType.DMA((9 * nz,)),
            pltpu.SemaphoreType.DMA((9 * nz,)),
        ]

    def order(self, me):
        return [lax.rem(me.z + k, me.nz) for k in range(1, me.nz)] + [me.z]

    def peers(self, me):
        return me.near() + [((me.d(z), me.tensor), None) for z in self.order(me)[:-1]]

    def rounds(
        self, me, g_ref, out_ref, mine, core_in, first_in, second_in, x_in, y_in, z_in, load_sem, send_sem, recv_sem
    ):
        nz = me.nz
        half = g_ref.shape[-1] // 2
        zs = self.order(me)

        def owner(place, k):
            return place in (0, 1), me.d(zs[k], place not in (0, 2))

        def remote(source, target, slot, device):
            return pltpu.make_async_remote_copy(
                src_ref=source, dst_ref=target, send_sem=send_sem.at[slot], recv_sem=recv_sem.at[slot],
                device_id=device, device_id_type=MESH,
            )

        def to_core(place, k):
            x_other, d = owner(place, k)
            return remote(g_ref.at[me.t_xc if x_other else me.t_c, d], core_in.at[place, k], place * nz + k, me.to_c)

        def load(place, k):
            x_other, d = owner(place, k)
            return pltpu.make_async_copy(
                g_ref.at[me.t_x if x_other else me.tensor, d], mine.at[place, k], load_sem.at[place * nz + k]
            )

        def first(k):
            return remote(mine.at[0, k, :, pl.ds(0, half)], first_in.at[k], 4 * nz + k, me.to_x)

        def second(k):
            return remote(mine.at[0, k, :, pl.ds(half, half)], second_in.at[k], 5 * nz + k, me.to_y)

        def along_x(k):
            return remote(mine.at[1, k], x_in.at[k], 6 * nz + k, me.to_x)

        def along_y(k):
            return remote(mine.at[2, k], y_in.at[k], 7 * nz + k, me.to_y)

        def along_z(k):
            return remote(mine.at[3, k], z_in.at[k], 8 * nz + k, (me.d(zs[k]), me.tensor))

        def both(place, k):
            load(place, k).wait()
            to_core(place, k).wait_recv()
            return mine[place, k].astype(F32) + core_in[place, k].astype(F32)

        def begin():
            for k in range(nz):
                for place in range(4):
                    to_core(place, k).start()
                    load(place, k).start()

        def middle(step):
            if step < nz:
                k = step
                mine[0, k] = both(0, k).astype(BF)
                first(k).start()
                second(k).start()
            if 0 <= step - 1 < nz:
                k = step - 1
                total = both(1, k)
                second(k).wait_recv()
                mine[1, k, :, :half] = total[:, :half].astype(BF)
                mine[1, k, :, half:] = (total[:, half:] + second_in[k].astype(F32)).astype(BF)
                along_x(k).start()
                total = both(2, k)
                first(k).wait_recv()
                mine[2, k, :, half:] = total[:, half:].astype(BF)
                mine[2, k, :, :half] = (total[:, :half] + first_in[k].astype(F32)).astype(BF)
                along_y(k).start()
            if 0 <= step - 2 < nz:
                k = step - 2
                total = both(3, k)
                along_x(k).wait_recv()
                total += x_in[k].astype(F32)
                along_y(k).wait_recv()
                total += y_in[k].astype(F32)
                if k < nz - 1:
                    mine[3, k] = total.astype(BF)
                    along_z(k).start()
                else:
                    for j in range(nz - 1):
                        along_z(j).wait_recv()
                        total += z_in[j].astype(F32)
                    out_ref[...] = total

        def end():
            for k in range(nz):
                for place in range(4):
                    to_core(place, k).wait_send()
                for made in (first, second, along_x, along_y):
                    made(k).wait_send()
                if k < nz - 1:
                    along_z(k).wait_send()

        return [begin] + [functools.partial(middle, step) for step in range(nz + 2)] + [end]


class Still:
    operands, in_specs, out_shape, out_specs, scratch = [], [], [], [], []


def call(kernel, name, side, mesh_sizes, collective_id, operands, in_specs, out_shape, out_specs, scratch, early=1):
    n = mesh_sizes[1]
    n_in, n_out, n_scr = len(operands), len(out_shape), len(scratch)
    m_in, m_out = len(side.operands), len(side.out_shape)

    def body(*refs):
        me = Place(*mesh_sizes)
        cut, parts = 0, []
        for size in (n_in, m_in, n_out, m_out, n_scr):
            parts.append(refs[cut : cut + size])
            cut += size
        parts.append(refs[cut:])
        rounds = []
        if not isinstance(side, Still):
            rounds = side.rounds(me, *parts[1], *parts[3], *parts[5])
        step = pl.program_id(0)

        def before(peers=()):
            if not rounds:
                return
            for i in range(n):
                @pl.when(step == i)
                def _(i=i):
                    if i == 0:
                        meet(side.peers(me) + list(peers))
                        for turn in rounds[:early]:
                            turn()
                    else:
                        rounds[early + i - 1]()

        def after():
            for turn in rounds[early + n - 1 :]:
                turn()

        kernel(me, before, after, *parts[0], *parts[2], *parts[4])

    remote = {} if isinstance(side, Still) else dict(collective_id=collective_id, has_side_effects=True)
    return pl.pallas_call(
        body, grid=(n,), in_specs=in_specs + side.in_specs, out_specs=out_specs + side.out_specs,
        out_shape=out_shape + side.out_shape, scratch_shapes=scratch + side.scratch,
        compiler_params=pltpu.CompilerParams(vmem_limit_bytes=60 * 1024 * 1024, **remote), name=name,
    )(*operands, *side.operands)


def start_kernel(
    n_dp, n_tensor, gather, rows,
    qkv_ref, ow_ref, up_ref, down_ref, qvb_ref, ub_ref, own_ref,
    a1_ref, f0_ref, f1_ref, win_ref, bias_ref, ga_ref,
    a0_ref, part_ref, come_ref, few_send, few_recv, win_send, win_recv, *gather_sems,
):
    me = Place(n_dp, n_tensor)
    layers = qkv_ref.shape[0]
    window = Window(me, own_ref.shape[0], rows)

    def pack_a(l, target):
        units = qkv_ref.shape[3]
        target[:, 0:units] = qkv_ref[l, 0]
        target[:, units : 2 * units] = flip(ow_ref[l])
        target[:, 2 * units : 3 * units] = qkv_ref[l, 1]
        target[:, 3 * units : 4 * units] = qkv_ref[l, 2]

    def pack_f(l, target):
        units = up_ref.shape[2]
        target[:, 0:units] = up_ref[l]
        target[:, units : 2 * units] = flip(down_ref[l])

    def place_biases():
        piece, wide = qvb_ref.shape[2], ub_ref.shape[1]
        units = qkv_ref.shape[3]
        width = bias_ref.shape[1]

        def spread(values, start):
            size = values.shape[1]
            source = lax.broadcasted_iota(I32, (size, width), 0)
            target = lax.broadcasted_iota(I32, (size, width), 1)
            return dot(values, (target == source + start).astype(F32).astype(BF))

        u = spread(ub_ref[...], U_AT + me.dp * wide)
        line = lax.broadcasted_iota(I32, (layers * n_tensor, width), 0)
        total = jnp.zeros((layers * n_tensor, width), F32)
        for l in range(layers):
            row = u[l : l + 1]
            row += spread(qvb_ref[l], Q_AT + me.dp * piece)[0:1]
            row += spread(qvb_ref[l], KV_AT + units + me.dp * piece)[1:2]
            total += jnp.where(line == l * n_tensor + me.tensor, row, 0.0)
        part_ref[0] = total

    pack_a(0, a0_ref)
    win_ref[...] = jnp.zeros(win_ref.shape, BF)
    meet(gather.peers(me) + me.far_z() + me.beside())
    turns = gather.rounds(me, a0_ref, ga_ref, *gather_sems)
    few = doubling_sum(me, place_biases, bias_ref, part_ref, come_ref, few_send, few_recv)
    turns[0]()
    window.send(own_ref, win_ref, (win_send, win_recv))
    few[0]()
    for j, place in enumerate(window.own_places()):
        win_ref[pl.ds(pl.multiple_of(place * BLK, BLK), BLK), :] = own_ref[pl.ds(j * BLK, BLK), :]
    turns[1]()
    few[1]()
    pack_f(0, f0_ref)
    turns[2]()
    few[2]()
    pack_a(1, a1_ref)
    turns[3]()
    few[3]()
    pack_f(1, f1_ref)
    rest, more = turns[4:], few[4:]
    for i in range(max(len(rest), len(more))):
        if i < len(rest):
            rest[i]()
        if i < len(more):
            more[i]()
    window.receive(win_ref, (win_send, win_recv))
    window.send(own_ref, win_ref, (win_send, win_recv), "wait_send")


def start(qkv, ow, up, down, qvb, ub, own, rows, n_dp, n_tensor):
    layers, _, shard, units = qkv.shape
    tokens, dim = own.shape
    a_shape, f_shape = (shard, 4 * units), (shard, 2 * up.shape[2])
    width = U_AT + up.shape[2]
    gather = Gather(sds(a_shape, BF), n_dp, n_tensor)
    few = (layers * n_tensor, width)
    return pl.pallas_call(
        functools.partial(start_kernel, n_dp, n_tensor, gather, rows),
        in_specs=[VMEM] * 7,
        out_specs=[VMEM] * 5 + [HBM],
        out_shape=[sds(a_shape, BF), sds(f_shape, BF), sds(f_shape, BF), sds((WIN, dim), BF), sds(few)] + gather.out_shape,
        scratch_shapes=[pltpu.VMEM(a_shape, BF)] + doubling_scratch(few, n_dp, n_tensor) + Window.sems(tokens) + gather.scratch,
        compiler_params=pltpu.CompilerParams(vmem_limit_bytes=40 * 1024 * 1024, collective_id=0, has_side_effects=True),
        name="start",
    )(qkv, ow, up, down, qvb, ub, own)


def ends_of(len_ref, row):
    total, ends = 0, []
    for k in range(len_ref.shape[1]):
        total = total + len_ref[row, k]
        ends.append(total)
    return ends


def segments(ends, place):
    seg = jnp.zeros(place.shape, I32)
    for end in ends:
        seg += (place >= end).astype(I32)
    return jnp.where(seg == len(ends), -1, seg)


def allowed_of(len_ref, row, offset, key_axis, heads):
    ends = ends_of(len_ref, row)
    k_shape = (1, PACK) if key_axis == 1 else (PACK, 1)
    q_shape = (BLK, 1) if key_axis == 1 else (1, BLK)
    kseg = segments(ends, lax.broadcasted_iota(I32, k_shape, key_axis))
    qseg = segments(ends, lax.broadcasted_iota(I32, q_shape, 1 - key_axis) + offset)
    allowed = jnp.logical_and(kseg >= 0, jnp.logical_or(kseg == qseg, qseg < 0))
    return jnp.concatenate([allowed] * heads, axis=1 - key_axis)


def lane_masks(first, count):
    slot = lax.broadcasted_iota(jnp.int32, (1, 256), 1) // HD
    return [(slot == first + i).astype(F32).astype(BF) for i in range(count)]


def stack_heads(block, masks):
    return jnp.concatenate([block * mask for mask in masks], axis=0)


def pick_heads(stacked, masks, size):
    total = None
    for i, mask in enumerate(masks):
        part = stacked[i * size : (i + 1) * size] * mask.astype(F32)
        total = part if total is None else total + part
    return total


def norm_forward(value, gain, shift):
    average = jnp.mean(value, axis=-1, keepdims=True)
    centered = value - average
    variance = jnp.mean(centered * centered, axis=-1, keepdims=True)
    scaled = lax.rsqrt(variance + EPS)
    unit = centered * scaled
    return unit * gain + shift, unit, scaled


def norm_back(grad, unit, scaled, gain):
    inner = grad * gain
    centered = inner - jnp.mean(inner, axis=-1, keepdims=True)
    return scaled * (centered - unit * jnp.mean(inner * unit, axis=-1, keepdims=True))


def attn_fwd_kernel(
    rows, layer, me, before, after, len_ref, win_ref, own_ref, g_ref, bias_ref, ob_ref, gain_ref, shift_ref,
    q_ref, kv_ref, ctx_ref, mid_ref, unit_ref, rs_ref, acc_ref,
):
    step, n = pl.program_id(0), pl.num_programs(0)
    tokens = own_ref.shape[0]
    heads = 3
    before()
    line = pl.ds(layer * me.n_tensor + step, 1)
    kv_ref[0] = (dot(win_ref[...], g_ref[0, :, 384:768]) + bias_ref[line, KV_AT : KV_AT + 384]).astype(BF)
    q_ref[0] = (dot(own_ref[...].astype(BF), g_ref[0, :, 0:256]) + bias_ref[line, Q_AT : Q_AT + 256]).astype(BF)
    q_masks, c_masks = lane_masks(0, heads), lane_masks(1, heads)
    for j, (row, slot, part) in enumerate(Window(me, tokens, rows).blocks()):
        here = pl.ds(j * BLK, BLK)
        keys = pl.ds(pl.multiple_of(slot * PACK, PACK), PACK)
        stacked = stack_heads(q_ref[0, here, :], q_masks)
        scores = dot_nt(stacked, kv_ref[0, keys, 0:256]) * (HD**-0.5)
        scores = jnp.where(allowed_of(len_ref, row, part * BLK, 1, heads), scores, NEG)
        peak = jnp.max(scores, axis=-1, keepdims=True)
        weights = jnp.exp(scores - peak)
        probs = weights * (1.0 / jnp.sum(weights, axis=-1, keepdims=True))
        out = dot(probs.astype(BF), kv_ref[0, keys, 128:384])
        ctx_ref[0, here, :] = pick_heads(out, c_masks, BLK).astype(BF)
    part = dot_nt(ctx_ref[0], g_ref[0, :, 128:384])

    @pl.when(step == 0)
    def _():
        acc_ref[...] = part

    @pl.when(step > 0)
    def _():
        acc_ref[...] += part

    @pl.when(step == n - 1)
    def _():
        line = pl.ds(layer, 1)
        total = own_ref[...].astype(F32) + acc_ref[...] + ob_ref[line, :]
        mid_ref[...], unit_ref[...], rs_ref[...] = norm_forward(total, gain_ref[line, :], shift_ref[line, :])
        after()


def attn_fwd(side, cid, layer, sizes, lens, win, own, g, bias, ob, gain, shift):
    n, (tokens, dim) = sizes[1], own.shape
    full = whole((tokens, dim))
    return call(
        functools.partial(attn_fwd_kernel, lens.shape[0], layer), "attn_fwd", side, sizes, cid,
        [lens, win, own, g, bias, ob, gain, shift],
        [SMEM, whole(win.shape), full, per_t((1, dim, dim)), whole(bias.shape)] + [whole(ob.shape)] * 3,
        [sds((n, tokens, 256), BF), sds((n, WIN, 384), BF), sds((n, tokens, 256), BF)]
        + [sds((tokens, dim)), sds((tokens, dim)), sds((tokens, 1))],
        [per_t((1, tokens, 256)), per_t((1, WIN, 384)), per_t((1, tokens, 256)), full, full, whole((tokens, 1))],
        [pltpu.VMEM((tokens, dim), F32)],
    )


def ffn_fwd_kernel(rows, layer, hand_on, me, before, after, mid_ref, up_ref, down_ref, bias_ref, db_ref, gain_ref, shift_ref, *refs):
    act_ref, slope_ref, out_ref, unit_ref, rs_ref, *refs = refs
    if hand_on:
        win_out_ref, acc_ref, low_ref, win_ref, *sems = refs
    else:
        (acc_ref,) = refs
    step, n = pl.program_id(0), pl.num_programs(0)
    dim = mid_ref.shape[1]
    if hand_on:
        @pl.when(step == 0)
        def _():
            win_ref[...] = jnp.zeros(win_ref.shape, BF)
    before(me.beside())
    upper = dot(mid_ref[...].astype(BF), up_ref[0]) + bias_ref[pl.ds(layer * me.n_tensor + step, 1), U_AT : U_AT + dim]
    half = 0.5 + 0.5 * lax.erf(upper * (0.5**0.5))
    act_ref[0] = (upper * half).astype(BF)
    slope_ref[0] = (half + upper * (jnp.exp(-0.5 * upper * upper) * 0.3989422804014327)).astype(BF)
    part = dot_nt(act_ref[0], down_ref[0])

    @pl.when(step == 0)
    def _():
        acc_ref[...] = part

    @pl.when(step > 0)
    def _():
        acc_ref[...] += part

    @pl.when(step == n - 1)
    def _():
        line = pl.ds(layer, 1)
        total = mid_ref[...] + acc_ref[...] + db_ref[line, :]
        out, unit_ref[...], rs_ref[...] = norm_forward(total, gain_ref[line, :], shift_ref[line, :])
        out_ref[...] = out
        if hand_on:
            window = Window(me, mid_ref.shape[0], rows)
            low_ref[...] = out.astype(BF)
            window.send(low_ref, win_ref, sems)
            for j, place in enumerate(window.own_places()):
                win_ref[pl.ds(pl.multiple_of(place * BLK, BLK), BLK), :] = low_ref[pl.ds(j * BLK, BLK), :]
        after()
        if hand_on:
            window.receive(win_ref, sems)
            win_out_ref[...] = win_ref[...]
            window.send(low_ref, win_ref, sems, "wait_send")


def ffn_fwd(side, cid, layer, sizes, rows, mid, g, bias, db, gain, shift):
    n, (tokens, dim) = sizes[1], mid.shape
    hand_on = not isinstance(side, Still)
    full = whole((tokens, dim))
    return call(
        functools.partial(ffn_fwd_kernel, rows, layer, hand_on), "ffn_fwd", side, sizes, cid,
        [mid, g, g, bias, db, gain, shift],
        [full, per_t((1, dim, dim), 0, 0), per_t((1, dim, dim), 0, 1), whole(bias.shape)] + [whole(db.shape)] * 3,
        [sds((n, tokens, dim), BF), sds((n, tokens, dim), BF), sds((tokens, dim)), sds((tokens, dim)), sds((tokens, 1))]
        + ([sds((WIN, dim), BF)] if hand_on else []),
        [per_t((1, tokens, dim)), per_t((1, tokens, dim)), full, full, whole((tokens, 1))]
        + ([whole((WIN, dim))] if hand_on else []),
        [pltpu.VMEM((tokens, dim), F32)]
        + ([pltpu.VMEM((tokens, dim), BF), pltpu.VMEM((WIN, dim), BF)] + Window.sems(tokens) if hand_on else []),
    )


def ffn_bwd_kernel(
    layer, me, before, after, grad_ref, mid_ref, unit2_ref, rs2_ref, unit1_ref, rs1_ref, up_ref, down_ref, act_ref, slope_ref,
    gain1_ref, gain2_ref, dg_ref, ub_ref, dvec_ref, dfirst_ref, acc_ref, low_ref, low_t_ref, mid_t_ref,
):
    step, n = pl.program_id(0), pl.num_programs(0)
    dim = grad_ref.shape[1]
    line = pl.ds(layer, 1)
    before()

    @pl.when(step == 0)
    def _():
        grad = grad_ref[...]
        dsecond = norm_back(grad, unit2_ref[...], rs2_ref[...], gain2_ref[line, :])
        dvec_ref[4:5] = column_sum(grad * unit2_ref[...])
        dvec_ref[5:6] = column_sum(grad)
        dvec_ref[3:4] = column_sum(dsecond)
        dvec_ref[6:8] = jnp.zeros((2, dim), F32)
        acc_ref[...] = dsecond
        low_ref[...] = dsecond.astype(BF)
        low_t_ref[...] = dsecond.T.astype(BF)
        mid_t_ref[...] = mid_ref[...].T.astype(BF)

    dupper = dot(low_ref[...], down_ref[0]) * slope_ref[0].astype(F32)
    ub_ref[0] = column_sum(dupper)
    dupper_low = dupper.astype(BF)
    dg_ref[0, :, 0:dim] = dot(mid_t_ref[...], dupper_low).astype(BF)
    dg_ref[0, :, dim : 2 * dim] = dot(low_t_ref[...], act_ref[0]).astype(BF)
    acc_ref[...] += dot_nt(dupper_low, up_ref[0])

    @pl.when(step == n - 1)
    def _():
        dmid = acc_ref[...]
        dfirst = norm_back(dmid, unit1_ref[...], rs1_ref[...], gain1_ref[line, :])
        dvec_ref[1:2] = column_sum(dmid * unit1_ref[...])
        dvec_ref[2:3] = column_sum(dmid)
        dvec_ref[0:1] = column_sum(dfirst)
        dfirst_ref[...] = dfirst
        after()


def ffn_bwd(side, cid, layer, sizes, grad, mid, unit2, rs2, unit1, rs1, g, act, slope, gain1, gain2):
    n, (tokens, dim) = sizes[1], mid.shape
    full, thin = whole((tokens, dim)), whole((tokens, 1))
    return call(
        functools.partial(ffn_bwd_kernel, layer), "ffn_bwd", side, sizes, cid,
        [grad, mid, unit2, rs2, unit1, rs1, g, g, act, slope, gain1, gain2],
        [full, full, full, thin, full, thin, per_t((1, dim, dim), 0, 0), per_t((1, dim, dim), 0, 1)]
        + [per_t((1, tokens, dim))] * 2 + [whole(gain1.shape)] * 2,
        [sds(g.shape, BF), sds((n, 1, dim)), sds((8, dim)), sds((tokens, dim))],
        [per_t((1, dim, 2 * dim)), per_t((1, 1, dim)), whole((8, dim)), full],
        [
            pltpu.VMEM((tokens, dim), F32), pltpu.VMEM((tokens, dim), BF),
            pltpu.VMEM((dim, tokens), BF), pltpu.VMEM((dim, tokens), BF),
        ],
        early=2,
    )


def attn_bwd_kernel(
    rows, me, before, after, len_ref, dfirst_ref, own_ref, win_ref, g_ref, q_ref, kv_ref, ctx_ref,
    dg_ref, qb_ref, vb_ref, grad_ref, low_ref, low_t_ref, own_t_ref, win_t_ref, dctx_ref, dq_ref, dkv_ref,
    win_grad_ref, win_low_ref, back_ref, *sems,
):
    step, n = pl.program_id(0), pl.num_programs(0)
    tokens = own_ref.shape[0]
    heads = 3
    before(me.beside())

    @pl.when(step == 0)
    def _():
        dfirst = dfirst_ref[...]
        low_ref[...] = dfirst.astype(BF)
        low_t_ref[...] = dfirst.T.astype(BF)
        own_t_ref[...] = flip(own_ref[...])
        win_t_ref[...] = flip(win_ref[...])
        grad_ref[...] = dfirst
        win_grad_ref[...] = jnp.zeros(win_grad_ref.shape, F32)

    dctx_ref[...] = dot(low_ref[...], g_ref[0, :, 128:384]).astype(BF)
    dkv_ref[...] = jnp.zeros(dkv_ref.shape, F32)
    q_masks, c_masks = lane_masks(0, heads), lane_masks(1, heads)
    window = Window(me, tokens, rows)
    for j, (row, slot, part) in enumerate(window.blocks()):
        here = pl.ds(j * BLK, BLK)
        keys = pl.ds(pl.multiple_of(slot * PACK, PACK), PACK)
        q_stack = stack_heads(q_ref[0, here, :], q_masks)
        d_stack = stack_heads(dctx_ref[here, :], c_masks)
        scores = dot_nt(kv_ref[0, keys, 0:256], q_stack) * (HD**-0.5)
        scores = jnp.where(allowed_of(len_ref, row, part * BLK, 0, heads), scores, NEG)
        peak = jnp.max(scores, axis=0, keepdims=True)
        weights = jnp.exp(scores - peak)
        probs = weights * (1.0 / jnp.sum(weights, axis=0, keepdims=True))
        dprobs = dot_nt(kv_ref[0, keys, 128:384], d_stack)
        weighted = probs * dprobs
        inner = jnp.sum(weighted, axis=0, keepdims=True)
        dscores = ((weighted - probs * inner) * (HD**-0.5)).astype(BF)
        dkv_ref[keys, 128:384] += dot(probs.astype(BF), d_stack)
        dkv_ref[keys, 0:256] += dot(dscores, q_stack)
        dq_ref[here, :] = pick_heads(dot_tn(dscores, kv_ref[0, keys, 0:256]), q_masks, BLK)
    dq, dkv = dq_ref[...], dkv_ref[...]
    qb_ref[0] = column_sum(dq)
    vb_ref[0] = column_sum(dkv)
    dq_low, dkv_low = dq.astype(BF), dkv.astype(BF)
    grad_q = dot(own_t_ref[...], dq_low)
    grad_o = dot(low_t_ref[...], ctx_ref[0])
    dg_ref[0, :, 0:128] = grad_q[:, 0:128].astype(BF)
    dg_ref[0, :, 128:256] = (grad_q[:, 128:256] + grad_o[:, 0:128]).astype(BF)
    dg_ref[0, :, 256:384] = grad_o[:, 128:256].astype(BF)
    dg_ref[0, :, 384:768] = dot(win_t_ref[...], dkv_low).astype(BF)
    grad_ref[...] += dot_nt(dq_low, g_ref[0, :, 0:256])
    win_grad_ref[...] += dot_nt(dkv_low, g_ref[0, :, 384:768])

    @pl.when(step == n - 1)
    def _():
        win_low_ref[...] = win_grad_ref[...].astype(BF)
        window.send_back(win_low_ref, back_ref, sems)
        for j, place in enumerate(window.own_places()):
            grad_ref[pl.ds(j * BLK, BLK), :] += win_grad_ref[pl.ds(pl.multiple_of(place * BLK, BLK), BLK), :]
        after()

        def add(j, value):
            grad_ref[pl.ds(j * BLK, BLK), :] += value.astype(F32)

        window.receive_back(back_ref, sems, add)
        window.send_back(win_low_ref, back_ref, sems, "wait_send")


def attn_bwd(side, cid, sizes, lens, dfirst, own, win, g, q, kv, ctx):
    n, (tokens, dim) = sizes[1], own.shape
    full = whole((tokens, dim))
    return call(
        functools.partial(attn_bwd_kernel, lens.shape[0]), "attn_bwd", side, sizes, cid,
        [lens, dfirst, own, win, g, q, kv, ctx],
        [SMEM, full, full, whole(win.shape), per_t((1, dim, dim)), per_t((1, tokens, 256)), per_t((1, WIN, 384)), per_t((1, tokens, 256))],
        [sds(g.shape, BF), sds((n, 1, 256)), sds((n, 1, 384)), sds((tokens, dim))],
        [per_t((1, dim, dim)), per_t((1, 1, 256)), per_t((1, 1, 384)), full],
        [
            pltpu.VMEM((tokens, dim), BF), pltpu.VMEM((dim, tokens), BF), pltpu.VMEM((dim, tokens), BF),
            pltpu.VMEM((dim, WIN), BF), pltpu.VMEM((tokens, 256), BF), pltpu.VMEM((tokens, 256), F32),
            pltpu.VMEM((WIN, 384), F32), pltpu.VMEM((WIN, dim), F32), pltpu.VMEM((WIN, dim), BF),
            pltpu.VMEM((2 * (tokens // BLK), BLK, dim), BF),
        ] + Window.sems(tokens),
        early=2,
    )


def finish_kernel(n_dp, n_tensor, scatter, layers, *refs):
    g_ref, few_refs, refs = refs[0], refs[1 : 1 + 4 * layers], refs[1 + 4 * layers :]
    out_ref, total_ref, part_ref, come_ref, few_send, few_recv, *scratch = refs
    me = Place(n_dp, n_tensor)

    def place_sums():
        part_ref[0] = jnp.zeros(part_ref.shape[1:], F32)
        for l in range(layers):
            dvec, ub, qb, vb = few_refs[4 * l : 4 * l + 4]
            at = 2 * 8 * l
            part_ref[0, at : at + 8, :] = dvec[...]
            for t in range(n_tensor):
                part_ref[0, at + 8 + t : at + 9 + t, :] = ub[t]
                part_ref[0, at + 12 + t : at + 13 + t, 0:256] = qb[t]
                part_ref[0, at + 12 + t : at + 13 + t, 256:640] = vb[t]

    meet(scatter.peers(me))
    turns = scatter.rounds(me, g_ref, out_ref, *scratch)
    few = doubling_sum(me, place_sums, total_ref, part_ref, come_ref, few_send, few_recv)
    for i in range(max(len(turns), len(few))):
        if i < len(turns):
            turns[i]()
        if i < len(few):
            few[i]()


def finish(dg, few, n_dp, n_tensor, layers):
    scatter = Scatter(dg, n_dp, n_tensor)
    rows, cols = scatter.out_shape[0].shape
    shape = (16 * layers, cols)
    return pl.pallas_call(
        functools.partial(finish_kernel, n_dp, n_tensor, scatter, layers),
        in_specs=[HBM] + [VMEM] * len(few),
        out_specs=[VMEM, VMEM],
        out_shape=[sds((rows, cols)), sds(shape)],
        scratch_shapes=doubling_scratch(shape, n_dp, n_tensor) + scatter.scratch,
        compiler_params=pltpu.CompilerParams(vmem_limit_bytes=40 * 1024 * 1024, collective_id=9, has_side_effects=True),
        name="finish",
    )(*scatter.operands, *few)


def body(n_dp, n_tensor, block_input, passage_lengths, qkv_weight, qv_bias, out_weight, out_bias, first_gain,
         first_shift, up_weight, up_bias, down_weight, down_bias, second_gain, second_shift, output_grad):
    layers = qkv_weight.shape[0]
    tokens, dim = block_input.shape
    rows = passage_lengths.shape[0]
    t, dp = lax.axis_index("tensor"), lax.axis_index("dp")
    shard, units = qkv_weight.shape[2], qkv_weight.shape[3]
    hidden_units = up_weight.shape[2]
    sizes = (n_dp, n_tensor)
    lens = passage_lengths

    def flat(g):
        return g.reshape(n_tensor, n_dp * shard, g.shape[-1])

    own = block_input
    a1, f0, f1, win, bias, ga0 = start(qkv_weight, out_weight, up_weight, down_weight, qv_bias, up_bias, own, rows, n_dp, n_tensor)
    ga, gf, kept = [flat(ga0), None], [None, None], []
    for l in range(layers):
        side = Gather(f0 if l == 0 else f1, n_dp, n_tensor)
        q, kv, ctx, mid, unit1, rs1, gathered = attn_fwd(
            side, 1 + 2 * l, l, sizes, lens, win, own, ga[l], bias, out_bias, first_gain, first_shift
        )
        gf[l] = flat(gathered)
        side = Gather(a1, n_dp, n_tensor) if l == 0 else Still()
        act, slope, out, unit2, rs2, *more = ffn_fwd(
            side, 2, l, sizes, rows, mid, gf[l], bias, down_bias, second_gain, second_shift
        )
        kept.append((own, win, q, kv, ctx, mid, unit1, rs1, act, slope, unit2, rs2))
        own = out
        if l == 0:
            win, gathered = more
            ga[1] = flat(gathered)
    block_output = own

    grad = output_grad
    da, few = None, [None] * layers
    sum_f, sum_a = [None] * layers, [None] * layers
    for l in reversed(range(layers)):
        own, win, q, kv, ctx, mid, unit1, rs1, act, slope, unit2, rs2 = kept[l]
        side = Still() if da is None else Scatter(da, n_dp, n_tensor)
        df, ub, dvec, dfirst, *more = ffn_bwd(
            side, 6, l, sizes, grad, mid, unit2, rs2, unit1, rs1, gf[l], act, slope, first_gain, second_gain
        )
        if more:
            sum_a[l + 1] = more[0]
        da, qb, vb, grad, sum_f[l] = attn_bwd(Scatter(df, n_dp, n_tensor), 5 + 2 * l, sizes, lens, dfirst, own, win, ga[l], q, kv, ctx)
        few[l] = [dvec, ub, qb, vb]
    sum_a[0], totals = finish(da, sum(few, []), n_dp, n_tensor, layers)

    totals = totals.reshape(layers, 16, dim)
    piece, wide = qv_bias.shape[2], up_bias.shape[1]
    mine = lax.dynamic_slice(totals, (0, 8 + t, 0), (layers, 1, dim))
    u_grad = lax.dynamic_slice(mine, (0, 0, dp * wide), (layers, 1, wide)).reshape(layers, wide)
    mine = lax.dynamic_slice(totals, (0, 12 + t, 0), (layers, 1, dim))
    q_grad = lax.dynamic_slice(mine, (0, 0, dp * piece), (layers, 1, piece))
    v_grad = lax.dynamic_slice(mine, (0, 0, 256 + units + dp * piece), (layers, 1, piece))
    wa, wf = jnp.stack(sum_a), jnp.stack(sum_f)
    cols = [wa[:, :, i * units : (i + 1) * units] for i in range(4)]
    return (
        block_output,
        grad,
        jnp.stack([cols[0], cols[2], cols[3]], axis=1),
        jnp.concatenate([q_grad, v_grad], axis=1),
        cols[1].transpose(0, 2, 1),
        totals[:, 0],
        totals[:, 1],
        totals[:, 2],
        wf[:, :, :hidden_units],
        u_grad,
        wf[:, :, hidden_units:].transpose(0, 2, 1),
        totals[:, 3],
        totals[:, 4],
        totals[:, 5],
    )


def solution(mesh):
    n_dp, n_tensor = mesh.shape["dp"], mesh.shape["tensor"]
    tokens = P(("dp", "tensor"), None)
    in_specs = (
        tokens, P("dp", None), P(None, None, "dp", "tensor"), P(None, None, ("tensor", "dp")), P(None, "tensor", "dp"),
        P(), P(), P(), P(None, "dp", "tensor"), P(None, ("tensor", "dp")), P(None, "tensor", "dp"), P(), P(), P(), tokens,
    )
    out_specs = (
        tokens, tokens, P(None, None, "dp", "tensor"), P(None, None, ("tensor", "dp")), P(None, "tensor", "dp"),
        P(), P(), P(), P(None, "dp", "tensor"), P(None, ("tensor", "dp")), P(None, "tensor", "dp"), P(), P(), P(),
    )
    return jax.shard_map(
        functools.partial(body, n_dp, n_tensor), mesh=mesh, in_specs=in_specs, out_specs=out_specs, check_vma=False
    )
```

time: 701 us -> 437 us (0.62)
  waiting for transfers between devices: 124 us -> 0 us
  blocking collectives: 59.3 us -> 0 us
  starting transfers between devices: 22.7 us -> 0 us
  Pallas kernels: 426 us -> 407 us
  between operations: 15 us -> 1.09 us
  local copies, waits for them, and re-layouts: 33 us -> 21.3 us
  other arithmetic: 13.3 us -> 1.91 us
    psum x1 -> x0, waiting for transfers between devices: 117 us -> none  [body(): totals = lax.psum(jnp.stack(smalls), ('dp', 'tensor'))]
    all_gather x1 -> x0, blocking collectives: 59.3 us -> none  [body(): small = lax.all_gather(small, ('tensor', 'dp'), axis=0).astype(F32)]
    ppermute x8 -> x0, starting transfers between devices: 22.7 us -> none  [the longest x2 7.5 us: window_back(): lax.ppermute(line[pad + 2 * tokens:pad + 3 * tokens].astype(BF), 'tensor'...]
    pallas_call x12 -> x10, Pallas kernels: 426 us -> 407 us  [the longest x8 335 us: call(): pl.pallas_call(body, grid=(n,), in_specs=in_specs + side.in_specs, out_sp...]
    unnamed x66 -> x54, local copies, waits for them, and re-layouts: 10.5 us -> 18.7 us
  transfers between devices with their start and end apart: 9 -> 0, of which waited for: 2 -> 0; matrix products, arithmetic and copies ran while one was open for 4% -> 0% of each run, Pallas kernels for 40% -> 0%
where the time goes in v3:
time: 437 us; the launch traced here: 431 us
  Pallas kernels  407 us (93%)
  local copies, waits for them, and re-layouts  21.3 us (5%)
    pallas_call x8, Pallas kernels, call(): pl.pallas_call(body, grid=(n,), in_specs=in_specs + side.in_specs, out_sp...  335 us
    pallas_call x1, Pallas kernels, start(): pl.pallas_call(functools.partial(start_kernel, n_dp, n_tensor, gather, ro...  38 us
    pallas_call x1, Pallas kernels, finish(): pl.pallas_call(functools.partial(finish_kernel, n_dp, n_tensor, scatter,...  33.7 us
    unnamed x54, local copies, waits for them, and re-layouts  18.7 us

profile of v3, /device:TPU:1, one launch (start us, length us, event | category | flops | bytes accessed | tf_op | source)
XLA Modules:
  0.0 431.0 jit_solution(711933766027694045)
XLA Ops:
  0.6 1.2 copy.29.down_ref
  1.8 0.0 copy-start.2
  1.8 1.1 copy-done.2
  2.9 1.0 copy-done.6
  3.9 1.0 copy-done.7
  4.8 0.9 copy-done.10
  5.7 0.7 copy-done.19
  6.4 0.7 copy-done.20
  7.1 38.0 %start.1 = (bf16[96,768]{1,0:T(8,128)(2,1)S(1)}, bf16[96,1536]{1,0:T(8,128)(2,1)S(1)}, bf16[96,1536]{1,0:T(8,128)(2,1)S(1)}, bf16[1024,768]{1,0:T(8,128)(2,1)S(1...) custom-call(bf16[2,3,96,192]{3,2,1,0:T(8,128)(2,1)S(1)} %copy-done.6, bf16[2,192,96]{2,1,0:T(8,128)(2,1)S(1)} %copy-done.10, ...), custom_call_target="tpu_custom_call" | custom-call | tf_op jit(solution)/shard_map/start/pallas_call | solution.py:612
  45.1 2.1 copy-done
  47.2 1.1 copy-done.1
  48.3 0.6 copy-done.4
  49.0 0.7 copy-done.5
  49.7 0.7 copy-done.8
  50.4 0.7 copy-done.9
  51.1 52.6 %attn_fwd.2 = (bf16[4,384,256]{2,1,0:T(8,128)(2,1)}, bf16[4,1024,384]{2,1,0:T(8,128)(2,1)}, bf16[4,384,256]{2,1,0:T(8,128)(2,1)}, f32[384,768]{1,0:T(8,128)}, f3...) custom-call(s32[3,4]{1,0:T(4,128)} %refs_0_.9, bf16[1024,768]{1,0:T(8,128)(2,1)} %copy-done.1, ...), custom_call_target="tpu_custom_call" | custom-call | tf_op jit(solution)/shard_map/attn_fwd/pallas_call | solution.py:526
  103.6 37.0 %ffn_fwd.2 = (bf16[4,384,768]{2,1,0:T(8,128)(2,1)}, bf16[4,384,768]{2,1,0:T(8,128)(2,1)}, f32[384,768]{1,0:T(8,128)}, f32[384,768]{1,0:T(8,128)}, f32[384,1]{1,0...) custom-call(f32[384,768]{1,0:T(8,128)} %get-tuple-element.71.refs_0_.refs_1_, ...), custom_call_target="tpu_custom_call" | custom-call | tf_op jit(solution)/shard_map/ffn_fwd/pallas_call | solution.py:526
  140.6 52.9 %attn_fwd.3 = (bf16[4,384,256]{2,1,0:T(8,128)(2,1)}, bf16[4,1024,384]{2,1,0:T(8,128)(2,1)}, bf16[4,384,256]{2,1,0:T(8,128)(2,1)}, f32[384,768]{1,0:T(8,128)}, f3...) custom-call(s32[3,4]{1,0:T(4,128)} %refs_0_.9, ...), custom_call_target="tpu_custom_call" | custom-call | tf_op jit(solution)/shard_map/attn_fwd/pallas_call | solution.py:526
  193.5 11.7 %ffn_fwd.3 = (bf16[4,384,768]{2,1,0:T(8,128)(2,1)}, bf16[4,384,768]{2,1,0:T(8,128)(2,1)}, f32[384,768]{1,0:T(8,128)}, f32[384,768]{1,0:T(8,128)}, f32[384,1]{1,0:T(8,128)}) custom-call(f32[384,768]{1,0:T(8,128)} %get-tuple-element.78.refs_0_.refs_1_, bf16[4,768,1536]{2,1,0:T(8,128)(2,1)} %bitcast.47, bf16[4,768,1536]{2,1,0:T(8,128)(2,1)} %bitcast.48, ...), custom_call_target="tpu_custom_call" | custom-call | tf_op jit(solution)/shard_map/ffn_fwd/pallas_call | solution.py:526
  205.2 17.4 %ffn_bwd.2 = (bf16[4,768,1536]{2,1,0:T(8,128)(2,1)}, f32[4,1,768]{2,1,0:T(1,128)}, f32[8,768]{1,0:T(8,128)}, f32[384,768]{1,0:T(8,128)}) custom-call(f32[384,768]{1,0:T(8,128)} %refs_0_.7, f32[384,768]{1,0:T(8,128)} %get-tuple-element.78.refs_0_.refs_1_, f32[384,768]{1,0:T(8,128)} %get-tuple-element.81.refs_2_, f32[384,1]{1,0:T(8,128)} %get-tuple-element.82.refs_3_, ...), custom_call_target="tpu_custom_call" | custom-call | tf_op jit(solution)/shard_map/ffn_bwd/pallas_call | solution.py:526
  222.6 56.8 %attn_bwd.2 = (bf16[4,768,768]{2,1,0:T(8,128)(2,1)}, f32[4,1,256]{2,1,0:T(1,128)}, f32[4,1,384]{2,1,0:T(1,128)}, f32[384,768]{1,0:T(8,128)}, f32[96,1536]{1,0:T(8,128)}) custom-call(s32[3,4]{1,0:T(4,128)} %refs_0_.9, f32[384,768]{1,0:T(8,128)} %get-tuple-element.87.refs_1_, f32[384,768]{1,0:T(8,128)} %get-tuple-element.75.refs_2_, ...), custom_call_target="tpu_custom_call" | custom-call | tf_op jit(solution)/shard_map/attn_bwd/pallas_call | solution.py:526
  279.4 49.2 %ffn_bwd.3 = (bf16[4,768,1536]{2,1,0:T(8,128)(2,1)}, f32[4,1,768]{2,1,0:T(1,128)}, f32[8,768]{1,0:T(8,128)}, f32[384,768]{1,0:T(8,128)}, f32[96,768]{1,0:T(8,128)}) custom-call(f32[384,768]{1,0:T(8,128)} %get-tuple-element.92.refs_0_, f32[384,768]{1,0:T(8,128)} %get-tuple-element.71.refs_0_.refs_1_, f32[384,768]{1,0:T(8,128)} %get-tuple-element.93.refs_2_, ...), custom_call_target="tpu_custom_call" | custom-call | tf_op jit(solution)/shard_map/ffn_bwd/pallas_call | solution.py:526
  328.6 0.0 copy-start.11
  328.6 0.0 copy-start.13
  328.6 57.5 %attn_bwd.3 = (bf16[4,768,768]{2,1,0:T(8,128)(2,1)}, f32[4,1,256]{2,1,0:T(1,128)}, f32[4,1,384]{2,1,0:T(1,128)}, f32[384,768]{1,0:T(8,128)}, f32[96,1536]{1,0:T(8,128)}) custom-call(s32[3,4]{1,0:T(4,128)} %refs_0_.9, f32[384,768]{1,0:T(8,128)} %get-tuple-element.100.refs_1_, bf16[384,768]{1,0:T(8,128)(2,1)} %refs_2_.3, bf16[1024,768]{1,0:T(8,128)(2,1)} %copy-done.1, ...), custom_call_target="tpu_custom_call" | custom-call | tf_op jit(solution)/shard_map/attn_bwd/pallas_call | solution.py:526
  386.2 0.0 copy-done.11
  386.2 0.0 copy-done.12
  386.2 0.0 copy-done.13
  386.2 0.0 copy-done.14
  386.2 0.0 copy-done.15
  386.2 0.0 copy-done.17
  386.3 0.0 copy-start.3
  386.3 2.3 copy-done.3
  388.6 0.7 copy-done.16
  389.3 0.7 copy-done.18
  390.0 33.7 %finish.1 = (f32[96,768]{1,0:T(8,128)S(1)}, f32[32,768]{1,0:T(8,128)S(1)}) custom-call(bf16[4,8,96,768]{3,2,1,0:T(8,128)(2,1)S(1)} %bitcast.38, f32[8,768]{1,0:T(8,128)S(1)} %copy-done.12, f32[4,1,768]{2,1,0:T(1,128)S(1)} %copy-done.14, f32[4,1,256]{2,1,0:T(1,128)S(1)} %copy-done.18, f32[4,1,384]{2,1,0:T(1,128)S(1)} %copy-done.16, f32[8,768]{1,0:T(8,128)S(1)} %copy-done.11, ...), custom_call_target="tpu_custom_call" | custom-call | tf_op jit(solution)/shard_map/finish/pallas_call | solution.py:974
  423.7 0.2 fusion.8
  423.9 0.0 copy-start.23
  423.9 0.9 copy.36
  424.8 0.1 constant_dynamic-slice_fusion.2
  424.8 0.6 pad_maximum_fusion.3
  425.4 0.8 copy.37
  426.3 0.6 copy_bitcast_fusion.4
  426.9 0.6 copy_bitcast_fusion.2
  427.5 1.1 fusion.1
  428.6 0.6 constant_dynamic-slice_fusion
  429.2 0.6 copy_bitcast_fusion
  429.8 1.0 copy.51
  (26 shorter events, 0.1 us)
Async XLA Ops:
  1.8 1.1 copy-start.2
  2.9 1.0 copy-start.6
  3.9 1.0 copy-start.7
  4.8 0.9 copy-start.10
  5.7 0.7 copy-start.19
  6.4 0.7 copy-start.20
  45.1 2.1 copy-start
  47.2 1.1 copy-start.1
  48.3 0.6 copy-start.4
  49.0 0.7 copy-start.5
  49.7 0.7 copy-start.8
  50.4 0.7 copy-start.9
  328.6 57.6 %copy-start.11 = (f32[8,768]{1,0:T(8,128)S(1)}, f32[8,768]{1,0:T(8,128)}, u32[]{:S(2)}) copy-start(f32[8,768]{1,0:T(8,128)} %get-tuple-element.111.refs_5_) | copy-start | bytes 73732
  328.6 57.6 %copy-start.12 = (f32[8,768]{1,0:T(8,128)S(1)}, f32[8,768]{1,0:T(8,128)}, u32[]{:S(2)}) copy-start(f32[8,768]{1,0:T(8,128)} %get-tuple-element.107.refs_1_) | copy-start | bytes 73732
  328.6 57.6 %copy-start.13 = (f32[4,1,768]{2,1,0:T(1,128)S(1)}, f32[4,1,768]{2,1,0:T(1,128)}, u32[]{:S(2)}) copy-start(f32[4,1,768]{2,1,0:T(1,128)} %get-tuple-element.112.refs_6_) | copy-start | bytes 36868
  328.6 57.6 %copy-start.14 = (f32[4,1,768]{2,1,0:T(1,128)S(1)}, f32[4,1,768]{2,1,0:T(1,128)}, u32[]{:S(2)}) copy-start(f32[4,1,768]{2,1,0:T(1,128)} %get-tuple-element.108.refs_2_) | copy-start | bytes 36868
  328.6 57.6 %copy-start.15 = (f32[4,1,384]{2,1,0:T(1,128)S(1)}, f32[4,1,384]{2,1,0:T(1,128)}, u32[]{:S(2)}) copy-start(f32[4,1,384]{2,1,0:T(1,128)} %get-tuple-element.114.refs_8_) | copy-start | bytes 18436
  328.6 57.6 %copy-start.17 = (f32[4,1,256]{2,1,0:T(1,128)S(1)}, f32[4,1,256]{2,1,0:T(1,128)}, u32[]{:S(2)}) copy-start(f32[4,1,256]{2,1,0:T(1,128)} %get-tuple-element.113.refs_7_) | copy-start | bytes 12292
  386.3 2.3 copy-start.3
  388.6 0.7 copy-start.16
  389.3 0.7 copy-start.18
  390.0 33.7 %copy-start.24 = (f32[96,768]{1,0:T(8,128)S(1)}, f32[96,768]{1,0:T(8,128)}, u32[]{:S(2)}) copy-start(f32[96,768]{1,0:T(8,128)} %get-tuple-element.116) | copy-start | bytes 884740
  423.8 3.6 copy-start.22
  423.9 3.6 copy-start.23
  424.8 5.1 %copy-start.21 = (f32[384,768]{1,0:T(8,128)S(1)}, f32[384,768]{1,0:T(8,128)}, u32[]{:S(2)}) copy-start(f32[384,768]{1,0:T(8,128)} %get-tuple-element.169) | copy-start | bytes 3538948

commit v4 on v3

v4 whole, which is shorter than its diff:
```python
import functools

import jax
import jax.numpy as jnp
from jax import lax
from jax.experimental import pallas as pl
from jax.experimental.pallas import tpu as pltpu
from jax.sharding import PartitionSpec as P

HD = 64
PACK = 512
BLK = 128
PER = PACK // BLK
WIN = 2 * PACK
EPS = 1e-05
NEG = -1e30
MESH = pl.DeviceIdType.MESH
BF = jnp.bfloat16
F32 = jnp.float32
I32 = jnp.int32
HBM = pl.BlockSpec(memory_space=pltpu.MemorySpace.HBM)
VMEM = pl.BlockSpec(memory_space=pltpu.MemorySpace.VMEM)
SMEM = pl.BlockSpec(memory_space=pltpu.MemorySpace.SMEM)
Q_AT, KV_AT = 0, 256


def dot(a, b):
    return jnp.dot(a, b, preferred_element_type=F32)


def dot_nt(a, b):
    return lax.dot_general(a, b, (((1,), (1,)), ((), ())), preferred_element_type=F32)


def dot_tn(a, b):
    return lax.dot_general(a, b, (((0,), (0,)), ((), ())), preferred_element_type=F32)


def whole(shape):
    return pl.BlockSpec(shape, lambda t: (0,) * len(shape))


def per_t(shape, *rest):
    tail = rest if rest else (0,) * (len(shape) - 1)
    return pl.BlockSpec(shape, lambda t: (t,) + tail)


def sds(shape, dtype=F32):
    return jax.ShapeDtypeStruct(shape, dtype)


def column_sum(value):
    return jnp.sum(value, axis=0, keepdims=True)


def flip(value):
    return value.astype(F32).T.astype(BF)


class Place:
    def __init__(self, n_dp, n_tensor):
        self.n_dp, self.n_tensor = n_dp, n_tensor
        self.nz = n_dp // 2
        dp, tensor = lax.axis_index("dp"), lax.axis_index("tensor")
        self.dp, self.tensor = dp, tensor
        self.z, self.y = dp // 2, dp % 2
        self.x, self.c = tensor // 2, tensor % 2
        self.dp_y = 2 * self.z + 1 - self.y
        self.t_x = 2 * (1 - self.x) + self.c
        self.t_c = 2 * self.x + 1 - self.c
        self.t_xc = 2 * (1 - self.x) + 1 - self.c
        self.to_x = (dp, self.t_x)
        self.to_y = (self.dp_y, tensor)
        self.to_c = (dp, self.t_c)

    def d(self, z, same_y=True):
        return 2 * z + (self.y if same_y else 1 - self.y)

    def near(self):
        return [(self.to_x, None), (self.to_y, None), (self.to_c, None)]

    def along_z(self):
        return [((self.dp - 2, self.tensor), self.z > 0), ((self.dp + 2, self.tensor), self.z < self.nz - 1)]

    def far_z(self):
        return [((self.dp ^ (2 << b), self.tensor), None) for b in range(1, bits(self.nz))]

    def beside(self):
        other = self.tensor - 1 + 2 * self.c
        return [((self.dp, other), jnp.logical_and(other >= 0, other < self.n_tensor))]


def meet(peers):
    barrier = pltpu.get_barrier_semaphore()
    count = 0
    for device, valid in peers:
        def signal(device=device):
            pl.semaphore_signal(barrier, inc=1, device_id=device, device_id_type=MESH)
        if valid is None:
            signal()
            count = count + 1
        else:
            pl.when(valid)(signal)
            count = count + valid.astype(I32)
    return lambda: pl.semaphore_wait(barrier, count)


def bits(n):
    return n.bit_length() - 1


def pairs(me):
    found = [(me.dp, me.tensor ^ (1 << b)) for b in range(bits(me.n_tensor))]
    return found + [(me.dp ^ (1 << b), me.tensor) for b in range(bits(me.n_dp))]


def rounds_of(n_dp, n_tensor):
    return bits(n_dp) + bits(n_tensor)


def doubling_sum(me, first, total_ref, part_ref, come_ref, send_sem, recv_sem):
    copies = [
        pltpu.make_async_remote_copy(
            src_ref=part_ref.at[i], dst_ref=come_ref.at[i], send_sem=send_sem.at[i], recv_sem=recv_sem.at[i],
            device_id=device, device_id_type=MESH,
        )
        for i, device in enumerate(pairs(me))
    ]

    def begin():
        first()
        copies[0].start()

    def middle(i):
        copies[i].wait_recv()
        total = part_ref[i] + come_ref[i]
        if i + 1 < len(copies):
            part_ref[i + 1] = total
            copies[i + 1].start()
        else:
            total_ref[...] = total

    def end():
        for copy in copies:
            copy.wait_send()

    return [begin] + [functools.partial(middle, i) for i in range(len(copies))] + [end]


def doubling_scratch(shape, n_dp, n_tensor):
    n = rounds_of(n_dp, n_tensor)
    return [
        pltpu.VMEM((n,) + shape, F32), pltpu.VMEM((n,) + shape, F32),
        pltpu.SemaphoreType.DMA((n,)), pltpu.SemaphoreType.DMA((n,)),
    ]


class Window:
    def __init__(self, me, tokens, rows):
        self.me, self.count, self.rows = me, tokens // BLK, rows

    def first(self, t):
        return jnp.minimum(t * self.count // PER, self.rows - 2)

    def blocks(self):
        t = self.me.tensor
        found = []
        for j in range(self.count):
            g = t * self.count + j
            found.append((g // PER, g // PER - self.first(t), g % PER))
        return found

    def needed(self, source, j, target):
        g = source * self.count + j
        row = g // PER
        inside = jnp.logical_and(row >= target * self.count // PER, row <= (target * self.count + self.count - 1) // PER)
        exists = jnp.logical_and(jnp.logical_and(source >= 0, source < self.me.n_tensor),
                                 jnp.logical_and(target >= 0, target < self.me.n_tensor))
        return jnp.logical_and(inside, exists), g - self.first(target) * PER

    def own_places(self):
        t = self.me.tensor
        return [t * self.count + j - self.first(t) * PER for j in range(self.count)]

    def _each(self, outgoing):
        t = self.me.tensor
        for i, step in enumerate((1, -1)):
            for j in range(self.count):
                source, target = (t, t + step) if outgoing else (t - step, t)
                valid, place = self.needed(source, j, target)
                yield i * self.count + j, j, source, target, valid, pl.multiple_of(place * BLK, BLK)

    def _copy(self, source, target, slot, device, sems):
        return pltpu.make_async_remote_copy(
            src_ref=source, dst_ref=target, send_sem=sems[0].at[slot], recv_sem=sems[1].at[slot],
            device_id=(self.me.dp, device), device_id_type=MESH,
        )

    def send(self, low_ref, win_ref, sems, what="start"):
        for slot, j, source, target, valid, place in self._each(True):
            copy = self._copy(low_ref.at[pl.ds(j * BLK, BLK)], win_ref.at[pl.ds(place, BLK)], slot, target, sems)
            pl.when(valid)(getattr(copy, what))

    def receive(self, win_ref, sems):
        for slot, j, source, target, valid, place in self._each(False):
            here = win_ref.at[pl.ds(place, BLK)]
            pl.when(valid)(pltpu.make_async_copy(here, here, sems[1].at[slot]).wait)

    def send_back(self, grad_ref, back_ref, sems, what="start"):
        for slot, j, source, target, valid, place in self._each(False):
            copy = self._copy(grad_ref.at[pl.ds(place, BLK)], back_ref.at[slot], slot, source, sems)
            pl.when(valid)(getattr(copy, what))

    def receive_back(self, back_ref, sems, add):
        for slot, j, source, target, valid, place in self._each(True):
            def take(slot=slot, j=j):
                pltpu.make_async_copy(back_ref.at[slot], back_ref.at[slot], sems[1].at[slot]).wait()
                add(j, back_ref[slot])
            pl.when(valid)(take)

    def sems(tokens):
        n = 2 * (tokens // BLK)
        return [pltpu.SemaphoreType.DMA((n,)), pltpu.SemaphoreType.DMA((n,))]


class Gather:
    def __init__(self, n_dp):
        self.slots = 12 * (n_dp // 2)

    def scratch(self):
        return [pltpu.SemaphoreType.DMA, pltpu.SemaphoreType.DMA((self.slots,)), pltpu.SemaphoreType.DMA((self.slots,))]

    def rounds(self, me, own_ref, out_ref, own_sem, send_sem, recv_sem):
        nz, cols = me.nz, own_ref.shape[-1]
        sixth = cols // 6 // 128 * 128
        cuts = {0: (0, cols // 2), 1: (cols // 2, cols), 2: (0, sixth), 3: (sixth, 2 * sixth), 4: (2 * sixth, cols)}

        def piece(r, d, part):
            if part is None:
                return out_ref.at[r, d]
            lo, hi = cuts[part]
            return out_ref.at[r, d, :, pl.ds(lo, hi - lo)]

        def copy(source, r, d, part, turn, route, p, device):
            slot = route * nz + p
            return pltpu.make_async_remote_copy(
                src_ref=source if source is not None else piece(r, d, part), dst_ref=piece(r ^ turn, d, part),
                send_sem=send_sem.at[slot], recv_sem=recv_sem.at[slot], device_id=device, device_id_type=MESH,
            )

        def arrived(r, d, part, route, p):
            pltpu.make_async_copy(piece(r, d, part), piece(r, d, part), recv_sem.at[route * nz + p]).wait()

        mine = pltpu.make_async_copy(own_ref, out_ref.at[0, me.dp], own_sem)
        up, down = (me.dp + 2, me.tensor), (me.dp - 2, me.tensor)
        can_up, can_down = me.z < nz - 1, me.z > 0

        def z_copy(p, upward, source=None):
            return copy(source, 0, me.d(p), None, 0, 0 if upward else 1, p, up if upward else down)

        def x_copy(p, source=None):
            return copy(source, 0, me.d(p), None, 2, 2, p, me.to_x)

        def y_copy(p, source=None):
            return copy(source, 0, me.d(p), None, 0, 3, p, me.to_y)

        def first_copy(p, here):
            return copy(None, 2, me.d(p), 0 if here else 2, 0, 4, p, me.to_y)

        def second_copy(p, here):
            return copy(None, 0, me.d(p, False), 1 if here else 3, 2, 5, p, me.to_x)

        def diagonal_z(p, upward):
            return copy(None, 2, me.d(p, False), 4, 0, 6 if upward else 7, p, up if upward else down)

        def core_copy(kind, p, source=None):
            return copy(source, 0 if kind in (0, 2) else 2, me.d(p, kind in (0, 1)), None, 1, 8 + kind, p, me.to_c)

        def own_round():
            mine.start()
            pl.when(can_up)(z_copy(me.z, True, own_ref).start)
            pl.when(can_down)(z_copy(me.z, False, own_ref).start)
            x_copy(me.z, own_ref).start()
            y_copy(me.z, own_ref).start()
            core_copy(0, me.z, own_ref).start()

        def z_round(p, upward, valid):
            @pl.when(valid)
            def _():
                arrived(0, me.d(p), None, 0 if upward else 1, p)
                pl.when(can_up if upward else can_down)(z_copy(p, upward).start)
                x_copy(p).start()
                y_copy(p).start()
                core_copy(0, p).start()

        def xy_round(p, here, valid=None):
            def go():
                arrived(2, me.d(p), None, 2, p)
                first_copy(p, here).start()
                core_copy(1, p).start()
                arrived(0, me.d(p, False), None, 3, p)
                second_copy(p, here).start()
                core_copy(2, p).start()
            go() if valid is None else pl.when(valid)(go)

        def diagonal_here():
            arrived(2, me.d(me.z, False), 0, 4, me.z)
            arrived(2, me.d(me.z, False), 1, 5, me.z)
            pl.when(can_up)(diagonal_z(me.z, True).start)
            pl.when(can_down)(diagonal_z(me.z, False).start)
            core_copy(3, me.z).start()

        def diagonal_round(p, upward, valid):
            @pl.when(valid)
            def _():
                arrived(2, me.d(p, False), 4, 6 if upward else 7, p)
                pl.when(can_up if upward else can_down)(diagonal_z(p, upward).start)
                arrived(2, me.d(p, False), 2, 4, p)
                arrived(2, me.d(p, False), 3, 5, p)
                core_copy(3, p).start()

        def middle(s):
            low, high = me.z - s, me.z + s
            if s < nz:
                z_round(low, True, low >= 0)
                z_round(high, False, high < nz)
            if s == 1:
                xy_round(me.z, True)
            elif s - 1 < nz:
                xy_round(low + 1, False, low + 1 >= 0)
                xy_round(high - 1, False, high - 1 < nz)
            if s == 2:
                diagonal_here()
            elif 2 < s < nz + 2:
                diagonal_round(low + 2, True, low + 2 >= 0)
                diagonal_round(high - 2, False, high - 2 < nz)

        def several(start, stop):
            for s in range(start, stop):
                middle(s)

        def from_core(kinds):
            for p in range(nz):
                for kind in kinds:
                    arrived(1 if kind in (0, 2) else 3, me.d(p, kind in (0, 1)), None, 8 + kind, p)

        def end():
            for p in range(nz):
                here = me.z == p
                pl.when(jnp.logical_and(can_up, p <= me.z))(z_copy(p, True).wait_send)
                pl.when(jnp.logical_and(can_down, p >= me.z))(z_copy(p, False).wait_send)
                x_copy(p).wait_send()
                y_copy(p).wait_send()
                for made in (first_copy, second_copy):
                    pl.when(here)(made(p, True).wait_send)
                    pl.when(jnp.logical_not(here))(made(p, False).wait_send)
                pl.when(jnp.logical_and(can_up, p <= me.z))(diagonal_z(p, True).wait_send)
                pl.when(jnp.logical_and(can_down, p >= me.z))(diagonal_z(p, False).wait_send)
                for kind in range(4):
                    core_copy(kind, p).wait_send()

        third = (nz - 1) // 3
        return {
            "T0": own_round,
            "T1": functools.partial(several, 1, 1 + third),
            "T2": functools.partial(several, 1 + third, 1 + 2 * third),
            "T3": functools.partial(several, 1 + 2 * third, nz),
            "T4": lambda: (mine.wait(), middle(nz)),
            "T5": functools.partial(middle, nz + 1),
            "E1": functools.partial(from_core, (0, 2)),
            "E3": functools.partial(from_core, (1, 3)),
            "E": end,
        }


class Scatter:
    def __init__(self, n_dp, rows, cols, sets):
        self.nz, self.rows, self.cols, self.sets = n_dp // 2, rows, cols, sets

    def buffers(self):
        nz, rows, cols, sets = self.nz, self.rows, self.cols, self.sets
        return [
            pltpu.VMEM((2 * sets, 2 * nz, rows, cols), BF),
            pltpu.VMEM((2 * nz, rows, cols), BF),
            pltpu.VMEM((sets, nz, rows, cols // 2), BF),
            pltpu.VMEM((sets, nz, rows, cols // 2), BF),
            pltpu.VMEM((sets, nz, rows, cols), BF),
            pltpu.VMEM((sets, nz, rows, cols), BF),
            pltpu.VMEM((sets, nz - 1, rows, cols), BF),
            pltpu.VMEM((sets, rows, cols), F32),
        ]

    def block(self, layer, block):
        return 2 * layer + block if self.sets > 1 else block

    def sems(self, layers):
        return [
            pltpu.SemaphoreType.DMA((layers, 5 * self.nz + 2)), pltpu.SemaphoreType.DMA((layers, 5 * self.nz + 2)),
            pltpu.SemaphoreType.DMA((layers,)), pltpu.SemaphoreType.REGULAR,
        ]

    def order(self, me):
        return [lax.rem(me.z + k, me.nz) for k in range(1, me.nz)] + [me.z]

    def peers(self, me):
        return me.near() + [((me.d(z), me.tensor), None) for z in self.order(me)[:-1]]

    def core(self, me, buffers, sems, layer, block):
        sums, stage = buffers[:2]
        slot = 5 * self.nz + block
        return pltpu.make_async_remote_copy(
            src_ref=stage, dst_ref=sums.at[self.block(layer, block)], send_sem=sems[0].at[layer, slot], recv_sem=sems[1].at[layer, slot],
            device_id=me.to_c, device_id_type=MESH,
        )

    def wait_credit(self, me, sems):
        pl.semaphore_wait(sems[3], len(self.peers(me)))

    def rounds(self, me, buffers, sems, layer, out_ref):
        which = layer if self.sets > 1 else 0
        sums, _, *rest = buffers
        sums = sums.at[pl.ds(2 * which, 2)]
        first_in, second_in, x_in, y_in, z_in, total_ref = [item.at[which] for item in rest]
        send_sem, recv_sem, out_sem, credit = sems
        nz = self.nz
        half = self.cols // 2
        zs = self.order(me)

        def remote(source, target, slot, device):
            return pltpu.make_async_remote_copy(
                src_ref=source, dst_ref=target, send_sem=send_sem.at[layer, slot], recv_sem=recv_sem.at[layer, slot],
                device_id=device, device_id_type=MESH,
            )

        def first(k):
            return remote(sums.at[1, me.d(zs[k], False), :, pl.ds(0, half)], first_in.at[k], k, me.to_x)

        def second(k):
            return remote(sums.at[1, me.d(zs[k], False), :, pl.ds(half, half)], second_in.at[k], nz + k, me.to_y)

        def along_x(k):
            return remote(sums.at[1, me.d(zs[k])], x_in.at[k], 2 * nz + k, me.to_x)

        def along_y(k):
            return remote(sums.at[0, me.d(zs[k], False)], y_in.at[k], 3 * nz + k, me.to_y)

        def along_z(k):
            return remote(sums.at[0, me.d(zs[k])], z_in.at[k], 4 * nz + k, (me.d(zs[k]), me.tensor))

        def diagonals():
            for k in range(nz):
                first(k).start()
                second(k).start()

        def x_turn(k):
            second(k).wait_recv()
            d = me.d(zs[k])
            sums[1, d, :, half:] = (sums[1, d, :, half:].astype(F32) + second_in[k].astype(F32)).astype(BF)
            along_x(k).start()

        def y_turn(k):
            first(k).wait_recv()
            d = me.d(zs[k], False)
            sums[0, d, :, :half] = (sums[0, d, :, :half].astype(F32) + first_in[k].astype(F32)).astype(BF)
            along_y(k).start()

        def z_sum(k):
            along_x(k).wait_recv()
            along_y(k).wait_recv()
            return sums[0, me.d(zs[k])].astype(F32) + x_in[k].astype(F32) + y_in[k].astype(F32)

        def z_turn(k):
            sums[0, me.d(zs[k])] = z_sum(k).astype(BF)
            along_z(k).start()

        def last():
            total = z_sum(nz - 1)
            for k in range(nz - 1):
                along_z(k).wait_recv()
                total += z_in[k].astype(F32)
            total_ref[...] = total
            pltpu.make_async_copy(total_ref, out_ref, out_sem.at[layer]).start()

        def end():
            for k in range(nz):
                for made in (first, second, along_x, along_y):
                    made(k).wait_send()
                if k < nz - 1:
                    along_z(k).wait_send()
            pltpu.make_async_copy(total_ref, out_ref, out_sem.at[layer]).wait()

        def give_credit():
            for device, _ in self.peers(me):
                pl.semaphore_signal(credit, inc=1, device_id=device, device_id_type=MESH)

        def several(turn, start, stop):
            for k in range(start, stop):
                turn(k)

        found = {"D": diagonals, "L": last, "E": end}
        if self.sets == 1:
            found["C"] = give_credit
        for name, turn, count, parts in (("X", x_turn, nz, 4), ("Y", y_turn, nz, 4), ("Z", z_turn, nz - 1, 3)):
            for i in range(parts):
                found[name + str(i)] = functools.partial(several, turn, count * i // parts, count * (i + 1) // parts)
        return found


def ends_of(len_ref, row):
    total, ends = 0, []
    for k in range(len_ref.shape[1]):
        total = total + len_ref[row, k]
        ends.append(total)
    return ends


def segments(ends, place):
    seg = jnp.zeros(place.shape, I32)
    for end in ends:
        seg += (place >= end).astype(I32)
    return jnp.where(seg == len(ends), -1, seg)


def allowed_of(len_ref, row, offset, key_axis, heads):
    ends = ends_of(len_ref, row)
    k_shape = (1, PACK) if key_axis == 1 else (PACK, 1)
    q_shape = (BLK, 1) if key_axis == 1 else (1, BLK)
    kseg = segments(ends, lax.broadcasted_iota(I32, k_shape, key_axis))
    qseg = segments(ends, lax.broadcasted_iota(I32, q_shape, 1 - key_axis) + offset)
    allowed = jnp.logical_and(kseg >= 0, jnp.logical_or(kseg == qseg, qseg < 0))
    return jnp.concatenate([allowed] * heads, axis=1 - key_axis)


def lane_masks(first, count):
    slot = lax.broadcasted_iota(jnp.int32, (1, 256), 1) // HD
    return [(slot == first + i).astype(F32).astype(BF) for i in range(count)]


def stack_heads(block, masks):
    return jnp.concatenate([block * mask for mask in masks], axis=0)


def pick_heads(stacked, masks, size):
    total = None
    for i, mask in enumerate(masks):
        part = stacked[i * size : (i + 1) * size] * mask.astype(F32)
        total = part if total is None else total + part
    return total


def norm_forward(value, gain, shift):
    average = jnp.mean(value, axis=-1, keepdims=True)
    centered = value - average
    variance = jnp.mean(centered * centered, axis=-1, keepdims=True)
    scaled = lax.rsqrt(variance + EPS)
    unit = centered * scaled
    return unit * gain + shift, unit, scaled


def norm_back(grad, unit, scaled, gain):
    inner = grad * gain
    centered = inner - jnp.mean(inner, axis=-1, keepdims=True)
    return scaled * (centered - unit * jnp.mean(inner * unit, axis=-1, keepdims=True))


PLAN = [
    [
        "A0T0", "B0T0", "F0T0", "A0T1", "B0T1", "A0T2", "B0T2", "A1T0", "A0T3", "B0T3", "F0T1",
        "W0", "A0T4", "B0T4", "A0E1", "B0E1", "F0T2", "A1T1", "R0", "A0T5", "B0T5",
    ],
    ["F0T3"],
    ["A0E3", "B0E3", "F1T0"],
    ["F0T4", "A1T2"],
    ["F0E1", "F1T1"],
    ["F0T5"],
    [],
    ["A1T3", "F0E3"],
    ["A1T4", "F1T2", "A1E1", "R1"],
    ["A1T5"],
    ["A1E3", "F1T3"],
    [],
    ["F1T4"],
    ["F1E1"],
    ["F1T5"],
    ["F1E3"],
]


def forward_kernel(
    n_dp, n_tensor, len_ref, qkv_ref, ow_ref, up_ref, down_ref, qvb_ref, ub_ref, own_ref,
    ob_ref, gain1_ref, shift1_ref, db_ref, gain2_ref, shift2_ref,
    q_ref, kv_ref, ctx_ref, act_ref, slope_ref, mid_ref, unit1_ref, rs1_ref, unit2_ref, rs2_ref, out_ref,
    win_out_ref, ga_ref, gf_ref,
    gb_ref, a_ref, f_ref, b_ref, wa_ref, wf_ref, wb_ref, h_ref, acc_ref, low_ref, win_ref, bias_ref,
    wa_sem, wf_sem, wb_sem, win_sem, win_send, win_recv, *gather_sems,
):
    me = Place(n_dp, n_tensor)
    step, n = pl.program_id(0), n_tensor
    layers = qkv_ref.shape[0]
    tokens, dim = own_ref.shape
    rows = len_ref.shape[0]
    heads = 3
    layer, phase, r = step // (2 * n), step // n % 2, step % n
    vec = pl.ds(layer, 1)
    window = Window(me, tokens, rows)
    own_rows = pl.ds(pl.multiple_of(window.own_places()[0] * BLK, BLK), tokens)
    gather = Gather(n_dp)
    waves = {}
    for i, name in enumerate(("A0", "F0", "A1", "F1")):
        own, out = ((a_ref, ga_ref), (f_ref, gf_ref))[i % 2]
        for key, turn in gather.rounds(me, own.at[i // 2], out.at[i // 2], *gather_sems[3 * i : 3 * i + 3]).items():
            waves[name + key] = turn
    for key, turn in gather.rounds(me, b_ref, gb_ref, *gather_sems[12:15]).items():
        waves["B0" + key] = turn

    def window_sems(l):
        return win_send.at[l], win_recv.at[l]

    def pack_a(l):
        units = qkv_ref.shape[3]
        a_ref[l, :, 0:units] = qkv_ref[l, 0]
        a_ref[l, :, units : 2 * units] = flip(ow_ref[l])
        a_ref[l, :, 2 * units : 3 * units] = qkv_ref[l, 1]
        a_ref[l, :, 3 * units : 4 * units] = qkv_ref[l, 2]

    def pack_f(l):
        units = up_ref.shape[2]
        f_ref[l, :, 0:units] = up_ref[l]
        f_ref[l, :, units : 2 * units] = down_ref[l]

    def pack_b():
        piece, wide = qvb_ref.shape[2], ub_ref.shape[1]
        units = qkv_ref.shape[3]

        def spread(values, start):
            size = values.shape[1]
            source = lax.broadcasted_iota(I32, (size, dim), 0)
            target = lax.broadcasted_iota(I32, (size, dim), 1)
            return dot(values, (target == source + start).astype(F32).astype(BF))

        u = spread(ub_ref[...], me.dp * wide)
        place = lax.broadcasted_iota(I32, b_ref.shape, 0)
        total = jnp.zeros(b_ref.shape, F32)
        for l in range(layers):
            row = spread(qvb_ref[l], Q_AT + me.dp * piece)[0:1]
            row += spread(qvb_ref[l], KV_AT + units + me.dp * piece)[1:2]
            total += jnp.where(place == 2 * l, row, 0.0) + jnp.where(place == 2 * l + 1, u[l : l + 1], 0.0)
        b_ref[...] = total.astype(BF)

    def hand_on(l):
        window.send(low_ref, win_ref.at[l], window_sems(l))
        for j, place in enumerate(window.own_places()):
            win_ref[l, pl.ds(pl.multiple_of(place * BLK, BLK), BLK), :] = low_ref[pl.ds(j * BLK, BLK), :]

    def take_on(l):
        window.receive(win_ref.at[l], window_sems(l))
        window.send(low_ref, win_ref.at[l], window_sems(l), "wait_send")
        pltpu.make_async_copy(win_ref.at[l], win_out_ref.at[l], win_sem.at[l]).start()

    waves["R1"] = lambda: take_on(1)
    waves["W0"] = lambda: hand_on(0)
    waves["R0"] = lambda: take_on(0)

    def load(s):
        l, p, i = s // (2 * n), s // n % 2, s % n
        if p == 1:
            return [pltpu.make_async_copy(gf_ref.at[l, i], wf_ref.at[i % 2], wf_sem.at[i % 2])]
        copies = [pltpu.make_async_copy(ga_ref.at[l, i], wa_ref.at[i % 2], wa_sem.at[i % 2])]
        if l == 0:
            copies.append(pltpu.make_async_copy(gb_ref.at[i], wb_ref.at[i % 2], wb_sem.at[i % 2]))
        return copies

    def here(s):
        l, p, i = s // (2 * n), s // n % 2, s % n
        name = "AF"[p] + str(l) + ("T4", "E1", "T5", "E3")[i]
        return [k for k, names in enumerate(PLAN) if name in names][0]

    for s, names in enumerate(PLAN):
        @pl.when(step == s)
        def _(s=s, names=names):
            if s == 0:
                win_ref[...] = jnp.zeros(win_ref.shape, BF)
                met = meet(me.near() + me.along_z() + me.beside())
                for l in range(layers):
                    pack_a(l)
                    pack_f(l)
                pack_b()
                low_ref[...] = own_ref[...]
                h_ref[...] = own_ref[...].astype(F32)
                met()
            for name in names:
                waves[name]()
            begun = [k for k in (s, s + 1) if k < len(PLAN) and max(here(k), k - 1) == s]
            for k in begun:
                for copy in load(k):
                    copy.start()
            for copy in load(s):
                copy.wait()

    @pl.when(phase == 0)
    def _():
        slot = r % 2

        @pl.when(layer == 0)
        def _():
            bias_ref[r] = jnp.sum(wb_ref[slot].astype(F32), axis=0)

        def weights(lo, hi):
            return wa_ref[slot, :, :, lo:hi].reshape(dim, hi - lo)

        kv_ref[0, 0] = (dot(win_ref[layer], weights(384, 768)) + bias_ref[r, pl.ds(2 * layer, 1), KV_AT : KV_AT + 384]).astype(BF)
        q_ref[0, 0] = (dot(win_ref[layer, own_rows, :], weights(0, 256)) + bias_ref[r, pl.ds(2 * layer, 1), Q_AT : Q_AT + 256]).astype(BF)
        q_masks, c_masks = lane_masks(0, heads), lane_masks(1, heads)
        for j, (row, place, part) in enumerate(window.blocks()):
            here = pl.ds(j * BLK, BLK)
            keys = pl.ds(pl.multiple_of(place * PACK, PACK), PACK)
            stacked = stack_heads(q_ref[0, 0, here, :], q_masks)
            scores = dot_nt(stacked, kv_ref[0, 0, keys, 0:256]) * (HD**-0.5)
            scores = jnp.where(allowed_of(len_ref, row, part * BLK, 1, heads), scores, NEG)
            peak = jnp.max(scores, axis=-1, keepdims=True)
            exps = jnp.exp(scores - peak)
            probs = exps * (1.0 / jnp.sum(exps, axis=-1, keepdims=True))
            out = dot(probs.astype(BF), kv_ref[0, 0, keys, 128:384])
            ctx_ref[0, 0, here, :] = pick_heads(out, c_masks, BLK).astype(BF)
        part = dot_nt(ctx_ref[0, 0], weights(128, 384))

        @pl.when(r == 0)
        def _():
            acc_ref[...] = part

        @pl.when(r > 0)
        def _():
            acc_ref[...] += part

        @pl.when(r == n - 1)
        def _():
            total = h_ref[...] + acc_ref[...] + ob_ref[vec, :]
            h_ref[...], unit, rs1_ref[0] = norm_forward(total, gain1_ref[vec, :], shift1_ref[vec, :])
            unit1_ref[0] = unit.astype(BF)
            low_ref[...] = h_ref[...].astype(BF)
            mid_ref[0] = low_ref[...]

    @pl.when(phase == 1)
    def _():
        slot = r % 2

        def weights(lo, hi):
            return wf_ref[slot, :, :, lo:hi].reshape(dim, hi - lo)

        upper = dot(low_ref[...], weights(0, dim)) + bias_ref[r, pl.ds(2 * layer + 1, 1), :]
        half = 0.5 + 0.5 * lax.erf(upper * (0.5**0.5))
        act_ref[0, 0] = (upper * half).astype(BF)
        slope_ref[0, 0] = (half + upper * (jnp.exp(-0.5 * upper * upper) * 0.3989422804014327)).astype(BF)
        part = dot_nt(act_ref[0, 0], weights(dim, 2 * dim))

        @pl.when(r == 0)
        def _():
            acc_ref[...] = part

        @pl.when(r > 0)
        def _():
            acc_ref[...] += part

        @pl.when(r == n - 1)
        def _():
            total = h_ref[...] + acc_ref[...] + db_ref[vec, :]
            out, unit, rs2_ref[0] = norm_forward(total, gain2_ref[vec, :], shift2_ref[vec, :])
            unit2_ref[0] = unit.astype(BF)
            h_ref[...] = out

    @pl.when(step == 2 * n - 1)
    def _():
        low_ref[...] = h_ref[...].astype(BF)
        hand_on(1)

    @pl.when(step == pl.num_programs(0) - 1)
    def _():
        out_ref[...] = h_ref[...]
        for name in ("A0", "B0", "F0", "A1", "F1"):
            waves[name + "E"]()
        for l in range(layers):
            pltpu.make_async_copy(win_ref.at[l], win_out_ref.at[l], win_sem.at[l]).wait()


def forward(lens, qkv, ow, up, down, qvb, ub, own, vecs, n_dp, n_tensor):
    layers, _, shard, units = qkv.shape
    (tokens, dim), n = own.shape, n_tensor
    hidden = up.shape[2]
    a_cols, f_cols = 4 * units, 2 * hidden
    biases = (16, dim)
    gather = Gather(n_dp)
    blocks = 2 * (tokens // BLK)

    def in_attn(shape):
        def at(s):
            i = s // (2 * n) * n + jnp.where(s // n % 2 == 0, s % n, n - 1)
            return (i // n, i % n, 0, 0)
        return pl.BlockSpec((1, 1) + shape, at)

    def in_ffn(shape):
        def at(s):
            i = jnp.maximum(s // (2 * n) * n + jnp.where(s // n % 2 == 1, s % n, -1), 0)
            return (i // n, i % n, 0, 0)
        return pl.BlockSpec((1, 1) + shape, at)

    def per_layer(shape):
        return pl.BlockSpec((1,) + shape, lambda s: (s // (2 * n), 0, 0))

    operands = [lens, qkv, ow, up, down, qvb, ub, own] + vecs
    return pl.pallas_call(
        functools.partial(forward_kernel, n_dp, n_tensor),
        grid=(2 * n * layers,),
        in_specs=[SMEM] + [whole(item.shape) for item in operands[1:]],
        out_specs=[
            in_attn((tokens, 256)), in_attn((WIN, 384)), in_attn((tokens, 256)), in_ffn((tokens, hidden)), in_ffn((tokens, hidden)),
            per_layer((tokens, dim)), per_layer((tokens, dim)), per_layer((tokens, 1)), per_layer((tokens, dim)), per_layer((tokens, 1)),
            whole((tokens, dim)), HBM, HBM, HBM, HBM,
        ],
        out_shape=[
            sds((layers, n, tokens, 256), BF), sds((layers, n, WIN, 384), BF), sds((layers, n, tokens, 256), BF),
            sds((layers, n, tokens, hidden), BF), sds((layers, n, tokens, hidden), BF),
            sds((layers, tokens, dim), BF), sds((layers, tokens, dim), BF), sds((layers, tokens, 1)),
            sds((layers, tokens, dim), BF), sds((layers, tokens, 1)), sds((tokens, dim)), sds((layers, WIN, dim), BF),
            sds((layers, n, n_dp, shard, a_cols), BF), sds((layers, n, n_dp, shard, f_cols), BF),
            sds((n, n_dp) + biases, BF),
        ],
        scratch_shapes=[
            pltpu.VMEM((layers, shard, a_cols), BF), pltpu.VMEM((layers, shard, f_cols), BF), pltpu.VMEM(biases, BF),
            pltpu.VMEM((2, n_dp, shard, a_cols), BF), pltpu.VMEM((2, n_dp, shard, f_cols), BF), pltpu.VMEM((2, n_dp) + biases, BF),
            pltpu.VMEM((tokens, dim), F32), pltpu.VMEM((tokens, dim), F32), pltpu.VMEM((tokens, dim), BF),
            pltpu.VMEM((layers, WIN, dim), BF), pltpu.VMEM((n,) + biases, F32),
        ]
        + [pltpu.SemaphoreType.DMA((2,))] * 3 + [pltpu.SemaphoreType.DMA((layers,))]
        + [pltpu.SemaphoreType.DMA((layers, blocks))] * 2
        + gather.scratch() * 5,
        compiler_params=pltpu.CompilerParams(vmem_limit_bytes=60 * 1024 * 1024, collective_id=0, has_side_effects=True),
        name="forward",
    )(*operands)


PLAN_BACK = [
    [],
    [],
    ["F1D"],
    [],
    ["F1X0", "F1Y0"],
    ["F1Y1", "F1X1", "F1X2"],
    ["A1D"],
    ["F1Z0"],
    ["A1Y0", "A1Y1", "A1Y2", "A1X0", "A1X1", "F1Z1", "A1Y3", "A1X2", "R1", "F1Y2"],
    ["A1Z0", "A1X3", "A1Z1"],
    ["F0D", "A1Z2"],
    [],
    [
        "A1L", "F0Y0", "F0Y1", "S0", "F0X0", "F1Z2", "F0X1", "A1E", "A1C", "F0Y2", "S1",
        "F0X2",
    ],
    ["F0Z0"],
    ["F0Z1", "A0D"],
    ["S2", "A0X0"],
]
LAST_BACK = [
    "S3", "A0Y0", "Q0", "A0Y1", "A0X1", "F0Z2", "R0", "Q1", "A0Y2", "A0Y3", "A0Z0",
    "A0X2", "Q2", "F0X3", "A0Z1", "A0X3", "F0Y3", "Q3", "A0Z2", "F1X3", "F1Y3", "S4",
    "F0L", "Q4", "A0L", "F1L", "Q5", "S5",
]


def backward_kernel(
    n_dp, n_tensor, len_ref, grad_in_ref, up_ref, down_ref, g_ref, act_ref, slope_ref, q_ref, kv_ref, ctx_ref,
    mid_ref, unit1_ref, rs1_ref, unit2_ref, rs2_ref, win_ref, gain1_ref, gain2_ref,
    grad_out_ref, sum_f_ref, sum_a_ref, few_ref,
    grad_ref, acc_ref, low_ref, low_t_ref, own_t_ref, win_t_ref, dctx_ref, dq_ref, dkv_ref, win_grad_ref, win_low_ref, back_ref,
    part_ref, come_ref, few_send, few_recv, late_part_ref, late_come_ref, late_send, late_recv, early_ref, late_ref, rows_ref,
    back_send, back_recv, grad_sem, win_sem, *scratch,
):
    me = Place(n_dp, n_tensor)
    step, n = pl.program_id(0), n_tensor
    layers = few_ref.shape[0] // 16
    tokens, dim = grad_ref.shape
    rows = len_ref.shape[0]
    heads = 3
    layer, phase, r = layers - 1 - step // (2 * n), step // n % 2, n - 1 - step % n
    line, at = pl.ds(layer, 1), layer * 16
    mine = me.tensor ^ r
    window = Window(me, tokens, rows)
    own_rows = pl.ds(pl.multiple_of(window.own_places()[0] * BLK, BLK), tokens)
    shard = dim // n_dp
    kinds = {"F": Scatter(n_dp, shard, 2 * dim, layers), "A": Scatter(n_dp, shard, dim, 1)}
    buffers = {"F": scratch[0:8], "A": scratch[8:16]}
    sems = {"F": scratch[16:20], "A": scratch[20:24]}
    outs = {"F": sum_f_ref, "A": sum_a_ref}
    turns = {}
    for l in range(layers):
        for kind in kinds:
            made = kinds[kind].rounds(me, buffers[kind], sems[kind], l, outs[kind].at[l])
            for key, turn in made.items():
                turns[kind + str(l) + key] = turn

    def back_sems(l):
        return back_send.at[l], back_recv.at[l]

    def add_back(j, value):
        grad_ref[pl.ds(j * BLK, BLK), :] += value.astype(F32)

    def take_back(l):
        window.receive_back(back_ref.at[l], back_sems(l), add_back)
        window.send_back(win_low_ref, back_ref.at[l], back_sems(l), "wait_send")

    turns["R1"] = lambda: take_back(1)
    turns["R0"] = lambda: take_back(0)
    def early_sums():
        part_ref[0] = rows_ref[...]

    early = doubling_sum(me, early_sums, early_ref, part_ref, come_ref, few_send, few_recv)
    for i in range(6):
        turns["S" + str(i)] = early[i]
    turns["S6"] = lambda: [turn() for turn in early[6:]]

    def last_sums():
        late_part_ref[0] = jnp.zeros(late_part_ref.shape[1:], F32)
        for t in range(n):
            late_part_ref[0, t : t + 1, :] = rows_ref[12 + t : 13 + t, :]

    late = doubling_sum(me, last_sums, late_ref, late_part_ref, late_come_ref, late_send, late_recv)
    for i in range(6):
        turns["Q" + str(i)] = late[i]
    turns["Q6"] = lambda: [turn() for turn in late[6:]]

    @pl.when(step == 0)
    def _():
        load = pltpu.make_async_copy(grad_in_ref, grad_ref, grad_sem)
        load.start()
        met = meet(kinds["F"].peers(me) + me.beside())
        rows_ref[...] = jnp.zeros(rows_ref.shape, F32)
        load.wait()
        met()

    for i, names in enumerate(PLAN_BACK):
        if names:
            @pl.when(step == i)
            def _(names=names):
                for name in names:
                    turns[name]()

    def open_block(kind):
        scatter = kinds[kind]

        def core(l, block):
            return scatter.core(me, buffers[kind], sems[kind], l, block)

        @pl.when(r % 2 == 0)
        def _():
            core(layer, r // 2).wait_recv()

        @pl.when(r == 1)
        def _():
            core(layer, 1).wait_send()

        @pl.when(jnp.logical_and(r == 3, layer == 0))
        def _():
            core(1, 0).wait_send()

    def put(kind, lo, value):
        sums, stage = buffers[kind][:2]
        width = value.shape[1]
        value = value.reshape(n_dp, shard, width)

        @pl.when(r % 2 == 1)
        def _():
            stage[:, :, lo : lo + width] = value.astype(BF)

        @pl.when(r % 2 == 0)
        def _():
            block = kinds[kind].block(layer, r // 2)
            sums[block, :, :, lo : lo + width] = (sums[block, :, :, lo : lo + width].astype(F32) + value).astype(BF)

    def close_block(kind):
        scatter = kinds[kind]

        if scatter.sets == 1:
            @pl.when(jnp.logical_and(r == 3, layer == 0))
            def _():
                scatter.wait_credit(me, sems[kind])

        @pl.when(r % 2 == 1)
        def _():
            scatter.core(me, buffers[kind], sems[kind], layer, r // 2).start()

    @pl.when(phase == 0)
    def _():
        @pl.when(r == n - 1)
        def _():
            grad, unit = grad_ref[...], unit2_ref[0].astype(F32)
            dsecond = norm_back(grad, unit, rs2_ref[0], gain2_ref[line, :])
            rows_ref[pl.ds(at + 4, 1), :] = column_sum(grad * unit)
            rows_ref[pl.ds(at + 5, 1), :] = column_sum(grad)
            rows_ref[pl.ds(at + 3, 1), :] = column_sum(dsecond)
            acc_ref[...] = dsecond
            low_ref[...] = dsecond.astype(BF)
            low_t_ref[...] = dsecond.T.astype(BF)
            own_t_ref[...] = flip(mid_ref[0])

        @pl.when(r == 1)
        def _():
            pltpu.make_async_copy(win_ref.at[layer], win_low_ref, win_sem).start()

        dupper = dot(low_ref[...], down_ref[0, 0]) * slope_ref[0, 0].astype(F32)
        rows_ref[pl.ds(at + 8 + mine, 1), :] = column_sum(dupper)
        dupper_low = dupper.astype(BF)
        acc_ref[...] += dot_nt(dupper_low, up_ref[0, 0])
        open_block("F")
        put("F", 0, dot(own_t_ref[...], dupper_low))
        put("F", dim, dot(low_t_ref[...], act_ref[0, 0]))
        close_block("F")

        @pl.when(r == 0)
        def _():
            dmid, unit = acc_ref[...], unit1_ref[0].astype(F32)
            dfirst = norm_back(dmid, unit, rs1_ref[0], gain1_ref[line, :])
            rows_ref[pl.ds(at + 1, 1), :] = column_sum(dmid * unit)
            rows_ref[pl.ds(at + 2, 1), :] = column_sum(dmid)
            rows_ref[pl.ds(at, 1), :] = column_sum(dfirst)
            grad_ref[...] = dfirst
            low_ref[...] = dfirst.astype(BF)
            low_t_ref[...] = dfirst.T.astype(BF)

    @pl.when(phase == 1)
    def _():
        @pl.when(r == n - 1)
        def _():
            pltpu.make_async_copy(win_ref.at[layer], win_low_ref, win_sem).wait()
            own_t_ref[...] = flip(win_low_ref[own_rows, :])
            win_t_ref[...] = flip(win_low_ref[...])
            win_grad_ref[...] = jnp.zeros(win_grad_ref.shape, F32)

        dctx_ref[...] = dot(low_ref[...], g_ref[0, 0, :, 128:384]).astype(BF)
        dkv_ref[...] = jnp.zeros(dkv_ref.shape, F32)
        q_masks, c_masks = lane_masks(0, heads), lane_masks(1, heads)
        for j, (row, slot, part) in enumerate(window.blocks()):
            here = pl.ds(j * BLK, BLK)
            keys = pl.ds(pl.multiple_of(slot * PACK, PACK), PACK)
            q_stack = stack_heads(q_ref[0, 0, here, :], q_masks)
            d_stack = stack_heads(dctx_ref[here, :], c_masks)
            scores = dot_nt(kv_ref[0, 0, keys, 0:256], q_stack) * (HD**-0.5)
            scores = jnp.where(allowed_of(len_ref, row, part * BLK, 0, heads), scores, NEG)
            peak = jnp.max(scores, axis=0, keepdims=True)
            exps = jnp.exp(scores - peak)
            probs = exps * (1.0 / jnp.sum(exps, axis=0, keepdims=True))
            dprobs = dot_nt(kv_ref[0, 0, keys, 128:384], d_stack)
            weighted = probs * dprobs
            inner = jnp.sum(weighted, axis=0, keepdims=True)
            dscores = ((weighted - probs * inner) * (HD**-0.5)).astype(BF)
            dkv_ref[keys, 128:384] += dot(probs.astype(BF), d_stack)
            dkv_ref[keys, 0:256] += dot(dscores, q_stack)
            dq_ref[here, :] = pick_heads(dot_tn(dscores, kv_ref[0, 0, keys, 0:256]), q_masks, BLK)
        dq, dkv = dq_ref[...], dkv_ref[...]
        rows_ref[pl.ds(at + 12 + mine, 1), 0:256] = column_sum(dq)
        rows_ref[pl.ds(at + 12 + mine, 1), 256:640] = column_sum(dkv)
        dq_low, dkv_low = dq.astype(BF), dkv.astype(BF)
        grad_ref[...] += dot_nt(dq_low, g_ref[0, 0, :, 0:256])
        win_grad_ref[...] += dot_nt(dkv_low, g_ref[0, 0, :, 384:768])
        grad_q = dot(own_t_ref[...], dq_low)
        grad_o = dot(low_t_ref[...], ctx_ref[0, 0])
        open_block("A")
        put("A", 0, grad_q[:, 0:128])
        put("A", 128, grad_q[:, 128:256] + grad_o[:, 0:128])
        put("A", 256, grad_o[:, 128:256])
        put("A", 384, dot(win_t_ref[...], dkv_low))
        close_block("A")

        @pl.when(r == 0)
        def _():
            win_low_ref[...] = win_grad_ref[...].astype(BF)
            for l in range(layers):
                @pl.when(layer == l)
                def _(l=l):
                    window.send_back(win_low_ref, back_ref.at[l], back_sems(l))
            for j, place in enumerate(window.own_places()):
                grad_ref[pl.ds(j * BLK, BLK), :] += win_grad_ref[pl.ds(pl.multiple_of(place * BLK, BLK), BLK), :]

    @pl.when(step == pl.num_programs(0) - 1)
    def _():
        for name in LAST_BACK:
            turns[name]()
        for name in ("S6", "Q6", "F1E", "F0E", "A0E"):
            turns[name]()
        few_ref[...] = early_ref[...]
        few_ref[12 : 12 + n, :] = late_ref[0:n, :]
        store = pltpu.make_async_copy(grad_ref, grad_out_ref, grad_sem)
        store.start()
        for kind in kinds:
            kinds[kind].core(me, buffers[kind], sems[kind], 0, 0).wait_send()
        store.wait()


def backward(lens, grad, ga, gf, saved, gains, n_dp, n_tensor):
    q, kv, ctx, act, slope, mid, unit1, rs1, unit2, rs2, win = saved
    layers, n, (tokens, dim) = mid.shape[0], n_tensor, grad.shape
    shard = dim // n_dp
    blocks = 2 * (tokens // BLK)
    few = (16 * layers, dim)
    wide, narrow = Scatter(n_dp, shard, 2 * dim, layers), Scatter(n_dp, shard, dim, 1)

    def in_phase(phase, shape, *tail):
        held = 0 if phase == 0 else n - 1

        def at(s):
            r = jnp.where(s // n % 2 == phase, n - 1 - s % n, held)
            return (layers - 1 - s // (2 * n), r) + (tail if tail else (0, 0))
        return pl.BlockSpec((1, 1) + shape, at)

    def per_layer(shape):
        return pl.BlockSpec((1,) + shape, lambda s: (layers - 1 - s // (2 * n), 0, 0))

    doubling = doubling_scratch(few, n_dp, n_tensor) + doubling_scratch((8, dim), n_dp, n_tensor)
    doubling += [pltpu.VMEM(few, F32), pltpu.VMEM((8, dim), F32), pltpu.VMEM(few, F32)]
    return pl.pallas_call(
        functools.partial(backward_kernel, n_dp, n_tensor),
        grid=(2 * n * layers,),
        in_specs=[
            SMEM, HBM, in_phase(0, (dim, dim), 0, 0), in_phase(0, (dim, dim), 0, 1), in_phase(1, (dim, dim)),
            in_phase(0, (tokens, dim)), in_phase(0, (tokens, dim)),
            in_phase(1, (tokens, 256)), in_phase(1, (WIN, 384)), in_phase(1, (tokens, 256)),
            per_layer((tokens, dim)), per_layer((tokens, dim)), per_layer((tokens, 1)), per_layer((tokens, dim)), per_layer((tokens, 1)),
            HBM, whole(gains[0].shape), whole(gains[1].shape),
        ],
        out_specs=[HBM, HBM, HBM, whole(few)],
        out_shape=[sds((tokens, dim)), sds((layers, shard, 2 * dim)), sds((layers, shard, dim)), sds(few)],
        scratch_shapes=[
            pltpu.VMEM((tokens, dim), F32), pltpu.VMEM((tokens, dim), F32), pltpu.VMEM((tokens, dim), BF),
            pltpu.VMEM((dim, tokens), BF), pltpu.VMEM((dim, tokens), BF), pltpu.VMEM((dim, WIN), BF),
            pltpu.VMEM((tokens, 256), BF), pltpu.VMEM((tokens, 256), F32), pltpu.VMEM((WIN, 384), F32),
            pltpu.VMEM((WIN, dim), F32), pltpu.VMEM((WIN, dim), BF), pltpu.VMEM((layers, blocks, BLK, dim), BF),
        ]
        + doubling
        + [pltpu.SemaphoreType.DMA((layers, blocks)), pltpu.SemaphoreType.DMA((layers, blocks))] + [pltpu.SemaphoreType.DMA] * 2
        + wide.buffers() + narrow.buffers() + wide.sems(layers) + narrow.sems(layers),
        compiler_params=pltpu.CompilerParams(vmem_limit_bytes=67043328, collective_id=1, has_side_effects=True),
        name="backward",
    )(lens, grad, gf, gf, ga, act, slope, q, kv, ctx, mid, unit1, rs1, unit2, rs2, win, *gains)


def lay_out_kernel(
    n_dp, n_tensor, few_in, wf_in, wa_in, h_in, grad_in,
    h_out, grad_out, qkv_out, qv_out, ow_out, ob_out, gain1_out, shift1_out, up_out, ub_out, down_out, db_out, gain2_out, shift2_out,
    few_ref, wf_ref, wa_ref, sem,
):
    me = Place(n_dp, n_tensor)
    loads = [
        pltpu.make_async_copy(source, target, sem.at[i])
        for i, (source, target) in enumerate(
            ((wf_in, wf_ref), (wa_in, wa_ref), (few_in, few_ref), (h_in, h_out), (grad_in, grad_out))
        )
    ]
    for load in loads:
        load.start()
    for load in loads[:3]:
        load.wait()
    layers, units = qkv_out.shape[0], qkv_out.shape[3]
    dim, hidden = few_ref.shape[1], up_out.shape[2]
    wide, piece = ub_out.shape[1], qv_out.shape[2]
    def cut(row, start, size):
        return pltpu.roll(few_ref[pl.ds(row, 1), :], lax.rem(2 * dim - start, dim), 1)[:, 0:size]

    for l in range(layers):
        at = 16 * l
        for i, column in enumerate((0, 2, 3)):
            qkv_out[l, i] = wa_ref[l, :, column * units : (column + 1) * units]
        ow_out[l] = wa_ref[l, :, units : 2 * units].T
        up_out[l] = wf_ref[l, :, 0:hidden]
        down_out[l] = wf_ref[l, :, hidden : 2 * hidden]
        for k, out in enumerate((ob_out, gain1_out, shift1_out, db_out, gain2_out, shift2_out)):
            out[l : l + 1, :] = few_ref[at + k : at + k + 1, :]
        ub_out[l : l + 1, :] = cut(at + 8 + me.tensor, me.dp * wide, wide)
        qv_out[l, 0:1, :] = cut(at + 12 + me.tensor, Q_AT + me.dp * piece, piece)
        qv_out[l, 1:2, :] = cut(at + 12 + me.tensor, KV_AT + units + me.dp * piece, piece)
    for load in loads[3:]:
        load.wait()


def lay_out(few, wf, wa, h, grad, shapes, n_dp, n_tensor):
    return pl.pallas_call(
        functools.partial(lay_out_kernel, n_dp, n_tensor),
        in_specs=[HBM] * 5,
        out_specs=[VMEM] * len(shapes),
        out_shape=[sds(shape) for shape in shapes],
        scratch_shapes=[pltpu.VMEM(item.shape, F32) for item in (few, wf, wa)] + [pltpu.SemaphoreType.DMA((5,))],
        compiler_params=pltpu.CompilerParams(vmem_limit_bytes=67043328),
        name="lay_out",
    )(few, wf, wa, h, grad)


def body(n_dp, n_tensor, block_input, passage_lengths, qkv_weight, qv_bias, out_weight, out_bias, first_gain,
         first_shift, up_weight, up_bias, down_weight, down_bias, second_gain, second_shift, output_grad):
    layers = qkv_weight.shape[0]
    tokens, dim = block_input.shape
    rows = passage_lengths.shape[0]
    shard = qkv_weight.shape[2]
    lens = passage_lengths

    vecs = [out_bias, first_gain, first_shift, down_bias, second_gain, second_shift]
    q, kv, ctx, act, slope, mid, unit1, rs1, unit2, rs2, block_output, win, ga, gf, _ = forward(
        lens, qkv_weight, out_weight, up_weight, down_weight.transpose(0, 2, 1), qv_bias, up_bias, block_input, vecs, n_dp, n_tensor
    )
    ga, gf = (g.reshape(layers, n_tensor, n_dp * shard, g.shape[-1]) for g in (ga, gf))

    saved = (q, kv, ctx, act, slope, mid, unit1, rs1, unit2, rs2, win)
    grad, wf, wa, totals = backward(lens, output_grad, ga, gf, saved, [first_gain, second_gain], n_dp, n_tensor)

    shapes = [(tokens, dim)] * 2 + [
        item.shape
        for item in (qkv_weight, qv_bias, out_weight, out_bias, first_gain, first_shift,
                     up_weight, up_bias, down_weight, down_bias, second_gain, second_shift)
    ]
    down_at = 10
    layer, units, columns = shapes[down_at]
    shapes[down_at] = (layer, columns, units)
    results = list(lay_out(totals, wf, wa, block_output, grad, shapes, n_dp, n_tensor))
    results[down_at] = results[down_at].transpose(0, 2, 1)
    return tuple(results)


def solution(mesh):
    n_dp, n_tensor = mesh.shape["dp"], mesh.shape["tensor"]
    tokens = P(("dp", "tensor"), None)
    in_specs = (
        tokens, P("dp", None), P(None, None, "dp", "tensor"), P(None, None, ("tensor", "dp")), P(None, "tensor", "dp"),
        P(), P(), P(), P(None, "dp", "tensor"), P(None, ("tensor", "dp")), P(None, "tensor", "dp"), P(), P(), P(), tokens,
    )
    out_specs = (
        tokens, tokens, P(None, None, "dp", "tensor"), P(None, None, ("tensor", "dp")), P(None, "tensor", "dp"),
        P(), P(), P(), P(None, "dp", "tensor"), P(None, ("tensor", "dp")), P(None, "tensor", "dp"), P(), P(), P(),
    )
    return jax.shard_map(
        functools.partial(body, n_dp, n_tensor), mesh=mesh, in_specs=in_specs, out_specs=out_specs, check_vma=False
    )
```

time: 437 us -> 302 us (0.69); the launches traced: 431 us -> 302 us
  Pallas kernels: 407 us -> 301 us
  local copies, waits for them, and re-layouts: 21.3 us -> 0 us
    pallas_call x10 -> x3, Pallas kernels: 407 us -> 301 us  [the longest x1 154 us: backward(): pl.pallas_call(functools.partial(backward_kernel, n_dp, n_tensor), grid=(...]
    unnamed x54 -> x0, local copies, waits for them, and re-layouts: 18.7 us -> none
where the time goes in v4:
time: 302 us
  Pallas kernels  301 us (100%)
    pallas_call x1, Pallas kernels, backward(): pl.pallas_call(functools.partial(backward_kernel, n_dp, n_tensor), grid=(...  154 us
    pallas_call x1, Pallas kernels, forward(): pl.pallas_call(functools.partial(forward_kernel, n_dp, n_tensor), grid=(2...  142 us

profile of v4, /device:TPU:1, one launch (start us, length us, event | category | flops | bytes accessed | tf_op | source)
XLA Modules:
  0.0 301.6 jit_solution(13627308014437978590)
XLA Ops:
  0.6 142.2 %forward.1 = (bf16[2,4,384,256]{3,2,1,0:T(8,128)(2,1)}, bf16[2,4,1024,384]{3,2,1,0:T(8,128)(2,1)}, bf16[2,4,384,256]{3,2,1,0:T(8,128)(2,1)}, bf16[2,4,384,768]{3...) custom-call(s32[3,4]{1,0:T(4,128)} %len_ref.3, ...), custom_call_target="tpu_custom_call" | custom-call | tf_op jit(solution)/shard_map/forward/pallas_call | solution.py:810
  142.8 154.3 %backward.1 = (f32[384,768]{1,0:T(8,128)}, f32[2,96,1536]{2,1,0:T(8,128)}, f32[2,96,768]{2,1,0:T(8,128)}, f32[32,768]{1,0:T(8,128)}) custom-call(s32[3,4]{1,0:T(4,128)} %len_ref.3, f32[384,768]{1,0:T(8,128)} %grad_in_ref.1, bf16[2,4,768,1536]{3,2,1,0:T(8,128)(2,1)} %bitcast.4, bf16[2,4,768,1536]{3,2,1,0:T(8,128)(2,1)} %bitcast.5, ...), custom_call_target="tpu_custom_call" | custom-call | tf_op jit(solution)/shard_map/backward/pallas_call | solution.py:1118
  297.1 4.3 %lay_out.1 = (f32[384,768]{1,0:T(8,128)}, f32[384,768]{1,0:T(8,128)}, f32[2,3,96,192]{3,2,1,0:T(8,128)}, f32[2,2,24]{2,1,0:T(2,128)}, f32[2,192,96]{2,1,0:T(8,12...) custom-call(f32[32,768]{1,0:T(8,128)} %get-tuple-element.59.few_in, ...), custom_call_target="tpu_custom_call" | custom-call | tf_op jit(solution)/shard_map/lay_out/pallas_call | solution.py:1183
